TPU v7x, 512 devices: a whole 4x4x16 slice. The times are simulated.
512 devices in a mesh: head: 8 (over y, x_hi), seq: 64 (over z, x_lo, core).
Axes of the slice: x: 4 (x_hi: 2, x_lo: 2; x = x_hi * 2 + x_lo), y: 4, z: 16, core: 2. Of those that a mesh axis runs over, the one named last changes fastest.
Arguments:
- tokens: bfloat16 [49152, 2048], P('seq', 'head'), may hold values from -6 to 6
- weights: bfloat16 [3, 2048, 2048], P(None, 'seq', 'head'), may hold values from -0.06591797 to 0.06591797
- landmark_pos: int32 [16, 256], P('head'), may hold values from 0 to 49151, as said below
Outputs:
- attended: bfloat16 [49152, 2048], P('seq', 'head')
Inputs may be any that keep to these rules, and one draw needn't show every extreme that they name: `landmark_pos`: landmark number j of every head lies in tokens j * 192 to (j + 1) * 192 - 1.
All inputs are finite; a program needn't handle non-finite values. Where the computation divides by a largest or mean magnitude, that divisor is 1e-20 or more.
Results may differ from a plain program's by a relative error of at most 0.0041.
Values may be sent and summed in bfloat16 or wider, within the bound.
No kernel may reach another device: no remote copies, remote signals or barrier semaphores. Data moves between devices by JAX's collectives and lax.ppermute only.
A program may use at most 64 MiB of HBM per device.

v0:
```python
import math

import jax
import jax.numpy as jnp
from jax import lax
from jax.sharding import PartitionSpec as P

NSTEPS = 6


def gauss(left, right):
    inner = jnp.einsum("hie,hje->hij", left, right, preferred_element_type=jnp.float32)
    left32 = left.astype(jnp.float32)
    right32 = right.astype(jnp.float32)
    dist = (
        jnp.sum(left32 * left32, -1)[:, :, None]
        + jnp.sum(right32 * right32, -1)[:, None, :]
        - 2.0 * inner
    )
    return jnp.exp(-dist / (2.0 * math.sqrt(left.shape[-1])))


def batched(left, right):
    return jnp.einsum("hij,hjk->hik", left, right, precision=lax.Precision.HIGHEST)


def gather_landmarks(query, keys, landmark_pos):
    per_group = landmark_pos.shape[1] // lax.axis_size("seq")
    tok_rows = query.shape[1]
    group = lax.axis_index("seq")
    local_pos = lax.dynamic_slice_in_dim(landmark_pos, group * per_group, per_group, 1)
    offsets = local_pos - group * tok_rows
    picker = (offsets[:, :, None] == jnp.arange(tok_rows, dtype=jnp.int32)[None, None, :]).astype(
        jnp.bfloat16
    )
    picked_q = jnp.einsum("hjt,hte->hje", picker, query, preferred_element_type=jnp.float32)
    picked_k = jnp.einsum("hjt,hte->hje", picker, keys, preferred_element_type=jnp.float32)
    number = group * per_group + jnp.arange(per_group, dtype=jnp.int32)
    even = (number % 2 == 0)[None, :, None]
    local_marks = jnp.where(even, picked_q, picked_k).astype(jnp.bfloat16)
    return lax.all_gather(local_marks, "seq", axis=1, tiled=True)


def shards(tokens, weights, landmark_pos):
    tok_rows = tokens.shape[0]
    heads_dev = landmark_pos.shape[0]
    head_cols = weights.shape[2]
    head_size = head_cols // heads_dev
    whole = lax.all_gather(tokens, "head", axis=1, tiled=True)

    def heads_of(flat):
        return jnp.transpose(
            flat.astype(jnp.bfloat16).reshape(tok_rows, heads_dev, head_size), (1, 0, 2)
        )

    projected = jnp.einsum(
        "td,kdc->ktc",
        whole,
        lax.all_gather(weights, "seq", axis=1, tiled=True),
        preferred_element_type=jnp.float32,
    )
    query = heads_of(projected[0])
    keys = heads_of(projected[1])
    values = heads_of(projected[2])
    landmarks = gather_landmarks(query, keys, landmark_pos)
    key_weights = gauss(landmarks, keys).astype(jnp.bfloat16)
    partial_sum = jnp.einsum(
        "hjt,hte->hje", key_weights, values, preferred_element_type=jnp.float32
    )
    summary = lax.psum(partial_sum, "seq")
    inner = gauss(landmarks, landmarks)
    scale_cols = jnp.max(jnp.sum(jnp.abs(inner), 1), axis=-1)
    scale_rows = jnp.max(jnp.sum(jnp.abs(inner), 2), axis=-1)
    iterate = inner / (scale_cols * scale_rows)[:, None, None]
    for step in range(NSTEPS):
        iterate = 2.0 * iterate - batched(batched(iterate, inner), iterate)
    mixed = batched(iterate, summary).astype(jnp.bfloat16)
    query_weights = gauss(query, landmarks).astype(jnp.bfloat16)
    result = jnp.einsum("htm,hme->the", query_weights, mixed, preferred_element_type=jnp.float32)
    return result.reshape(tok_rows, head_cols).astype(jnp.bfloat16)


def solution(mesh):
    return jax.shard_map(
        shards,
        mesh=mesh,
        in_specs=(P("seq", "head"), P(None, "seq", "head"), P("head", None)),
        out_specs=P("seq", "head"),
        check_vma=False,
    )
```

profile of v0, /device:TPU:1, one launch (start us, length us, event | category | flops | bytes accessed | tf_op | source)
XLA Modules:
  0.0 707.9 jit_solution(10493289057307640920)
XLA Ops:
  6.5 0.7 all-gather.5.cloned.1.call-update
  7.3 0.7 all-gather.3.cloned.1.call-update
  8.1 0.8 dynamic-slice_subtract_fusion
  8.8 85.7 %all-gather.5.cloned.1.call-done = bf16[768,2048]{1,0:T(8,128)(2,1)} async-done(((bf16[768,256]{1,0:T(8,128)(2,1)}), bf16[768,2048]{1,0:T(8,128)(2,1)}) %all-gather.5.cloned.1.call-update) | async-done | bytes 3145744 | tf_op jit(solution)/shard_map/all_gather | solution.py:49
  94.6 124.4 %all-gather.3.cloned.1.call-done = bf16[3,2048,256]{2,1,0:T(8,128)(2,1)} async-done(((bf16[3,32,256]{2,1,0:T(8,128)(2,1)}), bf16[3,2048,256]{2,1,0:T(8,128)(2,1)}) %all-gather.3.cloned.1.call-update) | async-done | bytes 3145744 | tf_op jit(solution)/shard_map/all_gather | solution.py:59
  219.0 5.5 fusion.5
  224.6 0.2 copy.27
  224.8 0.3 multiply_reduce_fusion
  225.3 0.2 copy.28
  225.6 0.3 multiply_reduce_fusion.1
  225.9 0.2 fusion.15
  226.1 62.3 %all_gather.11 = bf16[2,256,128]{2,0,1:T(2,128)(2,1)S(1)} all-gather(bf16[2,4,128]{2,0,1:T(2,128)(2,1)S(1)} %copy.29), channel_id=1, replica_groups=mesh['head'=8,'seq'=64] {'seq'}, dimensions={1}, use_global_device_ids=true | all-gather | bytes 133120 | tf_op jit(solution)/shard_map/all_gather | solution.py:41
  288.4 0.3 multiply_reduce_fusion.2
  288.8 0.4 fusion.50
  289.5 0.7 fusion.24
  290.2 0.8 convolution_subtract_fusion.5
  291.0 0.7 fusion.52
  291.6 0.7 convolution_subtract_fusion.4
  292.3 0.7 fusion.53
  293.0 0.7 convolution_subtract_fusion.3
  293.6 0.7 fusion.54
  294.3 0.7 convolution_subtract_fusion.2
  295.0 0.7 fusion.55
  295.6 0.7 convolution_subtract_fusion.1
  296.3 0.7 fusion.56
  297.0 0.2 copy.36
  297.2 1.5 fusion.8
  298.7 0.7 convolution_subtract_fusion
  299.4 398.6 %all-reduce.2.cloned.1.call-done = f32[2,256,128]{2,1,0:T(8,128)} async-done(((f32[2,256,128]{2,1,0:T(8,128)}), f32[2,256,128]{2,1,0:T(8,128)}) %all-reduce.2.cloned.1.call-update) | async-done | bytes 262160 | tf_op jit(solution)/shard_map/psum | solution.py:70
  698.0 1.6 convolution_convert_fusion
  699.6 0.8 fusion.10
  700.4 0.9 copy.40
  (12 shorter events, 0.7 us)
Async XLA Ops:
  6.5 88.0 %all-gather.5.cloned.1.call-start = ((), (), s32[]{:S(2)}) async-start(), calls=%async_computation.1 | async-start | bytes 3538944 | tf_op jit(solution)/shard_map/all_gather | solution.py:49
  7.3 211.7 %all-gather.3.cloned.1.call-start = ((), (), s32[]{:S(2)}) async-start(), calls=%async_computation | async-start | bytes 3194880 | tf_op jit(solution)/shard_map/all_gather | solution.py:59
  8.0 690.0 %all-reduce.2.cloned.1.call-start = ((), (), s32[]{:S(2)}) async-start(), calls=%async_computation.2 | async-start | bytes 524288 | tf_op jit(solution)/shard_map/psum | solution.py:70
Sparse Core Ops, SparseCore 0:
  10.4 84.1 all-gather.4
  96.7 122.2 all-gather.2
  298.9 399.1 all-reduce.1
where the time goes:
time: 708 us
  waiting for transfers between devices  610 us (86%)
  blocking collectives  62.3 us (9%)
  matrix products  18.2 us (3%)
  between operations  13.3 us (2%)
    psum x1, waiting for transfers between devices, shards(): summary = lax.psum(partial_sum, 'seq')  399 us
    all_gather x1, waiting for transfers between devices, shards(): lax.all_gather(weights, 'seq', axis=1, tiled=True)  124 us
    all_gather x1, waiting for transfers between devices, shards(): whole = lax.all_gather(tokens, 'head', axis=1, tiled=True)  85.7 us
    all_gather x1, blocking collectives, gather_landmarks(): return lax.all_gather(local_marks, 'seq', axis=1, tiled=True)  62.3 us
  transfers between devices with their start and end apart: 3, of which 3 were waited for; matrix products, arithmetic and copies ran while one was open for 0% of the time, Pallas kernels for 0%

commit v1 on v0

v1 whole, which is shorter than its diff:
```python
import math

import jax
import jax.numpy as jnp
import numpy as np
from jax import lax
from jax.sharding import Mesh
from jax.sharding import PartitionSpec as P

NSTEPS = 6
AXES = ("y", "xh", "z", "xl", "c")
SIZES = (4, 2, 16, 2, 2)
HEAD = ("y", "xh")
SEQ = ("z", "xl", "c")


def shift(value, axis, step):
    size = lax.axis_size(axis)
    return lax.ppermute(value, axis, [(i, (i + step) % size) for i in range(size)])


def gauss(left, right):
    inner = jnp.einsum("hie,hje->hij", left, right, preferred_element_type=jnp.float32)
    left32 = left.astype(jnp.float32)
    right32 = right.astype(jnp.float32)
    dist = (
        jnp.sum(left32 * left32, -1)[:, :, None]
        + jnp.sum(right32 * right32, -1)[:, None, :]
        - 2.0 * inner
    )
    return jnp.exp(-dist / (2.0 * math.sqrt(left.shape[-1])))


def high(left, right):
    return jnp.dot(left, right, precision=lax.Precision.HIGHEST)


def gather_tokens(own):
    spread = jnp.broadcast_to(own[None], (8,) + own.shape)
    return lax.all_to_all(spread, HEAD, 0, 0, tiled=True)


def gather_weights(own):
    kinds, depth, cols = own.shape
    xl, c = lax.axis_index("xl"), lax.axis_index("c")
    column = lax.all_gather(own, "z", axis=1)
    across = shift(column, "xl", 1)
    core = shift(column, "c", 1)
    both = shift(across, "c", 1)

    def ordered(index, first, second, axis):
        return jnp.where(
            index == 0, jnp.stack([first, second], axis), jnp.stack([second, first], axis)
        )

    rows = ordered(xl, ordered(c, column, core, 2), ordered(c, across, both, 2), 2)
    return rows.reshape(kinds, 8, 256, cols)


def shards(tokens, weights, landmark_pos):
    tok_rows = tokens.shape[0]
    heads_dev = landmark_pos.shape[0]
    head_cols = weights.shape[2]
    head_size = head_cols // heads_dev
    c, xl = lax.axis_index("c"), lax.axis_index("xl")
    group = lax.axis_index(SEQ)
    whole = gather_tokens(tokens)
    gathered = gather_weights(weights)
    projected = jnp.einsum("btd,kbdc->ktc", whole, gathered, preferred_element_type=jnp.float32)

    def heads_of(flat):
        return jnp.transpose(
            flat.astype(jnp.bfloat16).reshape(tok_rows, heads_dev, head_size), (1, 0, 2)
        )

    query, keys, values = heads_of(projected[0]), heads_of(projected[1]), heads_of(projected[2])
    per_group = landmark_pos.shape[1] // 64
    local_pos = lax.dynamic_slice_in_dim(landmark_pos, group * per_group, per_group, 1)
    offsets = local_pos - group * tok_rows
    picker = (offsets[:, :, None] == jnp.arange(tok_rows, dtype=jnp.int32)[None, None, :]).astype(
        jnp.bfloat16
    )
    picked_q = jnp.einsum("hjt,hte->hje", picker, query, preferred_element_type=jnp.float32)
    picked_k = jnp.einsum("hjt,hte->hje", picker, keys, preferred_element_type=jnp.float32)
    even = (jnp.arange(per_group) % 2 == 0)[None, :, None]
    local_marks = jnp.where(even, picked_q, picked_k).astype(jnp.bfloat16)
    block = local_marks.reshape(heads_dev * per_group, head_size)
    spread = jnp.broadcast_to(block[None], (64,) + block.shape)
    marks = lax.all_to_all(spread, SEQ, 0, 0, tiled=True)
    landmarks = jnp.transpose(
        marks.reshape(64, heads_dev, per_group, head_size), (1, 0, 2, 3)
    ).reshape(heads_dev, 64 * per_group, head_size)
    key_weights = gauss(keys, landmarks).astype(jnp.bfloat16)
    partial = jnp.einsum("hte,htj->hej", values, key_weights, preferred_element_type=jnp.float32)
    give = lax.dynamic_index_in_dim(partial, 1 - c, 0, keepdims=False)
    keep = lax.dynamic_index_in_dim(partial, c, 0, keepdims=False)
    mine = lax.dynamic_index_in_dim(landmarks, c, 0, keepdims=True)
    inner = gauss(mine, mine)[0]
    chip = keep + shift(give, "c", 1)
    half = head_size // 2
    give = lax.dynamic_slice_in_dim(chip, (1 - xl) * half, half, 0)
    keep = lax.dynamic_slice_in_dim(chip, xl * half, half, 0)
    quarter = keep + shift(give, "xl", 1)
    scale_cols = jnp.max(jnp.sum(jnp.abs(inner), 0))
    scale_rows = jnp.max(jnp.sum(jnp.abs(inner), 1))
    iterate = inner / (scale_cols * scale_rows)
    for step in range(NSTEPS):
        iterate = 2.0 * iterate - high(high(iterate, inner), iterate)
    pieces = lax.all_gather(quarter.astype(jnp.bfloat16), "z", axis=0)
    summed = jnp.sum(pieces.astype(jnp.float32), 0)
    mixed = lax.dot_general(
        summed, iterate, (((1,), (1,)), ((), ())), precision=lax.Precision.HIGHEST
    ).astype(jnp.bfloat16)
    other = shift(mixed, "xl", 1)
    one = jnp.where(xl == 0, jnp.concatenate([mixed, other], 0), jnp.concatenate([other, mixed], 0))
    two = shift(one, "c", 1)
    mixed_all = jnp.where(c == 0, jnp.stack([one, two]), jnp.stack([two, one]))
    query_weights = gauss(query, landmarks).astype(jnp.bfloat16)
    result = jnp.einsum(
        "htm,hem->the", query_weights, mixed_all, preferred_element_type=jnp.float32
    )
    return result.reshape(tok_rows, head_cols).astype(jnp.bfloat16)


def solution(mesh):
    fine = Mesh(mesh.devices.reshape(SIZES), AXES)
    return jax.shard_map(
        shards,
        mesh=fine,
        in_specs=(P(SEQ, HEAD), P(None, SEQ, HEAD), P(HEAD, None)),
        out_specs=P(SEQ, HEAD),
        check_vma=False,
    )
```

time: 708 us -> 166 us (0.23)
  waiting for transfers between devices: 610 us -> 28.1 us
  starting transfers between devices: 0.08 us -> 57.9 us
  between operations: 13.3 us -> 1.71 us
    psum x1 -> x0, waiting for transfers between devices: 399 us -> none  [shards(): summary = lax.psum(partial_sum, 'seq')]
    all_gather x2 -> x0, waiting for transfers between devices: 210 us -> none  [the longest x1 124 us: shards(): lax.all_gather(weights, 'seq', axis=1, tiled=True)]
    ppermute x0 -> x7, starting transfers between devices: none -> 37.6 us  [shift(): lax.ppermute(value, axis, [(i, (i + step) % size) for i in range(size)])]
    all_to_all x0 -> x2, starting transfers between devices: none -> 20.3 us  [the longest x1 12.7 us: shards(): marks = lax.all_to_all(spread, SEQ, 0, 0, tiled=True)]
    all_to_all x0 -> x2, waiting for transfers between devices: none -> 16.8 us  [the longest x1 16.8 us: shards(): marks = lax.all_to_all(spread, SEQ, 0, 0, tiled=True)]
    ppermute x0 -> x7, waiting for transfers between devices: none -> 11.3 us  [shift(): lax.ppermute(value, axis, [(i, (i + step) % size) for i in range(size)])]
    all_gather x1 -> x2, blocking collectives: 62.3 us -> 57.5 us  [the longest x1 35.3 us: gather_weights(): column = lax.all_gather(own, 'z', axis=1)]
  transfers between devices with their start and end apart: 3 -> 9, of which waited for: 3 -> 6; matrix products, arithmetic and copies ran while one was open for 0% -> 5% of each run, Pallas kernels for 0% -> 0%
where the time goes in v1:
time: 166 us
  starting transfers between devices  57.9 us (35%)
  blocking collectives  57.5 us (35%)
  waiting for transfers between devices  28.1 us (17%)
  matrix products  11.7 us (7%)
  local copies, waits for them, and re-layouts  5.41 us (3%)
  other arithmetic  3.26 us (2%)
  between operations  1.71 us (1%)
    ppermute x7, starting transfers between devices, shift(): lax.ppermute(value, axis, [(i, (i + step) % size) for i in range(size)])  37.6 us
    all_gather x1, blocking collectives, gather_weights(): column = lax.all_gather(own, 'z', axis=1)  35.3 us
    all_gather x1, blocking collectives, shards(): pieces = lax.all_gather(quarter.astype(jnp.bfloat16), 'z', axis=0)  22.2 us
    all_to_all x1, waiting for transfers between devices, shards(): marks = lax.all_to_all(spread, SEQ, 0, 0, tiled=True)  16.8 us
    all_to_all x1, starting transfers between devices, shards(): marks = lax.all_to_all(spread, SEQ, 0, 0, tiled=True)  12.7 us
    ppermute x7, waiting for transfers between devices, shift(): lax.ppermute(value, axis, [(i, (i + step) % size) for i in range(size)])  11.3 us
    all_to_all x1, starting transfers between devices, gather_tokens(): return lax.all_to_all(spread, HEAD, 0, 0, tiled=True)  7.61 us
    dot_general x12, matrix products, high(): return jnp.dot(left, right, precision=lax.Precision.HIGHEST)  4.58 us
  transfers between devices with their start and end apart: 9, of which 6 were waited for; matrix products, arithmetic and copies ran while one was open for 5% of the time, Pallas kernels for 0%

profile of v1, /device:TPU:1, one launch (start us, length us, event | category | flops | bytes accessed | tf_op | source)
XLA Modules:
  0.0 165.6 jit_solution(10176438391730719403)
XLA Ops:
  0.0 2.9 %broadcast_in_dim.14 = bf16[8,768,256]{2,1,0:T(8,128)(2,1)} broadcast(bf16[768,256]{1,0:T(8,128)(2,1)} %param.3), dimensions={1,2} | broadcast | bytes 3538944 | tf_op jit(solution)/shard_map/broadcast_in_dim | solution.py:39
  2.9 7.6 %all-to-all-start = ((bf16[8,768,256]{2,1,0:T(8,128)(2,1)}), bf16[8,768,256]{2,1,0:T(8,128)(2,1)}, u32[]{:S(2)}, u32[]{:S(2)}) async-start(bf16[8,768,256]{2,1,0:T(8,128)(2,1)} %broadcast_in_dim.14), calls=%async_computation | async-start | bytes 6291456 | tf_op jit(solution)/shard_map/all_to_all | solution.py:40
  10.5 35.3 %all-gather = bf16[3,512,256]{2,1,0:T(8,128)(2,1)S(1)} all-gather(bf16[3,32,256]{2,1,0:T(8,128)(2,1)S(1)} %copy-done), channel_id=2, replica_groups=mesh['y'=4,'xh'=2,'z'=16,'xl'=2,'c'=2] {'z'}, dimensions={1}, use_global_device_ids=true | all-gather | bytes 835584 | tf_op jit(solution)/shard_map/all_gather | solution.py:46
  45.9 2.6 %collective-permute-start.1 = (bf16[3,16,32,256]{3,2,1,0:T(8,128)(2,1)S(1)}, bf16[3,16,32,256]{3,2,1,0:T(8,128)(2,1)S(1)}, u32[]{:S(2)}, u32[]{:S(2)}) collective-permute-start(bf16[3,16,32,256]{3,2,1,0:T(8,128)(2,1)S(1)} %bitcast.89), channel_id=1, source_target_pairs={{0,2},{2,0},{1,3},{3,1},{4,6},{6,4},{5,7},{7,5},{8,10},{10,8},{9,1... | collective-permute-start | bytes 2359304 | tf_op jit(solution)/shard_map/ppermute | solution.py:19
  48.5 7.4 %collective-permute-start = (bf16[3,16,32,256]{3,2,1,0:T(8,128)(2,1)S(1)}, bf16[3,16,32,256]{3,2,1,0:T(8,128)(2,1)S(1)}, u32[]{:S(2)}, u32[]{:S(2)}) collective-permute-start(bf16[3,16,32,256]{3,2,1,0:T(8,128)(2,1)S(1)} %bitcast.90), channel_id=1, source_target_pairs={{0,1},{1,0},{2,3},{3,2},{4,5},{5,4},{6,7},{7,6},{8,9},{9,8},{10,11... | collective-permute-start | bytes 2359304 | tf_op jit(solution)/shard_map/ppermute | solution.py:19
  55.9 5.2 %collective-permute-done.1 = bf16[3,16,32,256]{3,2,1,0:T(8,128)(2,1)S(1)} collective-permute-done((bf16[3,16,32,256]{3,2,1,0:T(8,128)(2,1)S(1)}, bf16[3,16,32,256]{3,2,1,0:T(8,128)(2,1)S(1)}, u32[]{:S(2)}, u32[]{:S(2)}) %collective-permute-start.1) | collective-permute-done | bytes 786464 | tf_op jit(solution)/shard_map/ppermute | solution.py:19
  61.1 8.5 %collective-permute-start.2 = (bf16[3,16,32,256]{3,2,1,0:T(8,128)(2,1)S(1)}, bf16[3,16,32,256]{3,2,1,0:T(8,128)(2,1)S(1)}, u32[]{:S(2)}, u32[]{:S(2)}) collective-permute-start(bf16[3,16,32,256]{3,2,1,0:T(8,128)(2,1)S(1)} %collective-permute-done.1), channel_id=1, source_target_pairs={{0,1},{1,0},{2,3},{3,2},{4,5},{5,4},{6,7},{7,6},{8,9},{9,8},{10,11... | collective-permute-start | bytes 2359304 | tf_op jit(solution)/shard_map/ppermute | solution.py:19
  70.2 1.3 collective-permute-done.2
  72.0 4.5 %fusion.4 = bf16[3,768,256]{1,2,0:T(8,128)(2,1)S(1)} fusion(bf16[3,8,256,256]{3,2,1,0:T(8,128)(2,1)S(1)} %bitcast.92, bf16[8,768,256]{2,1,0:T(8,128)(2,1)} %all-to-all-done), kind=kOutput, calls=%fused_computation.10 | convolution fusion | flops 2416508928 | bytes 7471104 | tf_op jit(solution)/shard_map/btd,kbdc->ktc/dot_general | solution.py:69
  77.5 0.7 broadcast_in_dim.17
  78.2 12.7 %all-to-all-start.1 = ((bf16[64,8,128]{2,1,0:T(8,128)(2,1)}), bf16[64,8,128]{2,1,0:T(8,128)(2,1)S(1)}, u32[]{:S(2)}, u32[]{:S(2)}) async-start(bf16[64,8,128]{2,1,0:T(8,128)(2,1)} %broadcast_in_dim.17), calls=%async_computation.1 | async-start | bytes 262144 | tf_op jit(solution)/shard_map/all_to_all | solution.py:89
  91.2 16.8 %all-to-all-done.1 = bf16[64,8,128]{2,1,0:T(8,128)(2,1)S(1)} async-done(((bf16[64,8,128]{2,1,0:T(8,128)(2,1)}), bf16[64,8,128]{2,1,0:T(8,128)(2,1)S(1)}, u32[]{:S(2)}, u32[]{:S(2)}) %all-to-all-start.1) | async-done | bytes 131104 | tf_op jit(solution)/shard_map/all_to_all | solution.py:89
  108.5 0.7 fusion.7
  109.3 2.3 %collective-permute-start.3 = (f32[128,256]{1,0:T(8,128)S(1)}, f32[128,256]{1,0:T(8,128)S(1)}, u32[]{:S(2)}, u32[]{:S(2)}) collective-permute-start(f32[128,256]{1,0:T(8,128)S(1)} %dynamic-slice_bitcast_fusion), channel_id=1, source_target_pairs={{0,1},{1,0},{2,3},{3,2},{4,5},{5,4},{6,7},{7,6},{8,9},{9,8},{10,11... | collective-permute-start | bytes 393224 | tf_op jit(solution)/shard_map/ppermute | solution.py:19
  112.0 0.6 reduce_max.18
  112.7 0.7 reduce_max.19
  114.7 0.4 fusion.30
  115.1 0.4 convolution_subtract_fusion.5
  115.5 0.4 fusion.55
  115.9 0.4 convolution_subtract_fusion.4
  116.6 0.4 convolution_subtract_fusion.3
  117.4 0.4 convolution_subtract_fusion.2
  118.2 0.4 convolution_subtract_fusion.1
  119.0 2.8 %collective-permute-start.4 = (f32[64,256]{1,0:T(8,128)S(1)}, f32[64,256]{1,0:T(8,128)S(1)}, u32[]{:S(2)}, u32[]{:S(2)}) collective-permute-start(f32[64,256]{1,0:T(8,128)S(1)} %constant_dynamic-slice_fusion), channel_id=1, source_target_pairs={{0,2},{2,0},{1,3},{3,1},{4,6},{6,4},{5,7},{7,5},{8,10},{10,8},{9,1... | collective-permute-start | bytes 196616 | tf_op jit(solution)/shard_map/ppermute | solution.py:19
  122.2 2.4 %collective-permute-done.4 = f32[64,256]{1,0:T(8,128)S(1)} collective-permute-done((f32[64,256]{1,0:T(8,128)S(1)}, f32[64,256]{1,0:T(8,128)S(1)}, u32[]{:S(2)}, u32[]{:S(2)}) %collective-permute-start.4) | collective-permute-done | bytes 65568 | tf_op jit(solution)/shard_map/ppermute | solution.py:19
  124.6 22.2 %all-gather.1 = bf16[1024,256]{1,0:T(8,128)(2,1)S(1)} all-gather(bf16[64,256]{1,0:T(8,128)(2,1)S(1)} %add_convert_fusion), channel_id=3, replica_groups=mesh['y'=4,'xh'=2,'z'=16,'xl'=2,'c'=2] {'z'}, dimensions={0}, use_global_device_ids=true | all-gather | bytes 557056 | tf_op jit(solution)/shard_map/all_gather | solution.py:109
  147.2 2.8 %collective-permute-start.5 = (bf16[64,256]{1,0:T(8,128)(2,1)S(1)}, bf16[64,256]{1,0:T(8,128)(2,1)S(1)}, u32[]{:S(2)}, u32[]{:S(2)}) collective-permute-start(bf16[64,256]{1,0:T(8,128)(2,1)S(1)} %convolution_convert_fusion), channel_id=1, source_target_pairs={{0,2},{2,0},{1,3},{3,1},{4,6},{6,4},{5,7},{7,5},{8,10},{10,8},{9,1... | collective-permute-start | bytes 98312 | tf_op jit(solution)/shard_map/ppermute | solution.py:19
  150.3 1.5 collective-permute-done.5
  151.9 11.2 %collective-permute-start.6 = (bf16[128,256]{1,0:T(8,128)(2,1)S(1)}, bf16[128,256]{1,0:T(8,128)(2,1)S(1)}, u32[]{:S(2)}, u32[]{:S(2)}) collective-permute-start(bf16[128,256]{1,0:T(8,128)(2,1)S(1)} %maximum_select_fusion.5), channel_id=1, source_target_pairs={{0,1},{1,0},{2,3},{3,2},{4,5},{5,4},{6,7},{7,6},{8,9},{9,8},{10,11... | collective-permute-start | bytes 196616 | tf_op jit(solution)/shard_map/ppermute | solution.py:19
  163.1 0.9 collective-permute-done.6
  164.0 0.7 fusion.9
  164.7 0.9 copy.28
  (40 shorter events, 5.9 us)
Async XLA Ops:
  2.9 7.6 %copy-start = (bf16[3,32,256]{2,1,0:T(8,128)(2,1)S(1)}, bf16[3,32,256]{2,1,0:T(8,128)(2,1)}, u32[]{:S(2)}) copy-start(bf16[3,32,256]{2,1,0:T(8,128)(2,1)} %param.4) | copy-start | bytes 147460
  2.9 66.7 %copy-start.1 = (s32[2,256]{1,0:T(2,128)S(1)}, s32[2,256]{1,0:T(2,128)}, u32[]{:S(2)}) copy-start(s32[2,256]{1,0:T(2,128)} %param.5) | copy-start | bytes 6148
  2.9 69.1 %all-to-all-start = ((bf16[8,768,256]{2,1,0:T(8,128)(2,1)}), bf16[8,768,256]{2,1,0:T(8,128)(2,1)}, u32[]{:S(2)}, u32[]{:S(2)}) async-start(bf16[8,768,256]{2,1,0:T(8,128)(2,1)} %broadcast_in_dim.14), calls=%async_computation | async-start | bytes 6291456 | tf_op jit(solution)/shard_map/all_to_all | solution.py:40
  45.9 15.2 %collective-permute-start.1 = (bf16[3,16,32,256]{3,2,1,0:T(8,128)(2,1)S(1)}, bf16[3,16,32,256]{3,2,1,0:T(8,128)(2,1)S(1)}, u32[]{:S(2)}, u32[]{:S(2)}) collective-permute-start(bf16[3,16,32,256]{3,2,1,0:T(8,128)(2,1)S(1)} %bitcast.89), channel_id=1, source_target_pairs={{0,2},{2,0},{1,3},{3,1},{4,6},{6,4},{5,7},{7,5},{8,10},{10,8},{9,1... | collective-permute-start | bytes 2359304 | tf_op jit(solution)/shard_map/ppermute | solution.py:19
  48.5 21.3 %collective-permute-start = (bf16[3,16,32,256]{3,2,1,0:T(8,128)(2,1)S(1)}, bf16[3,16,32,256]{3,2,1,0:T(8,128)(2,1)S(1)}, u32[]{:S(2)}, u32[]{:S(2)}) collective-permute-start(bf16[3,16,32,256]{3,2,1,0:T(8,128)(2,1)S(1)} %bitcast.90), channel_id=1, source_target_pairs={{0,1},{1,0},{2,3},{3,2},{4,5},{5,4},{6,7},{7,6},{8,9},{9,8},{10,11... | collective-permute-start | bytes 2359304 | tf_op jit(solution)/shard_map/ppermute | solution.py:19
  61.1 10.4 %collective-permute-start.2 = (bf16[3,16,32,256]{3,2,1,0:T(8,128)(2,1)S(1)}, bf16[3,16,32,256]{3,2,1,0:T(8,128)(2,1)S(1)}, u32[]{:S(2)}, u32[]{:S(2)}) collective-permute-start(bf16[3,16,32,256]{3,2,1,0:T(8,128)(2,1)S(1)} %collective-permute-done.1), channel_id=1, source_target_pairs={{0,1},{1,0},{2,3},{3,2},{4,5},{5,4},{6,7},{7,6},{8,9},{9,8},{10,11... | collective-permute-start | bytes 2359304 | tf_op jit(solution)/shard_map/ppermute | solution.py:19
  78.2 29.8 %all-to-all-start.1 = ((bf16[64,8,128]{2,1,0:T(8,128)(2,1)}), bf16[64,8,128]{2,1,0:T(8,128)(2,1)S(1)}, u32[]{:S(2)}, u32[]{:S(2)}) async-start(bf16[64,8,128]{2,1,0:T(8,128)(2,1)} %broadcast_in_dim.17), calls=%async_computation.1 | async-start | bytes 262144 | tf_op jit(solution)/shard_map/all_to_all | solution.py:89
  109.3 9.7 %collective-permute-start.3 = (f32[128,256]{1,0:T(8,128)S(1)}, f32[128,256]{1,0:T(8,128)S(1)}, u32[]{:S(2)}, u32[]{:S(2)}) collective-permute-start(f32[128,256]{1,0:T(8,128)S(1)} %dynamic-slice_bitcast_fusion), channel_id=1, source_target_pairs={{0,1},{1,0},{2,3},{3,2},{4,5},{5,4},{6,7},{7,6},{8,9},{9,8},{10,11... | collective-permute-start | bytes 393224 | tf_op jit(solution)/shard_map/ppermute | solution.py:19
  119.0 5.6 %collective-permute-start.4 = (f32[64,256]{1,0:T(8,128)S(1)}, f32[64,256]{1,0:T(8,128)S(1)}, u32[]{:S(2)}, u32[]{:S(2)}) collective-permute-start(f32[64,256]{1,0:T(8,128)S(1)} %constant_dynamic-slice_fusion), channel_id=1, source_target_pairs={{0,2},{2,0},{1,3},{3,1},{4,6},{6,4},{5,7},{7,5},{8,10},{10,8},{9,1... | collective-permute-start | bytes 196616 | tf_op jit(solution)/shard_map/ppermute | solution.py:19
  147.2 4.7 %collective-permute-start.5 = (bf16[64,256]{1,0:T(8,128)(2,1)S(1)}, bf16[64,256]{1,0:T(8,128)(2,1)S(1)}, u32[]{:S(2)}, u32[]{:S(2)}) collective-permute-start(bf16[64,256]{1,0:T(8,128)(2,1)S(1)} %convolution_convert_fusion), channel_id=1, source_target_pairs={{0,2},{2,0},{1,3},{3,1},{4,6},{6,4},{5,7},{7,5},{8,10},{10,8},{9,1... | collective-permute-start | bytes 98312 | tf_op jit(solution)/shard_map/ppermute | solution.py:19
  151.9 12.1 %collective-permute-start.6 = (bf16[128,256]{1,0:T(8,128)(2,1)S(1)}, bf16[128,256]{1,0:T(8,128)(2,1)S(1)}, u32[]{:S(2)}, u32[]{:S(2)}) collective-permute-start(bf16[128,256]{1,0:T(8,128)(2,1)S(1)} %maximum_select_fusion.5), channel_id=1, source_target_pairs={{0,1},{1,0},{2,3},{3,2},{4,5},{5,4},{6,7},{7,6},{8,9},{9,8},{10,11... | collective-permute-start | bytes 196616 | tf_op jit(solution)/shard_map/ppermute | solution.py:19

commit v2 on v1

v2 whole, which is shorter than its diff:
```python
import math

import jax
import jax.numpy as jnp
from jax import lax
from jax.experimental import pallas as pl
from jax.experimental.pallas import tpu as pltpu
from jax.sharding import Mesh
from jax.sharding import PartitionSpec as P

NSTEPS = 6
AXES = ("y", "xh", "z", "xl", "c")
SIZES = (4, 2, 16, 2, 2)
HEAD = ("y", "xh")
SEQ = ("z", "xl", "c")


def shift(value, axis, step):
    size = lax.axis_size(axis)
    return lax.ppermute(value, axis, [(i, (i + step) % size) for i in range(size)])


def gauss(left, right):
    inner = jnp.einsum("hie,hje->hij", left, right, preferred_element_type=jnp.float32)
    left32 = left.astype(jnp.float32)
    right32 = right.astype(jnp.float32)
    dist = (
        jnp.sum(left32 * left32, -1)[:, :, None]
        + jnp.sum(right32 * right32, -1)[:, None, :]
        - 2.0 * inner
    )
    return jnp.exp(-dist / (2.0 * math.sqrt(left.shape[-1])))


def high(left, right):
    return jnp.dot(left, right, precision=lax.Precision.HIGHEST)


def inverse_kernel(marks_ref, inverse_ref):
    marks = marks_ref[...]
    marks32 = marks.astype(jnp.float32)
    squares = marks32 * marks32
    across = (((1,), (1,)), ((), ()))
    product = lax.dot_general(marks, marks, across, preferred_element_type=jnp.float32)
    down_norm = jnp.sum(squares, 1, keepdims=True)
    ones = jnp.ones((8, squares.shape[1]), jnp.float32)
    side_norm = lax.dot_general(
        ones, squares, across, precision=lax.Precision.HIGHEST, preferred_element_type=jnp.float32
    )[:1]
    inner = jnp.exp((down_norm + side_norm - 2.0 * product) * (-0.5 / math.sqrt(marks.shape[1])))
    scale_cols = jnp.max(jnp.sum(jnp.abs(inner), 0, keepdims=True), 1, keepdims=True)
    scale_rows = jnp.max(jnp.sum(jnp.abs(inner), 1, keepdims=True), 0, keepdims=True)
    iterate = inner / (scale_cols * scale_rows)
    for step in range(NSTEPS):
        iterate = 2.0 * iterate - high(high(iterate, inner), iterate)
    inverse_ref[...] = iterate


def invert(marks):
    count = marks.shape[0]
    return pl.pallas_call(
        inverse_kernel,
        out_shape=jax.ShapeDtypeStruct((count, count), jnp.float32),
        in_specs=[pl.BlockSpec(memory_space=pltpu.VMEM)],
        out_specs=pl.BlockSpec(memory_space=pltpu.VMEM),
        cost_estimate=pl.CostEstimate(
            flops=2 * 6 * 12 * count**3, bytes_accessed=4 * count**2, transcendentals=count**2
        ),
        name="inverse",
    )(marks)


def gather_tokens(own):
    spread = jnp.broadcast_to(own[None], (8,) + own.shape)
    return lax.all_to_all(spread, HEAD, 0, 0, tiled=True)


def in_order(column, core, across, both):
    kinds, _, _, cols = column.shape
    xl, c = lax.axis_index("xl"), lax.axis_index("c")

    def ordered(index, first, second):
        return jnp.where(index == 0, jnp.stack([first, second], 2), jnp.stack([second, first], 2))

    rows = ordered(xl, ordered(c, column, core), ordered(c, across, both))
    return rows.reshape(kinds, 8, 256, cols)


def shards(tokens, weights, landmark_pos):
    tok_rows = tokens.shape[0]
    heads_dev = landmark_pos.shape[0]
    head_cols = weights.shape[2]
    head_size = head_cols // heads_dev
    c = lax.axis_index("c")
    group = lax.axis_index(SEQ)
    whole = gather_tokens(tokens)
    column = lax.all_gather(weights, "z", axis=1, tiled=True).reshape(3, 16, 32, head_cols)
    column_qk, column_v = column[:2], column[2:]
    across_qk, core_qk = shift(column_qk, "xl", 1), shift(column_qk, "c", 1)
    across_qk, column_v = lax.optimization_barrier((across_qk, column_v))
    both_qk = shift(across_qk, "c", 1)
    across_v, core_v = shift(column_v, "xl", 1), shift(column_v, "c", 1)

    def project(matrix):
        flat = jnp.einsum("btd,kbdc->ktc", whole, matrix, preferred_element_type=jnp.float32)
        parts = flat.astype(jnp.bfloat16).reshape(-1, tok_rows, heads_dev, head_size)
        return jnp.transpose(parts, (0, 2, 1, 3))

    query, keys = project(in_order(column_qk, core_qk, across_qk, both_qk))
    per_group = landmark_pos.shape[1] // 64
    local_pos = lax.dynamic_slice_in_dim(landmark_pos, group * per_group, per_group, 1)
    offsets = local_pos - group * tok_rows
    picker = (offsets[:, :, None] == jnp.arange(tok_rows, dtype=jnp.int32)[None, None, :]).astype(
        jnp.bfloat16
    )
    picked_q = jnp.einsum("hjt,hte->hje", picker, query, preferred_element_type=jnp.float32)
    picked_k = jnp.einsum("hjt,hte->hje", picker, keys, preferred_element_type=jnp.float32)
    even = (jnp.arange(per_group) % 2 == 0)[None, :, None]
    local_marks = jnp.where(even, picked_q, picked_k).astype(jnp.bfloat16)
    block = local_marks.reshape(heads_dev * per_group, head_size)
    spread = jnp.broadcast_to(block[None], (64,) + block.shape)
    spread, across_v = lax.optimization_barrier((spread, across_v))
    marks = lax.all_to_all(spread, SEQ, 0, 0, tiled=True)
    both_v = shift(across_v, "c", 1)
    values = project(in_order(column_v, core_v, across_v, both_v))[0]
    marks, values = lax.optimization_barrier((marks, values))
    landmarks = jnp.transpose(
        marks.reshape(64, heads_dev, per_group, head_size), (1, 0, 2, 3)
    ).reshape(heads_dev, 64 * per_group, head_size)
    key_weights = gauss(keys, landmarks).astype(jnp.bfloat16)
    partial = jnp.einsum("hte,htj->hej", values, key_weights, preferred_element_type=jnp.float32)
    give = lax.dynamic_index_in_dim(partial, 1 - c, 0, keepdims=False)
    keep = lax.dynamic_index_in_dim(partial, c, 0, keepdims=False)
    mine = lax.dynamic_index_in_dim(landmarks, c, 0, keepdims=True)
    chip = keep + shift(give, "c", 1)
    chip, mine = lax.optimization_barrier((chip, mine))
    iterate = invert(mine[0])
    pieces = lax.all_to_all(chip.reshape(32, -1, chip.shape[1]), ("z", "xl"), 0, 0, tiled=True)
    summed = jnp.sum(pieces, 0)
    mixed = lax.dot_general(
        summed, iterate, (((1,), (1,)), ((), ())), precision=lax.Precision.HIGHEST
    ).astype(jnp.bfloat16)
    one = lax.all_to_all(
        jnp.broadcast_to(mixed[None], (32,) + mixed.shape), ("z", "xl"), 0, 0, tiled=True
    ).reshape(head_size, -1)
    two = shift(one, "c", 1)
    mixed_all = jnp.where(c == 0, jnp.stack([one, two]), jnp.stack([two, one]))
    query_weights = gauss(query, landmarks).astype(jnp.bfloat16)
    result = jnp.einsum(
        "htm,hem->the", query_weights, mixed_all, preferred_element_type=jnp.float32
    )
    return result.reshape(tok_rows, head_cols).astype(jnp.bfloat16)


def solution(mesh):
    fine = Mesh(mesh.devices.reshape(SIZES), AXES)
    return jax.shard_map(
        shards,
        mesh=fine,
        in_specs=(P(SEQ, HEAD), P(None, SEQ, HEAD), P(HEAD, None)),
        out_specs=P(SEQ, HEAD),
        check_vma=False,
    )
```

time: 166 us -> 169 us (1.018)
  other arithmetic: 3.26 us -> 11.1 us
  Pallas kernels: 0 us -> 7.66 us
  blocking collectives: 57.5 us -> 51.3 us
  local copies, waits for them, and re-layouts: 5.41 us -> 11.4 us
  waiting for transfers between devices: 28.1 us -> 22.2 us
  starting transfers between devices: 57.9 us -> 53.2 us
    all_gather x2 -> x1, blocking collectives: 57.5 us -> 34.6 us  [shards(): lax.all_gather(weights, 'z', axis=1, tiled=True)]
    all_to_all x0 -> x1, blocking collectives: none -> 16.6 us  [shards(): lax.all_to_all(jnp.broadcast_to(mixed[None], (32,) + mixed.shape), ('z',...]
    ppermute x7 -> x8, waiting for transfers between devices: 11.3 us -> 1.19 us  [shift(): lax.ppermute(value, axis, [(i, (i + step) % size) for i in range(size)])]
    all_to_all x0 -> x1, waiting for transfers between devices: none -> 8.11 us  [shards(): lax.all_to_all(chip.reshape(32, -1, chip.shape[1]), ('z', 'xl'), 0, 0, ti...]
    pallas_call x0 -> x1, Pallas kernels: none -> 7.66 us  [invert(): pl.pallas_call(inverse_kernel, out_shape=jax.ShapeDtypeStruct((count, cou...]
    ppermute x7 -> x8, starting transfers between devices: 37.6 us -> 31.8 us  [shift(): lax.ppermute(value, axis, [(i, (i + step) % size) for i in range(size)])]
    select_n x5 -> x6, other arithmetic: 0.68 us -> 6.3 us  [ordered(): jnp.where(index == 0, jnp.stack([first, second], 2), jnp.stack([second, f...]
    dot_general x14 -> x2, matrix products: 9.42 us -> 5.39 us  [project(): jnp.einsum('btd,kbdc->ktc', whole, matrix, preferred_element_type=jnp.flo...]
  transfers between devices with their start and end apart: 9 -> 11, of which waited for: 6 -> 4; matrix products, arithmetic and copies ran while one was open for 5% -> 14% of each run, Pallas kernels for 0% -> 5%
where the time goes in v2:
time: 169 us; the launch traced here: 168 us
  starting transfers between devices  53.2 us (31%)
  blocking collectives  51.3 us (30%)
  waiting for transfers between devices  22.2 us (13%)
  local copies, waits for them, and re-layouts  11.4 us (7%)
  other arithmetic  11.1 us (7%)
  matrix products  10.4 us (6%)
  Pallas kernels  7.66 us (5%)
    all_gather x1, blocking collectives, shards(): lax.all_gather(weights, 'z', axis=1, tiled=True)  34.6 us
    ppermute x8, starting transfers between devices, shift(): lax.ppermute(value, axis, [(i, (i + step) % size) for i in range(size)])  31.8 us
    all_to_all x1, blocking collectives, shards(): lax.all_to_all(jnp.broadcast_to(mixed[None], (32,) + mixed.shape), ('z',...  16.6 us
    all_to_all x1, waiting for transfers between devices, shards(): marks = lax.all_to_all(spread, SEQ, 0, 0, tiled=True)  12.9 us
    all_to_all x1, starting transfers between devices, shards(): marks = lax.all_to_all(spread, SEQ, 0, 0, tiled=True)  9.82 us
    all_to_all x1, waiting for transfers between devices, shards(): lax.all_to_all(chip.reshape(32, -1, chip.shape[1]), ('z', 'xl'), 0, 0, ti...  8.11 us
    pallas_call x1, Pallas kernels, invert(): pl.pallas_call(inverse_kernel, out_shape=jax.ShapeDtypeStruct((count, cou...  7.66 us
    all_to_all x1, starting transfers between devices, gather_tokens(): return lax.all_to_all(spread, HEAD, 0, 0, tiled=True)  7.61 us
  transfers between devices with their start and end apart: 11, of which 4 were waited for; matrix products, arithmetic and copies ran while one was open for 14% of the time, Pallas kernels for 5%

profile of v2, /device:TPU:1, one launch (start us, length us, event | category | flops | bytes accessed | tf_op | source)
XLA Modules:
  0.0 167.6 jit_solution(6602570215127684896)
XLA Ops:
  0.0 2.8 %broadcast_in_dim.17 = bf16[8,768,256]{2,1,0:T(8,128)(2,1)} broadcast(bf16[768,256]{1,0:T(8,128)(2,1)} %param.3), dimensions={1,2} | broadcast | bytes 3538944 | tf_op jit(solution)/shard_map/broadcast_in_dim | solution.py:74
  2.8 7.6 %all-to-all-start = ((bf16[8,768,256]{2,1,0:T(8,128)(2,1)}), bf16[8,768,256]{2,1,0:T(8,128)(2,1)S(1)}, u32[]{:S(2)}, u32[]{:S(2)}) async-start(bf16[8,768,256]{2,1,0:T(8,128)(2,1)} %broadcast_in_dim.17), calls=%async_computation | async-start | bytes 6291456 | tf_op jit(solution)/shard_map/all_to_all | solution.py:75
  10.5 34.6 %all_gather.3 = bf16[3,512,256]{2,1,0:T(8,128)(2,1)S(1)} all-gather(bf16[3,32,256]{2,1,0:T(8,128)(2,1)S(1)} %copy-done.3), channel_id=1, replica_groups=mesh['y'=4,'xh'=2,'z'=16,'xl'=2,'c'=2] {'z'}, dimensions={1}, use_global_device_ids=true | all-gather | bytes 835584 | tf_op jit(solution)/shard_map/all_gather | solution.py:97
  46.8 2.5 %collective-permute-start.1 = (bf16[2,16,32,256]{3,2,1,0:T(8,128)(2,1)}, bf16[2,16,32,256]{3,2,1,0:T(8,128)(2,1)}, u32[]{:S(2)}, u32[]{:S(2)}) collective-permute-start(bf16[2,16,32,256]{3,2,1,0:T(8,128)(2,1)} %bitcast.1), channel_id=1, source_target_pairs={{0,2},{2,0},{1,3},{3,1},{4,6},{6,4},{5,7},{7,5},{8,10},{10,8},{9,1... | collective-permute-start | bytes 1572872 | tf_op jit(solution)/shard_map/ppermute | solution.py:20
  49.3 8.3 %collective-permute-start = (bf16[2,16,32,256]{3,2,1,0:T(8,128)(2,1)}, bf16[2,16,32,256]{3,2,1,0:T(8,128)(2,1)}, u32[]{:S(2)}, u32[]{:S(2)}) collective-permute-start(bf16[2,16,32,256]{3,2,1,0:T(8,128)(2,1)} %bitcast.1), channel_id=1, source_target_pairs={{0,1},{1,0},{2,3},{3,2},{4,5},{5,4},{6,7},{7,6},{8,9},{9,8},{10,11... | collective-permute-start | bytes 1572872 | tf_op jit(solution)/shard_map/ppermute | solution.py:20
  57.6 1.0 slice.25
  58.7 3.1 %collective-permute-start.3 = (bf16[1,16,32,256]{3,2,1,0:T(8,128)(2,1)S(1)}, bf16[1,16,32,256]{3,2,1,0:T(8,128)(2,1)}, u32[]{:S(2)}, u32[]{:S(2)}) collective-permute-start(bf16[1,16,32,256]{3,2,1,0:T(8,128)(2,1)S(1)} %bitcast.80), channel_id=1, source_target_pairs={{0,2},{2,0},{1,3},{3,1},{4,6},{6,4},{5,7},{7,5},{8,10},{10,8},{9,1... | collective-permute-start | bytes 786440 | tf_op jit(solution)/shard_map/ppermute | solution.py:20
  61.8 7.3 %collective-permute-start.4 = (bf16[1,16,32,256]{3,2,1,0:T(8,128)(2,1)S(1)}, bf16[1,16,32,256]{3,2,1,0:T(8,128)(2,1)S(1)}, u32[]{:S(2)}, u32[]{:S(2)}) collective-permute-start(bf16[1,16,32,256]{3,2,1,0:T(8,128)(2,1)S(1)} %bitcast.81), channel_id=1, source_target_pairs={{0,1},{1,0},{2,3},{3,2},{4,5},{5,4},{6,7},{7,6},{8,9},{9,8},{10,11... | collective-permute-start | bytes 786440 | tf_op jit(solution)/shard_map/ppermute | solution.py:20
  69.1 1.9 %collective-permute-start.2 = (bf16[2,16,32,256]{3,2,1,0:T(8,128)(2,1)}, bf16[2,16,32,256]{3,2,1,0:T(8,128)(2,1)S(1)}, u32[]{:S(2)}, u32[]{:S(2)}) collective-permute-start(bf16[2,16,32,256]{3,2,1,0:T(8,128)(2,1)} %collective-permute-done.1), channel_id=1, source_target_pairs={{0,1},{1,0},{2,3},{3,2},{4,5},{5,4},{6,7},{7,6},{8,9},{9,8},{10,11... | collective-permute-start | bytes 1572872 | tf_op jit(solution)/shard_map/ppermute | solution.py:20
  71.1 1.7 %pad_maximum_fusion = (bf16[2,16,1,2,32,256]{5,4,1,0,3,2:T(8,128)(2,1)S(1)}, bf16[2,16,1,2,32,256]{5,4,1,0,3,2:T(8,128)(2,1)S(1)}) fusion(bf16[2,16,1,1,32,256]{5,4,1,0,3,2:T(8,128)(2,1)} %bitcast.2, bf16[2,16,1,1,32,256]{5,4,1,0,3,2:T(8,128)(2,1)} %bitcast), kind=kLoop, calls=%fused_computation.15 | loop fusion | flops 1048576 | bytes 3145728 | tf_op jit(solution)/shard_map/stack | solution.py:83
  72.9 1.1 pad_maximum_fusion.2
  74.0 1.3 maximum_select_fusion.1
  75.4 1.5 maximum_select_fusion
  76.9 4.3 %bitcast_convert_fusion = bf16[2,256,768]{2,1,0:T(8,128)(2,1)} fusion(bf16[2,8,256,256]{3,2,1,0:T(8,128)(2,1)} %bitcast.76, bf16[8,768,256]{2,1,0:T(8,128)(2,1)S(1)} %all-to-all-done), kind=kOutput, calls=%fused_computation.3 | convolution fusion | flops 1611005952 | bytes 6029312 | tf_op jit(solution)/shard_map/btd,kbdc->ktc/dot_general | solution.py:105
  81.2 2.3 %copy.20 = bf16[2,768,2,128]{3,1,2,0:T(8,128)(2,1)} copy(bf16[2,768,2,128]{1,3,2,0:T(8,128)(2,1)} %bitcast.83) | data formatting | bytes 1572864 | tf_op jit(solution)/shard_map/reshape | solution.py:106
  83.5 1.2 fusion.19
  84.7 1.2 fusion.9
  86.7 2.4 %collective-permute-start.5 = (bf16[1,16,32,256]{3,2,1,0:T(8,128)(2,1)}, bf16[1,16,32,256]{3,2,1,0:T(8,128)(2,1)S(1)}, u32[]{:S(2)}, u32[]{:S(2)}) collective-permute-start(bf16[1,16,32,256]{3,2,1,0:T(8,128)(2,1)} %collective-permute-done.3), channel_id=1, source_target_pairs={{0,1},{1,0},{2,3},{3,2},{4,5},{5,4},{6,7},{7,6},{8,9},{9,8},{10,11... | collective-permute-start | bytes 786440 | tf_op jit(solution)/shard_map/ppermute | solution.py:20
  89.1 2.1 %copy_select_fusion.1 = bf16[1,16,1,2,32,256]{5,4,3,2,1,0:T(8,128)(2,1)} fusion(bf16[1,16,1,2,32,256]{5,4,1,3,2,0:T(8,128)(2,1)} %get-tuple-element.26, bf16[1,16,1,2,32,256]{5,4,1,3,2,0:T(8,128)(2,1)} %get-tuple-element.25, pred[]{:T(512)S(6)} %eq.33), kind=kLoop, calls=%fused_computation.33 | loop fusion | flops 262144 | bytes 1572865 | tf_op jit(solution)/shard_map/jit(_where)/select_n | solution.py:83
  91.1 9.8 %all-to-all-start.1 = ((bf16[64,8,128]{2,1,0:T(8,128)(2,1)}), bf16[64,8,128]{2,1,0:T(8,128)(2,1)S(1)}, u32[]{:S(2)}, u32[]{:S(2)}) async-start(bf16[64,8,128]{2,1,0:T(8,128)(2,1)} %broadcast_in_dim.19), calls=%async_computation.1 | async-start | bytes 262144 | tf_op jit(solution)/shard_map/all_to_all | solution.py:123
  101.0 1.7 multiply_reduce_fusion.1
  102.6 1.1 maximum_select_fusion.3
  103.9 1.1 fusion.8
  105.1 12.9 %all-to-all-done.1 = bf16[64,8,128]{2,1,0:T(8,128)(2,1)S(1)} async-done(((bf16[64,8,128]{2,1,0:T(8,128)(2,1)}), bf16[64,8,128]{2,1,0:T(8,128)(2,1)S(1)}, u32[]{:S(2)}, u32[]{:S(2)}) %all-to-all-start.1) | async-done | bytes 131104 | tf_op jit(solution)/shard_map/all_to_all | solution.py:123
  119.3 2.3 %collective-permute-start.6 = (f32[128,256]{1,0:T(8,128)S(1)}, f32[128,256]{1,0:T(8,128)S(1)}, u32[]{:S(2)}, u32[]{:S(2)}) collective-permute-start(f32[128,256]{1,0:T(8,128)S(1)} %dynamic-slice_bitcast_fusion), channel_id=1, source_target_pairs={{0,1},{1,0},{2,3},{3,2},{4,5},{5,4},{6,7},{7,6},{8,9},{9,8},{10,11... | collective-permute-start | bytes 393224 | tf_op jit(solution)/shard_map/ppermute | solution.py:20
  123.3 4.0 %all-to-all-start.2 = ((f32[32,4,256]{2,1,0:T(4,128)}), f32[32,4,256]{2,1,0:T(4,128)S(1)}, u32[]{:S(2)}, u32[]{:S(2)}) async-start(f32[32,4,256]{2,1,0:T(4,128)} %reshape.386), calls=%async_computation.2 | async-start | bytes 262144 | tf_op jit(solution)/shard_map/all_to_all | solution.py:138
  127.3 7.7 %inverse.1 = f32[256,256]{1,0:T(8,128)} custom-call(bf16[256,128]{1,0:T(8,128)(2,1)} %bitcast.91), custom_call_target="tpu_custom_call" | custom-call | flops 2415919104 | bytes 262144 | tf_op jit(solution)/shard_map/inverse/pallas_call | solution.py:61
  135.0 8.1 %all-to-all-done.2 = f32[32,4,256]{2,1,0:T(4,128)S(1)} async-done(((f32[32,4,256]{2,1,0:T(4,128)}), f32[32,4,256]{2,1,0:T(4,128)S(1)}, u32[]{:S(2)}, u32[]{:S(2)}) %all-to-all-start.2) | async-done | bytes 131104 | tf_op jit(solution)/shard_map/all_to_all | solution.py:138
  143.1 1.2 convolution_convert_fusion
  144.4 16.6 %all_to_all.20 = bf16[32,4,256]{2,1,0:T(4,128)(2,1)S(1)} all-to-all(bf16[32,4,256]{2,1,0:T(4,128)(2,1)S(1)} %broadcast_in_dim.20), channel_id=1, replica_groups=mesh['y'=4,'xh'=2,'z'=16,'xl'=2,'c'=2] {'z','xl'}, dimensions={0} | all-to-all | bytes 131072 | tf_op jit(solution)/shard_map/all_to_all | solution.py:143
  161.1 3.9 %collective-permute-start.7 = (bf16[128,256]{1,0:T(8,128)(2,1)S(1)}, bf16[128,256]{1,0:T(8,128)(2,1)S(1)}, u32[]{:S(2)}, u32[]{:S(2)}) collective-permute-start(bf16[128,256]{1,0:T(8,128)(2,1)S(1)} %reshape.387), channel_id=1, source_target_pairs={{0,1},{1,0},{2,3},{3,2},{4,5},{5,4},{6,7},{7,6},{8,9},{9,8},{10,11... | collective-permute-start | bytes 196616 | tf_op jit(solution)/shard_map/ppermute | solution.py:20
  166.6 0.9 copy.28
  (43 shorter events, 7.5 us)
Async XLA Ops:
  2.8 7.6 %copy-start.3 = (bf16[3,32,256]{2,1,0:T(8,128)(2,1)S(1)}, bf16[3,32,256]{2,1,0:T(8,128)(2,1)}, u32[]{:S(2)}) copy-start(bf16[3,32,256]{2,1,0:T(8,128)(2,1)} %param.4) | copy-start | bytes 147460
  2.8 74.1 %all-to-all-start = ((bf16[8,768,256]{2,1,0:T(8,128)(2,1)}), bf16[8,768,256]{2,1,0:T(8,128)(2,1)S(1)}, u32[]{:S(2)}, u32[]{:S(2)}) async-start(bf16[8,768,256]{2,1,0:T(8,128)(2,1)} %broadcast_in_dim.17), calls=%async_computation | async-start | bytes 6291456 | tf_op jit(solution)/shard_map/all_to_all | solution.py:75
  10.4 48.2 %copy-start.4 = (s32[2,256]{1,0:T(2,128)S(1)}, s32[2,256]{1,0:T(2,128)}, u32[]{:S(2)}) copy-start(s32[2,256]{1,0:T(2,128)} %param.5) | copy-start | bytes 6148
  45.1 0.9 copy-start.1
  46.8 11.9 %collective-permute-start.1 = (bf16[2,16,32,256]{3,2,1,0:T(8,128)(2,1)}, bf16[2,16,32,256]{3,2,1,0:T(8,128)(2,1)}, u32[]{:S(2)}, u32[]{:S(2)}) collective-permute-start(bf16[2,16,32,256]{3,2,1,0:T(8,128)(2,1)} %bitcast.1), channel_id=1, source_target_pairs={{0,2},{2,0},{1,3},{3,1},{4,6},{6,4},{5,7},{7,5},{8,10},{10,8},{9,1... | collective-permute-start | bytes 1572872 | tf_op jit(solution)/shard_map/ppermute | solution.py:20
  49.3 21.8 %collective-permute-start = (bf16[2,16,32,256]{3,2,1,0:T(8,128)(2,1)}, bf16[2,16,32,256]{3,2,1,0:T(8,128)(2,1)}, u32[]{:S(2)}, u32[]{:S(2)}) collective-permute-start(bf16[2,16,32,256]{3,2,1,0:T(8,128)(2,1)} %bitcast.1), channel_id=1, source_target_pairs={{0,1},{1,0},{2,3},{3,2},{4,5},{5,4},{6,7},{7,6},{8,9},{9,8},{10,11... | collective-permute-start | bytes 1572872 | tf_op jit(solution)/shard_map/ppermute | solution.py:20
  58.7 27.2 %collective-permute-start.3 = (bf16[1,16,32,256]{3,2,1,0:T(8,128)(2,1)S(1)}, bf16[1,16,32,256]{3,2,1,0:T(8,128)(2,1)}, u32[]{:S(2)}, u32[]{:S(2)}) collective-permute-start(bf16[1,16,32,256]{3,2,1,0:T(8,128)(2,1)S(1)} %bitcast.80), channel_id=1, source_target_pairs={{0,2},{2,0},{1,3},{3,1},{4,6},{6,4},{5,7},{7,5},{8,10},{10,8},{9,1... | collective-permute-start | bytes 786440 | tf_op jit(solution)/shard_map/ppermute | solution.py:20
  61.8 11.1 %collective-permute-start.4 = (bf16[1,16,32,256]{3,2,1,0:T(8,128)(2,1)S(1)}, bf16[1,16,32,256]{3,2,1,0:T(8,128)(2,1)S(1)}, u32[]{:S(2)}, u32[]{:S(2)}) collective-permute-start(bf16[1,16,32,256]{3,2,1,0:T(8,128)(2,1)S(1)} %bitcast.81), channel_id=1, source_target_pairs={{0,1},{1,0},{2,3},{3,2},{4,5},{5,4},{6,7},{7,6},{8,9},{9,8},{10,11... | collective-permute-start | bytes 786440 | tf_op jit(solution)/shard_map/ppermute | solution.py:20
  69.1 4.9 %collective-permute-start.2 = (bf16[2,16,32,256]{3,2,1,0:T(8,128)(2,1)}, bf16[2,16,32,256]{3,2,1,0:T(8,128)(2,1)S(1)}, u32[]{:S(2)}, u32[]{:S(2)}) collective-permute-start(bf16[2,16,32,256]{3,2,1,0:T(8,128)(2,1)} %collective-permute-done.1), channel_id=1, source_target_pairs={{0,1},{1,0},{2,3},{3,2},{4,5},{5,4},{6,7},{7,6},{8,9},{9,8},{10,11... | collective-permute-start | bytes 1572872 | tf_op jit(solution)/shard_map/ppermute | solution.py:20
  86.7 16.0 %collective-permute-start.5 = (bf16[1,16,32,256]{3,2,1,0:T(8,128)(2,1)}, bf16[1,16,32,256]{3,2,1,0:T(8,128)(2,1)S(1)}, u32[]{:S(2)}, u32[]{:S(2)}) collective-permute-start(bf16[1,16,32,256]{3,2,1,0:T(8,128)(2,1)} %collective-permute-done.3), channel_id=1, source_target_pairs={{0,1},{1,0},{2,3},{3,2},{4,5},{5,4},{6,7},{7,6},{8,9},{9,8},{10,11... | collective-permute-start | bytes 786440 | tf_op jit(solution)/shard_map/ppermute | solution.py:20
  91.1 26.9 %all-to-all-start.1 = ((bf16[64,8,128]{2,1,0:T(8,128)(2,1)}), bf16[64,8,128]{2,1,0:T(8,128)(2,1)S(1)}, u32[]{:S(2)}, u32[]{:S(2)}) async-start(bf16[64,8,128]{2,1,0:T(8,128)(2,1)} %broadcast_in_dim.19), calls=%async_computation.1 | async-start | bytes 262144 | tf_op jit(solution)/shard_map/all_to_all | solution.py:123
  101.0 2.8 %copy-start.2 = (bf16[1,16,1,2,32,256]{5,4,3,2,1,0:T(8,128)(2,1)S(1)}, bf16[1,16,1,2,32,256]{5,4,3,2,1,0:T(8,128)(2,1)}, u32[]{:S(2)}) copy-start(bf16[1,16,1,2,32,256]{5,4,3,2,1,0:T(8,128)(2,1)} %copy_select_fusion.1) | copy-start | bytes 1572868
  105.0 13.6 %copy-start = (bf16[2,768,2,128]{3,1,2,0:T(8,128)(2,1)S(1)}, bf16[2,768,2,128]{3,1,2,0:T(8,128)(2,1)}, u32[]{:S(2)}) copy-start(bf16[2,768,2,128]{3,1,2,0:T(8,128)(2,1)} %copy.20) | copy-start | bytes 2359300
  119.3 3.3 %collective-permute-start.6 = (f32[128,256]{1,0:T(8,128)S(1)}, f32[128,256]{1,0:T(8,128)S(1)}, u32[]{:S(2)}, u32[]{:S(2)}) collective-permute-start(f32[128,256]{1,0:T(8,128)S(1)} %dynamic-slice_bitcast_fusion), channel_id=1, source_target_pairs={{0,1},{1,0},{2,3},{3,2},{4,5},{5,4},{6,7},{7,6},{8,9},{9,8},{10,11... | collective-permute-start | bytes 393224 | tf_op jit(solution)/shard_map/ppermute | solution.py:20
  123.3 19.8 %all-to-all-start.2 = ((f32[32,4,256]{2,1,0:T(4,128)}), f32[32,4,256]{2,1,0:T(4,128)S(1)}, u32[]{:S(2)}, u32[]{:S(2)}) async-start(f32[32,4,256]{2,1,0:T(4,128)} %reshape.386), calls=%async_computation.2 | async-start | bytes 262144 | tf_op jit(solution)/shard_map/all_to_all | solution.py:138
  161.1 4.8 %collective-permute-start.7 = (bf16[128,256]{1,0:T(8,128)(2,1)S(1)}, bf16[128,256]{1,0:T(8,128)(2,1)S(1)}, u32[]{:S(2)}, u32[]{:S(2)}) collective-permute-start(bf16[128,256]{1,0:T(8,128)(2,1)S(1)} %reshape.387), channel_id=1, source_target_pairs={{0,1},{1,0},{2,3},{3,2},{4,5},{5,4},{6,7},{7,6},{8,9},{9,8},{10,11... | collective-permute-start | bytes 196616 | tf_op jit(solution)/shard_map/ppermute | solution.py:20

commit v3 on v0

v3 whole, which is shorter than its diff:
```python
import math

import jax
import jax.numpy as jnp
from jax import lax
from jax.experimental import pallas as pl
from jax.experimental.pallas import tpu as pltpu
from jax.sharding import Mesh
from jax.sharding import PartitionSpec as P

NSTEPS = 6
AXES = ("y", "xh", "z", "xl", "c")
SIZES = (4, 2, 16, 2, 2)
HEAD = ("y", "xh")
SEQ = ("z", "xl", "c")
CHIPS = ("z", "xl")

VMEM = pl.BlockSpec(memory_space=pltpu.VMEM)
SMEM = pl.BlockSpec(memory_space=pltpu.SMEM)
ANY = pl.BlockSpec(memory_space=pltpu.HBM)
BF16 = jnp.bfloat16
F32 = jnp.float32
ROWS = (((1,), (1,)), ((), ()))
COLS = (((0,), (0,)), ((), ()))


def call(kernel, name, outs, ins, flops, nbytes, scratch=(), exps=0):
    return pl.pallas_call(
        kernel,
        out_shape=outs,
        in_specs=ins,
        out_specs=jax.tree.map(lambda _: VMEM, outs),
        scratch_shapes=list(scratch),
        cost_estimate=pl.CostEstimate(flops=flops, bytes_accessed=nbytes, transcendentals=exps),
        compiler_params=pltpu.CompilerParams(vmem_limit_bytes=16 << 20),
        name=name,
    )


def shift(value, axis, step):
    size = lax.axis_size(axis)
    return lax.ppermute(value, axis, [(i, (i + step) % size) for i in range(size)])


def high(left, right, dims=(((1,), (0,)), ((), ()))):
    return lax.dot_general(
        left, right, dims, precision=lax.Precision.HIGHEST, preferred_element_type=F32
    )


def side_norm(rows):
    rows32 = rows.astype(F32)
    ones = jnp.ones((8, rows.shape[1]), F32)
    return high(ones, rows32 * rows32, ROWS)[:1]


def down_norm(rows):
    rows32 = rows.astype(F32)
    return jnp.sum(rows32 * rows32, 1, keepdims=True)


def gauss(left, right, left_norm, right_norm):
    product = lax.dot_general(left, right, ROWS, preferred_element_type=F32)
    return jnp.exp((left_norm + right_norm - 2.0 * product) * (-0.5 / math.sqrt(left.shape[1])))


def load(kinds, first, tokens, pieces, x, w, sems):
    xl, c = lax.axis_index("xl"), lax.axis_index("c")
    places = ((xl, c), (xl, 1 - c), (1 - xl, c), (1 - xl, 1 - c))
    copies = []
    for piece, (row, core) in zip(pieces, places, strict=True):
        copies.append(
            pltpu.make_async_copy(
                piece.at[pl.ds(first, kinds)], w.at[:, :, row, core], sems.at[len(copies)]
            )
        )
    width = tokens.shape[2]
    for block in range(tokens.shape[0]):
        copies.append(
            pltpu.make_async_copy(
                tokens.at[block], x.at[:, pl.ds(block * width, width)], sems.at[len(copies)]
            )
        )
    for copy in copies:
        copy.start()
    for copy in copies:
        copy.wait()


def query_key_kernel(
    pos_ref, tokens, column, core, across, both, query, keys, spread, x, w, full, block, sems
):
    rows = x.shape[0]
    load(2, 0, tokens, (column, core, across, both), x, w, sems)
    depth = x.shape[1]

    @pl.loop(0, 3)
    def _(step):
        here = pl.ds(pl.multiple_of(step * (rows // 3), rows // 3), rows // 3)
        left = x[here, :]
        for kind, out in ((0, query), (1, keys)):
            flat = jnp.dot(left, w[kind].reshape(depth, -1), preferred_element_type=F32)
            for head in range(2):
                full[kind * 2 + head, here, :] = flat[:, head * 128 : (head + 1) * 128]
            out[here, :] = flat.astype(BF16)

    group = (lax.axis_index("z") * 2 + lax.axis_index("xl")) * 2 + lax.axis_index("c")
    for head in range(2):
        for mark in range(4):
            row = pos_ref[head, group * 4 + mark] - group * rows
            block[pl.ds(head * 4 + mark, 1), :] = full[(mark % 2) * 2 + head, pl.ds(row, 1), :]
    chosen = block[...].astype(BF16)
    for place in range(spread.shape[0]):
        spread[place] = chosen


def value_kernel(tokens, column, core, across, both, keys, values, norms, x, w, sems):
    rows, depth = x.shape
    load(1, 2, tokens, (column, core, across, both), x, w, sems)

    @pl.loop(0, 3)
    def _(step):
        here = pl.ds(pl.multiple_of(step * (rows // 3), rows // 3), rows // 3)
        flat = jnp.dot(x[here, :], w[0].reshape(depth, -1), preferred_element_type=F32)
        values[here, :] = flat.astype(BF16)
        for head in range(2):
            norms[head, here, :] = down_norm(keys[here, pl.ds(head * 128, 128)])


def summary_kernel(own, other, keys, values, norms, marks, give, keep, flat, part):
    c = lax.axis_index("c")
    flat[c] = own[...].reshape(256, 128).astype(F32)
    flat[1 - c] = other[...].reshape(256, 128).astype(F32)
    for head in range(2):
        pieces = [
            flat[core, pl.ds(head * 4 + mark, 32, stride=8), :]
            for core in range(2)
            for mark in range(4)
        ]
        marks[head] = jnp.concatenate(pieces, 0).astype(BF16)

    for head in range(2):
        rows = marks[head]
        cols = pl.ds(head * 128, 128)
        weights = gauss(keys[:, cols], rows, norms[head], side_norm(rows)).astype(BF16)
        part[head] = lax.dot_general(values[:, cols], weights, COLS, preferred_element_type=F32)

    for out, head in ((give, 1 - c), (keep, c)):
        for half in range(2):
            for four in range(4):
                out[pl.ds(half * 4 + four, 32, stride=8), :] = part[
                    head, pl.ds(four * 32, 32), pl.ds(half * 128, 128)
                ]


def inverse_kernel(marks_ref, inverse_ref):
    marks = marks_ref[lax.axis_index("c")]
    inner = gauss(marks, marks, down_norm(marks), side_norm(marks))
    scale_cols = jnp.max(jnp.sum(jnp.abs(inner), 0, keepdims=True), 1, keepdims=True)
    scale_rows = jnp.max(jnp.sum(jnp.abs(inner), 1, keepdims=True), 0, keepdims=True)
    iterate = inner / (scale_cols * scale_rows)
    for step in range(NSTEPS):
        iterate = 2.0 * iterate - high(high(iterate, inner), iterate)
    inverse_ref[...] = iterate


def mixed_kernel(pieces, inverse, spread):
    summed = jnp.sum(pieces[...], 0)
    left = high(summed, inverse[:, :128], ROWS)
    right = high(summed, inverse[:, 128:], ROWS)
    mixed = left[:4] + right[4:]
    chosen = jnp.concatenate([mixed[:, :128], mixed[:, 128:]], 0).astype(BF16)
    for place in range(spread.shape[0]):
        spread[place] = chosen


def query_weight_kernel(query, marks, weights):
    for head in range(2):
        rows = marks[head]
        left = query[:, pl.ds(head * 128, 128)]
        weights[head] = gauss(left, rows, down_norm(left), side_norm(rows)).astype(BF16)


def output_kernel(own, other, weights, out, flat):
    c = lax.axis_index("c")
    flat[c] = own[...].reshape(256, 128).astype(F32)
    flat[1 - c] = other[...].reshape(256, 128).astype(F32)
    for head in range(2):
        halves = [
            jnp.concatenate(
                [flat[head, pl.ds(half * 4 + four, 32, stride=8), :] for four in range(4)], 0
            )
            for half in range(2)
        ]
        mixed = jnp.concatenate(halves, 1).astype(BF16)
        out[:, pl.ds(head * 128, 128)] = lax.dot_general(
            weights[head], mixed, ROWS, preferred_element_type=F32
        ).astype(BF16)


def shape(dims, dtype):
    return jax.ShapeDtypeStruct(dims, dtype)


def shards(tokens, weights, landmark_pos):
    whole = lax.all_to_all(
        jnp.broadcast_to(tokens[None], (8,) + tokens.shape), HEAD, 0, 0, tiled=True
    )
    column = lax.all_gather(weights, "z", axis=1, tiled=True).reshape(3, 16, 32, 256)
    across, core = shift(column, "xl", 1), shift(column, "c", 1)
    both = shift(across, "c", 1)
    whole, column, core, across, both = (
        pltpu.with_memory_space_constraint(value, pltpu.HBM)
        for value in (whole, column, core, across, both)
    )
    place = pltpu.VMEM((768, 2048), BF16)
    sems = pltpu.SemaphoreType.DMA((12,))
    query, keys, spread = call(
        query_key_kernel,
        "query_keys",
        (shape((768, 256), BF16), shape((768, 256), BF16), shape((32, 8, 128), BF16)),
        [SMEM] + [ANY] * 5,
        2 * 768 * 2048 * 512,
        5 << 20,
        [
            place,
            pltpu.VMEM((2, 16, 2, 2, 32, 256), BF16),
            pltpu.VMEM((4, 768, 128), F32),
            pltpu.VMEM((8, 128), F32),
            sems,
        ],
    )(landmark_pos, whole, column, core, across, both)
    own_marks = lax.all_to_all(spread, CHIPS, 0, 0, tiled=True)
    values, norms = call(
        value_kernel,
        "values",
        (shape((768, 256), BF16), shape((2, 768, 1), F32)),
        [ANY] * 5 + [VMEM],
        2 * 768 * 2048 * 256,
        4 << 20,
        [place, pltpu.VMEM((1, 16, 2, 2, 32, 256), BF16), sems],
    )(whole, column, core, across, both, keys)
    own_marks, values = lax.optimization_barrier((own_marks, values))
    other_marks = shift(own_marks, "c", 1)
    marks, give, keep = call(
        summary_kernel,
        "summary",
        (shape((2, 256, 128), BF16), shape((256, 128), F32), shape((256, 128), F32)),
        [VMEM] * 5,
        2 * 2 * 2 * 768 * 256 * 128,
        2 << 20,
        [pltpu.VMEM((2, 256, 128), F32), pltpu.VMEM((2, 128, 256), F32)],
        2 * 768 * 256,
    )(own_marks, other_marks, keys, values, norms)
    chip = keep + shift(give, "c", 1)
    chip, marks = lax.optimization_barrier((chip, marks))
    inverse = call(
        inverse_kernel,
        "inverse",
        shape((256, 256), F32),
        [VMEM],
        2 * 6 * 12 * 256**3,
        1 << 19,
        (),
        256 * 256,
    )(marks)
    pieces = lax.all_to_all(chip.reshape(32, 8, 128), CHIPS, 0, 0, tiled=True)
    mixed = call(
        mixed_kernel,
        "mixed",
        shape((32, 8, 128), BF16),
        [VMEM] * 2,
        2 * 6 * 16 * 256 * 128,
        1 << 19,
    )(pieces, inverse)
    mixed, marks, query = lax.optimization_barrier((mixed, marks, query))
    own_mixed = lax.all_to_all(mixed, CHIPS, 0, 0, tiled=True)
    query_weights = call(
        query_weight_kernel,
        "query_weights",
        shape((2, 768, 256), BF16),
        [VMEM] * 2,
        2 * 2 * 768 * 256 * 128,
        2 << 20,
        (),
        2 * 768 * 256,
    )(query, marks)
    own_mixed, query_weights = lax.optimization_barrier((own_mixed, query_weights))
    other_mixed = shift(own_mixed, "c", 1)
    return call(
        output_kernel,
        "attended",
        shape((768, 256), BF16),
        [VMEM] * 3,
        2 * 2 * 768 * 256 * 128,
        2 << 20,
        [pltpu.VMEM((2, 256, 128), F32)],
    )(own_mixed, other_mixed, query_weights)


def solution(mesh):
    fine = Mesh(mesh.devices.reshape(SIZES), AXES)
    return jax.shard_map(
        shards,
        mesh=fine,
        in_specs=(P(SEQ, HEAD), P(None, SEQ, HEAD), P(HEAD, None)),
        out_specs=P(SEQ, HEAD),
        check_vma=False,
    )
```

time: 708 us -> 156 us (0.22)
  waiting for transfers between devices: 610 us -> 39.7 us
  starting transfers between devices: 0.08 us -> 56.9 us
  blocking collectives: 62.3 us -> 35.3 us
  Pallas kernels: 0 us -> 20 us
  matrix products: 18.2 us -> 0 us
  between operations: 13.3 us -> 0.15 us
    psum x1 -> x0, waiting for transfers between devices: 399 us -> none  [shards(): summary = lax.psum(partial_sum, 'seq')]
    all_gather x2 -> x0, waiting for transfers between devices: 210 us -> none  [the longest x1 124 us: shards(): lax.all_gather(weights, 'seq', axis=1, tiled=True)]
    all_to_all x0 -> x4, waiting for transfers between devices: none -> 29.8 us  [the longest x1 11.7 us: shards(): own_mixed = lax.all_to_all(mixed, CHIPS, 0, 0, tiled=True)]
    ppermute x0 -> x6, starting transfers between devices: none -> 29.5 us  [shift(): lax.ppermute(value, axis, [(i, (i + step) % size) for i in range(size)])]
    all_to_all x0 -> x4, starting transfers between devices: none -> 27.3 us  [the longest x1 11.9 us: shards(): own_marks = lax.all_to_all(spread, CHIPS, 0, 0, tiled=True)]
    all_gather x1, blocking collectives: 62.3 us -> 35.3 us  [shards(): lax.all_gather(weights, 'z', axis=1, tiled=True).reshape(3, 16, 32, 256)]
    pallas_call x0 -> x7, Pallas kernels: none -> 20 us  [the longest x1 6.12 us: shards(): call(inverse_kernel, 'inverse', shape((256, 256), F32), [VMEM], 2 * 6 * 1...]
    dot_general x19 -> x0, matrix products: 18.2 us -> none  [the longest x13 9.65 us: batched(): jnp.einsum('hij,hjk->hik', left, right, precision=lax.Precision.HIGHEST)]
  transfers between devices with their start and end apart: 3 -> 10, of which waited for: 3 -> 8; matrix products, arithmetic and copies ran while one was open for 0% -> 0% of each run, Pallas kernels for 0% -> 7%
where the time goes in v3:
time: 156 us
  starting transfers between devices  56.9 us (36%)
  waiting for transfers between devices  39.7 us (25%)
  blocking collectives  35.3 us (23%)
  Pallas kernels  20 us (13%)
  local copies, waits for them, and re-layouts  2.9 us (2%)
    all_gather x1, blocking collectives, shards(): lax.all_gather(weights, 'z', axis=1, tiled=True).reshape(3, 16, 32, 256)  35.3 us
    ppermute x6, starting transfers between devices, shift(): lax.ppermute(value, axis, [(i, (i + step) % size) for i in range(size)])  29.5 us
    all_to_all x1, starting transfers between devices, shards(): own_marks = lax.all_to_all(spread, CHIPS, 0, 0, tiled=True)  11.9 us
    all_to_all x1, waiting for transfers between devices, shards(): own_mixed = lax.all_to_all(mixed, CHIPS, 0, 0, tiled=True)  11.7 us
    ppermute x6, waiting for transfers between devices, shift(): lax.ppermute(value, axis, [(i, (i + step) % size) for i in range(size)])  9.9 us
    all_to_all x1, waiting for transfers between devices, shards(): pieces = lax.all_to_all(chip.reshape(32, 8, 128), CHIPS, 0, 0, tiled=True)  9.2 us
    all_to_all x1, waiting for transfers between devices, shards(): own_marks = lax.all_to_all(spread, CHIPS, 0, 0, tiled=True)  8.98 us
    all_to_all x1, starting transfers between devices, shards(): lax.all_to_all(jnp.broadcast_to(tokens[None], (8,) + tokens.shape), HEAD,...  7.61 us
  transfers between devices with their start and end apart: 10, of which 8 were waited for; matrix products, arithmetic and copies ran while one was open for 0% of the time, Pallas kernels for 7%

profile of v3, /device:TPU:1, one launch (start us, length us, event | category | flops | bytes accessed | tf_op | source)
XLA Modules:
  0.0 155.7 jit_solution(4465821110711480805)
XLA Ops:
  0.0 2.9 %broadcast_in_dim.2 = bf16[8,768,256]{2,1,0:T(8,128)(2,1)} broadcast(bf16[768,256]{1,0:T(8,128)(2,1)} %param.3), dimensions={1,2} | broadcast | bytes 3538944 | tf_op jit(solution)/shard_map/broadcast_in_dim | solution.py:207
  2.9 7.6 %all-to-all-start = ((bf16[8,768,256]{2,1,0:T(8,128)(2,1)}), bf16[8,768,256]{2,1,0:T(8,128)(2,1)}, u32[]{:S(2)}, u32[]{:S(2)}) async-start(bf16[8,768,256]{2,1,0:T(8,128)(2,1)} %broadcast_in_dim.2), calls=%async_computation | async-start | bytes 6291456 | tf_op jit(solution)/shard_map/all_to_all | solution.py:206
  10.5 0.0 copy-done.4
  10.5 35.3 %all_gather.3 = bf16[3,512,256]{2,1,0:T(8,128)(2,1)S(1)} all-gather(bf16[3,32,256]{2,1,0:T(8,128)(2,1)S(1)} %copy-done.4), channel_id=1, replica_groups=mesh['y'=4,'xh'=2,'z'=16,'xl'=2,'c'=2] {'z'}, dimensions={1}, use_global_device_ids=true | all-gather | bytes 835584 | tf_op jit(solution)/shard_map/all_gather | solution.py:209
  45.8 2.6 %collective-permute-start.1 = (bf16[3,16,32,256]{3,2,1,0:T(8,128)(2,1)S(1)}, bf16[3,16,32,256]{3,2,1,0:T(8,128)(2,1)S(1)}, u32[]{:S(2)}, u32[]{:S(2)}) collective-permute-start(bf16[3,16,32,256]{3,2,1,0:T(8,128)(2,1)S(1)} %bitcast.2), channel_id=1, source_target_pairs={{0,2},{2,0},{1,3},{3,1},{4,6},{6,4},{5,7},{7,5},{8,10},{10,8},{9,1... | collective-permute-start | bytes 2359304 | tf_op jit(solution)/shard_map/ppermute | solution.py:42
  48.5 7.4 %collective-permute-start = (bf16[3,16,32,256]{3,2,1,0:T(8,128)(2,1)S(1)}, bf16[3,16,32,256]{3,2,1,0:T(8,128)(2,1)S(1)}, u32[]{:S(2)}, u32[]{:S(2)}) collective-permute-start(bf16[3,16,32,256]{3,2,1,0:T(8,128)(2,1)S(1)} %bitcast.3), channel_id=1, source_target_pairs={{0,1},{1,0},{2,3},{3,2},{4,5},{5,4},{6,7},{7,6},{8,9},{9,8},{10,11... | collective-permute-start | bytes 2359304 | tf_op jit(solution)/shard_map/ppermute | solution.py:42
  55.9 5.2 %collective-permute-done.1.across = bf16[3,16,32,256]{3,2,1,0:T(8,128)(2,1)S(1)} collective-permute-done((bf16[3,16,32,256]{3,2,1,0:T(8,128)(2,1)S(1)}, bf16[3,16,32,256]{3,2,1,0:T(8,128)(2,1)S(1)}, u32[]{:S(2)}, u32[]{:S(2)}) %collective-permute-start.1) | collective-permute-done | bytes 786464 | tf_op jit(solution)/shard_map/ppermute | solution.py:42
  61.1 8.5 %collective-permute-start.2 = (bf16[3,16,32,256]{3,2,1,0:T(8,128)(2,1)S(1)}, bf16[3,16,32,256]{3,2,1,0:T(8,128)(2,1)}, u32[]{:S(2)}, u32[]{:S(2)}) collective-permute-start(bf16[3,16,32,256]{3,2,1,0:T(8,128)(2,1)S(1)} %collective-permute-done.1.across), channel_id=1, source_target_pairs={{0,1},{1,0},{2,3},{3,2},{4,5},{5,4},{6,7},{7,6},{8,9},{9,8},{10,11... | collective-permute-start | bytes 2359304 | tf_op jit(solution)/shard_map/ppermute | solution.py:42
  69.6 0.0 collective-permute-done.core
  69.6 2.0 %collective-permute-done.2.both = bf16[3,16,32,256]{3,2,1,0:T(8,128)(2,1)} collective-permute-done((bf16[3,16,32,256]{3,2,1,0:T(8,128)(2,1)S(1)}, bf16[3,16,32,256]{3,2,1,0:T(8,128)(2,1)}, u32[]{:S(2)}, u32[]{:S(2)}) %collective-permute-start.2) | collective-permute-done | bytes 786464 | tf_op jit(solution)/shard_map/ppermute | solution.py:42
  71.6 0.0 copy-done.3
  71.6 0.0 all-to-all-done.tokens
  71.6 5.9 %query_keys.1 = (bf16[768,256]{1,0:T(8,128)(2,1)S(1)}, bf16[768,256]{1,0:T(8,128)(2,1)S(1)}, bf16[32,8,128]{2,1,0:T(8,128)(2,1)}) custom-call(s32[2,256]{1,0:T(2,128)S(1)} %copy-done, bf16[8,768,256]{2,1,0:T(8,128)(2,1)} %all-to-all-done.tokens, bf16[3,16,32,256]{3,2,1,0:T(8,128)(2,1)} %bitcast.4, bf16[3,16,32,256]{3,2,1,0:T(8,128)(2,1)} %copy-done.3, ...), custom_call_target="tpu_custom_call" | custom-call | flops 1610612736 | bytes 5242880 | tf_op jit(solution)/shard_map/query_keys/pallas_call | solution.py:218
  77.6 11.9 %all-to-all-start.1 = ((bf16[32,8,128]{2,1,0:T(8,128)(2,1)}), bf16[32,8,128]{2,1,0:T(8,128)(2,1)S(1)}, u32[]{:S(2)}, u32[]{:S(2)}) async-start(bf16[32,8,128]{2,1,0:T(8,128)(2,1)} %get-tuple-element.22), calls=%async_computation.1 | async-start | bytes 131072 | tf_op jit(solution)/shard_map/all_to_all | solution.py:233
  89.5 3.6 %values.1 = (bf16[768,256]{1,0:T(8,128)(2,1)S(1)}, f32[2,768,1]{2,1,0:T(8,128)S(1)}) custom-call(bf16[8,768,256]{2,1,0:T(8,128)(2,1)} %all-to-all-done.tokens, bf16[3,16,32,256]{3,2,1,0:T(8,128)(2,1)} %bitcast.5, bf16[3,16,32,256]{3,2,1,0:T(8,128)(2,1)} %copy-done.3, bf16[3,16,32,256]{3,2,1,0:T(8,128)(2,1)} %copy-done.2, ...), custom_call_target="tpu_custom_call" | custom-call | flops 805306368 | bytes 4194304 | tf_op jit(solution)/shard_map/values/pallas_call | solution.py:234
  93.1 9.0 %all-to-all-done.1.own = bf16[32,8,128]{2,1,0:T(8,128)(2,1)S(1)} async-done(((bf16[32,8,128]{2,1,0:T(8,128)(2,1)}), bf16[32,8,128]{2,1,0:T(8,128)(2,1)S(1)}, u32[]{:S(2)}, u32[]{:S(2)}) %all-to-all-start.1) | async-done | bytes 65568 | tf_op jit(solution)/shard_map/all_to_all | solution.py:233
  102.0 4.0 %collective-permute-start.3 = (bf16[32,8,128]{2,1,0:T(8,128)(2,1)S(1)}, bf16[32,8,128]{2,1,0:T(8,128)(2,1)S(1)}, u32[]{:S(2)}, u32[]{:S(2)}) collective-permute-start(bf16[32,8,128]{2,1,0:T(8,128)(2,1)S(1)} %all-to-all-done.1.own), channel_id=1, source_target_pairs={{0,1},{1,0},{2,3},{3,2},{4,5},{5,4},{6,7},{7,6},{8,9},{9,8},{10,11... | collective-permute-start | bytes 196616 | tf_op jit(solution)/shard_map/ppermute | solution.py:42
  106.0 0.9 collective-permute-done.3.other
  106.9 1.2 summary.1
  108.1 2.3 %collective-permute-start.4 = (f32[256,128]{1,0:T(8,128)S(1)}, f32[256,128]{1,0:T(8,128)S(1)}, u32[]{:S(2)}, u32[]{:S(2)}) collective-permute-start(f32[256,128]{1,0:T(8,128)S(1)} %get-tuple-element.29), channel_id=1, source_target_pairs={{0,1},{1,0},{2,3},{3,2},{4,5},{5,4},{6,7},{7,6},{8,9},{9,8},{10,11... | collective-permute-start | bytes 393224 | tf_op jit(solution)/shard_map/ppermute | solution.py:42
  110.4 1.0 collective-permute-done.4
  111.4 0.7 add.3
  112.0 3.9 %all-to-all-start.2 = ((f32[32,8,128]{2,1,0:T(8,128)}), f32[32,8,128]{2,1,0:T(8,128)S(1)}, u32[]{:S(2)}, u32[]{:S(2)}) async-start(f32[32,8,128]{2,1,0:T(8,128)} %bitcast.1), calls=%async_computation.2 | async-start | bytes 262144 | tf_op jit(solution)/shard_map/all_to_all | solution.py:267
  115.9 6.1 %inverse.1 = f32[256,256]{1,0:T(8,128)S(1)} custom-call(bf16[2,256,128]{2,1,0:T(8,128)(2,1)S(1)} %get-tuple-element.36.marks_ref.marks), custom_call_target="tpu_custom_call" | custom-call | flops 2415919104 | bytes 524288 | tf_op jit(solution)/shard_map/inverse/pallas_call | solution.py:257
  122.0 9.2 %all-to-all-done.2.pieces = f32[32,8,128]{2,1,0:T(8,128)S(1)} async-done(((f32[32,8,128]{2,1,0:T(8,128)}), f32[32,8,128]{2,1,0:T(8,128)S(1)}, u32[]{:S(2)}, u32[]{:S(2)}) %all-to-all-start.2) | async-done | bytes 131104 | tf_op jit(solution)/shard_map/all_to_all | solution.py:267
  131.2 1.0 mixed.1
  132.2 4.0 %all-to-all-start.3 = ((bf16[32,8,128]{2,1,0:T(8,128)(2,1)}), bf16[32,8,128]{2,1,0:T(8,128)(2,1)S(1)}, u32[]{:S(2)}, u32[]{:S(2)}) async-start(bf16[32,8,128]{2,1,0:T(8,128)(2,1)} %mixed.1), calls=%async_computation.3 | async-start | bytes 131072 | tf_op jit(solution)/shard_map/all_to_all | solution.py:277
  136.2 1.0 query_weights.1.weights
  137.2 11.7 %all-to-all-done.3.own = bf16[32,8,128]{2,1,0:T(8,128)(2,1)S(1)} async-done(((bf16[32,8,128]{2,1,0:T(8,128)(2,1)}), bf16[32,8,128]{2,1,0:T(8,128)(2,1)S(1)}, u32[]{:S(2)}, u32[]{:S(2)}) %all-to-all-start.3) | async-done | bytes 65568 | tf_op jit(solution)/shard_map/all_to_all | solution.py:277
  148.9 4.8 %collective-permute-start.5 = (bf16[32,8,128]{2,1,0:T(8,128)(2,1)S(1)}, bf16[32,8,128]{2,1,0:T(8,128)(2,1)S(1)}, u32[]{:S(2)}, u32[]{:S(2)}) collective-permute-start(bf16[32,8,128]{2,1,0:T(8,128)(2,1)S(1)} %all-to-all-done.3.own), channel_id=1, source_target_pairs={{0,1},{1,0},{2,3},{3,2},{4,5},{5,4},{6,7},{7,6},{8,9},{9,8},{10,11... | collective-permute-start | bytes 196616 | tf_op jit(solution)/shard_map/ppermute | solution.py:42
  153.6 0.9 collective-permute-done.5.other
  154.5 1.1 attended.1
  (8 shorter events, 0.0 us)
Async XLA Ops:
  2.9 7.6 %copy-start.4 = (bf16[3,32,256]{2,1,0:T(8,128)(2,1)S(1)}, bf16[3,32,256]{2,1,0:T(8,128)(2,1)}, u32[]{:S(2)}) copy-start(bf16[3,32,256]{2,1,0:T(8,128)(2,1)} %param.4) | copy-start | bytes 147460
  2.9 68.8 %copy-start = (s32[2,256]{1,0:T(2,128)S(1)}, s32[2,256]{1,0:T(2,128)}, u32[]{:S(2)}) copy-start(s32[2,256]{1,0:T(2,128)} %pos_ref.1) | copy-start | bytes 6148
  2.9 68.7 %all-to-all-start = ((bf16[8,768,256]{2,1,0:T(8,128)(2,1)}), bf16[8,768,256]{2,1,0:T(8,128)(2,1)}, u32[]{:S(2)}, u32[]{:S(2)}) async-start(bf16[8,768,256]{2,1,0:T(8,128)(2,1)} %broadcast_in_dim.2), calls=%async_computation | async-start | bytes 6291456 | tf_op jit(solution)/shard_map/all_to_all | solution.py:206
  45.8 25.8 %copy-start.1 = (bf16[3,512,256]{2,1,0:T(8,128)(2,1)}, bf16[3,512,256]{2,1,0:T(8,128)(2,1)S(1)}, u32[]{:S(2)}) copy-start(bf16[3,512,256]{2,1,0:T(8,128)(2,1)S(1)} %all_gather.3) | copy-start | bytes 2359300
  45.8 15.2 %collective-permute-start.1 = (bf16[3,16,32,256]{3,2,1,0:T(8,128)(2,1)S(1)}, bf16[3,16,32,256]{3,2,1,0:T(8,128)(2,1)S(1)}, u32[]{:S(2)}, u32[]{:S(2)}) collective-permute-start(bf16[3,16,32,256]{3,2,1,0:T(8,128)(2,1)S(1)} %bitcast.2), channel_id=1, source_target_pairs={{0,2},{2,0},{1,3},{3,1},{4,6},{6,4},{5,7},{7,5},{8,10},{10,8},{9,1... | collective-permute-start | bytes 2359304 | tf_op jit(solution)/shard_map/ppermute | solution.py:42
  48.5 21.1 %collective-permute-start = (bf16[3,16,32,256]{3,2,1,0:T(8,128)(2,1)S(1)}, bf16[3,16,32,256]{3,2,1,0:T(8,128)(2,1)S(1)}, u32[]{:S(2)}, u32[]{:S(2)}) collective-permute-start(bf16[3,16,32,256]{3,2,1,0:T(8,128)(2,1)S(1)} %bitcast.3), channel_id=1, source_target_pairs={{0,1},{1,0},{2,3},{3,2},{4,5},{5,4},{6,7},{7,6},{8,9},{9,8},{10,11... | collective-permute-start | bytes 2359304 | tf_op jit(solution)/shard_map/ppermute | solution.py:42
  61.1 10.6 %copy-start.2 = (bf16[3,16,32,256]{3,2,1,0:T(8,128)(2,1)}, bf16[3,16,32,256]{3,2,1,0:T(8,128)(2,1)S(1)}, u32[]{:S(2)}) copy-start(bf16[3,16,32,256]{3,2,1,0:T(8,128)(2,1)S(1)} %collective-permute-done.1.across) | copy-start | bytes 2359300
  61.1 10.5 %collective-permute-start.2 = (bf16[3,16,32,256]{3,2,1,0:T(8,128)(2,1)S(1)}, bf16[3,16,32,256]{3,2,1,0:T(8,128)(2,1)}, u32[]{:S(2)}, u32[]{:S(2)}) collective-permute-start(bf16[3,16,32,256]{3,2,1,0:T(8,128)(2,1)S(1)} %collective-permute-done.1.across), channel_id=1, source_target_pairs={{0,1},{1,0},{2,3},{3,2},{4,5},{5,4},{6,7},{7,6},{8,9},{9,8},{10,11... | collective-permute-start | bytes 2359304 | tf_op jit(solution)/shard_map/ppermute | solution.py:42
  69.6 2.0 %copy-start.3 = (bf16[3,16,32,256]{3,2,1,0:T(8,128)(2,1)}, bf16[3,16,32,256]{3,2,1,0:T(8,128)(2,1)S(1)}, u32[]{:S(2)}) copy-start(bf16[3,16,32,256]{3,2,1,0:T(8,128)(2,1)S(1)} %collective-permute-done.core) | copy-start | bytes 2359300
  77.6 24.5 %all-to-all-start.1 = ((bf16[32,8,128]{2,1,0:T(8,128)(2,1)}), bf16[32,8,128]{2,1,0:T(8,128)(2,1)S(1)}, u32[]{:S(2)}, u32[]{:S(2)}) async-start(bf16[32,8,128]{2,1,0:T(8,128)(2,1)} %get-tuple-element.22), calls=%async_computation.1 | async-start | bytes 131072 | tf_op jit(solution)/shard_map/all_to_all | solution.py:233
  102.0 4.8 %collective-permute-start.3 = (bf16[32,8,128]{2,1,0:T(8,128)(2,1)S(1)}, bf16[32,8,128]{2,1,0:T(8,128)(2,1)S(1)}, u32[]{:S(2)}, u32[]{:S(2)}) collective-permute-start(bf16[32,8,128]{2,1,0:T(8,128)(2,1)S(1)} %all-to-all-done.1.own), channel_id=1, source_target_pairs={{0,1},{1,0},{2,3},{3,2},{4,5},{5,4},{6,7},{7,6},{8,9},{9,8},{10,11... | collective-permute-start | bytes 196616 | tf_op jit(solution)/shard_map/ppermute | solution.py:42
  108.1 3.2 %collective-permute-start.4 = (f32[256,128]{1,0:T(8,128)S(1)}, f32[256,128]{1,0:T(8,128)S(1)}, u32[]{:S(2)}, u32[]{:S(2)}) collective-permute-start(f32[256,128]{1,0:T(8,128)S(1)} %get-tuple-element.29), channel_id=1, source_target_pairs={{0,1},{1,0},{2,3},{3,2},{4,5},{5,4},{6,7},{7,6},{8,9},{9,8},{10,11... | collective-permute-start | bytes 393224 | tf_op jit(solution)/shard_map/ppermute | solution.py:42
  112.0 19.2 %all-to-all-start.2 = ((f32[32,8,128]{2,1,0:T(8,128)}), f32[32,8,128]{2,1,0:T(8,128)S(1)}, u32[]{:S(2)}, u32[]{:S(2)}) async-start(f32[32,8,128]{2,1,0:T(8,128)} %bitcast.1), calls=%async_computation.2 | async-start | bytes 262144 | tf_op jit(solution)/shard_map/all_to_all | solution.py:267
  132.2 16.6 %all-to-all-start.3 = ((bf16[32,8,128]{2,1,0:T(8,128)(2,1)}), bf16[32,8,128]{2,1,0:T(8,128)(2,1)S(1)}, u32[]{:S(2)}, u32[]{:S(2)}) async-start(bf16[32,8,128]{2,1,0:T(8,128)(2,1)} %mixed.1), calls=%async_computation.3 | async-start | bytes 131072 | tf_op jit(solution)/shard_map/all_to_all | solution.py:277
  148.9 5.7 %collective-permute-start.5 = (bf16[32,8,128]{2,1,0:T(8,128)(2,1)S(1)}, bf16[32,8,128]{2,1,0:T(8,128)(2,1)S(1)}, u32[]{:S(2)}, u32[]{:S(2)}) collective-permute-start(bf16[32,8,128]{2,1,0:T(8,128)(2,1)S(1)} %all-to-all-done.3.own), channel_id=1, source_target_pairs={{0,1},{1,0},{2,3},{3,2},{4,5},{5,4},{6,7},{7,6},{8,9},{9,8},{10,11... | collective-permute-start | bytes 196616 | tf_op jit(solution)/shard_map/ppermute | solution.py:42

commit v4 on v3

--- a/solution.py
+++ b/solution.py
@@ -17,7 +17,8 @@
 
 VMEM = pl.BlockSpec(memory_space=pltpu.VMEM)
 SMEM = pl.BlockSpec(memory_space=pltpu.SMEM)
-ANY = pl.BlockSpec(memory_space=pltpu.HBM)
+HBM = pl.BlockSpec(memory_space=pltpu.HBM)
+ANY = pl.BlockSpec(memory_space=pl.ANY)
 BF16 = jnp.bfloat16
 F32 = jnp.float32
 ROWS = (((1,), (1,)), ((), ()))
@@ -64,65 +65,100 @@
     return jnp.exp((left_norm + right_norm - 2.0 * product) * (-0.5 / math.sqrt(left.shape[1])))
 
 
-def load(kinds, first, tokens, pieces, x, w, sems):
-    xl, c = lax.axis_index("xl"), lax.axis_index("c")
-    places = ((xl, c), (xl, 1 - c), (1 - xl, c), (1 - xl, 1 - c))
-    copies = []
-    for piece, (row, core) in zip(pieces, places, strict=True):
+def run(copies):
+    for copy in copies:
+        copy.start()
+    for copy in copies:
+        copy.wait()
+
+
+def pick_kernel(pos_ref, tokens, picked, groups, rows, sems):
+    group = (lax.axis_index("z") * 2 + lax.axis_index("xl")) * 2 + lax.axis_index("c")
+    blocks, count, width = tokens.shape
+    places, copies = [], []
+    for mark in range(8):
+        row = pos_ref[mark // 4, group * 4 + mark % 4] - group * count
+        start = pl.multiple_of((row // 8) * 8, 8)
+        places.append(row - start)
         copies.append(
             pltpu.make_async_copy(
-                piece.at[pl.ds(first, kinds)], w.at[:, :, row, core], sems.at[len(copies)]
+                tokens.at[:, pl.ds(start, 8), :], groups.at[mark], sems.at[mark]
             )
         )
+    run(copies)
+    index = lax.broadcasted_iota(jnp.int32, (8, width), 0)
+    for mark, place in enumerate(places):
+        for block in range(blocks):
+            eight = groups[mark, block].astype(F32)
+            rows[pl.ds(mark, 1), pl.ds(block * width, width)] = jnp.sum(
+                jnp.where(index == place, eight, 0.0), 0, keepdims=True
+            )
+    picked[...] = rows[...].astype(BF16)
+
+
+def partial_kernel(own, other, column, core, keep, give, w, sems):
+    xl, c = lax.axis_index("xl"), lax.axis_index("c")
+    run(
+        [
+            pltpu.make_async_copy(column.at[pl.ds(0, 2)], w.at[:, :, c], sems.at[0]),
+            pltpu.make_async_copy(core.at[pl.ds(0, 2)], w.at[:, :, 1 - c], sems.at[1]),
+        ]
+    )
+    rows = jnp.concatenate([own[...].astype(F32), other[...].astype(F32)], 0)
+    low = lax.broadcasted_iota(jnp.int32, (16, 128), 1) < 64
+    tiles = []
+    for pair in range(8):
+        even = rows[:, pair * 256 : pair * 256 + 128]
+        odd = rows[:, pair * 256 + 128 : pair * 256 + 256]
+        first = jnp.where(low, even, pltpu.roll(odd, 64, 1))
+        second = jnp.where(low, pltpu.roll(even, 64, 1), odd)
+        tiles.append(jnp.where(xl == 0, first, second))
+    left = jnp.concatenate(tiles, 1).astype(BF16)
+    results = [
+        jnp.dot(left, w[kind].reshape(1024, 256), preferred_element_type=F32) for kind in range(2)
+    ]
+    number = lax.broadcasted_iota(jnp.int32, (16, 256), 0)
+    both = jnp.where(number % 2 == 0, results[0], results[1])
+    chosen = jnp.where((number[:, :128] % 8) < 4, both[:, :128], both[:, 128:])
+    keep[...] = chosen[:8]
+    give[...] = chosen[8:]
+
+
+def finish_kernel(keep, received, spread):
+    chosen = (keep[...] + received[...]).astype(BF16)
+    for place in range(spread.shape[0]):
+        spread[place] = chosen
+
+
+def project_kernel(
+    tokens, column, core, across, both, query, keys, values, norms, x, w, sems
+):
+    rows, depth = x.shape
+    xl, c = lax.axis_index("xl"), lax.axis_index("c")
+    places = (
+        (column, xl, c), (core, xl, 1 - c), (across, 1 - xl, c), (both, 1 - xl, 1 - c)
+    )
+    copies = [
+        pltpu.make_async_copy(piece, w.at[:, :, row, part], sems.at[number])
+        for number, (piece, row, part) in enumerate(places)
+    ]
     width = tokens.shape[2]
     for block in range(tokens.shape[0]):
         copies.append(
             pltpu.make_async_copy(
-                tokens.at[block], x.at[:, pl.ds(block * width, width)], sems.at[len(copies)]
+                tokens.at[block], x.at[:, pl.ds(block * width, width)], sems.at[4 + block]
             )
         )
-    for copy in copies:
-        copy.start()
-    for copy in copies:
-        copy.wait()
-
-
-def query_key_kernel(
-    pos_ref, tokens, column, core, across, both, query, keys, spread, x, w, full, block, sems
-):
-    rows = x.shape[0]
-    load(2, 0, tokens, (column, core, across, both), x, w, sems)
-    depth = x.shape[1]
+    run(copies)
 
     @pl.loop(0, 3)
     def _(step):
         here = pl.ds(pl.multiple_of(step * (rows // 3), rows // 3), rows // 3)
         left = x[here, :]
-        for kind, out in ((0, query), (1, keys)):
-            flat = jnp.dot(left, w[kind].reshape(depth, -1), preferred_element_type=F32)
-            for head in range(2):
-                full[kind * 2 + head, here, :] = flat[:, head * 128 : (head + 1) * 128]
-            out[here, :] = flat.astype(BF16)
-
-    group = (lax.axis_index("z") * 2 + lax.axis_index("xl")) * 2 + lax.axis_index("c")
-    for head in range(2):
-        for mark in range(4):
-            row = pos_ref[head, group * 4 + mark] - group * rows
-            block[pl.ds(head * 4 + mark, 1), :] = full[(mark % 2) * 2 + head, pl.ds(row, 1), :]
-    chosen = block[...].astype(BF16)
-    for place in range(spread.shape[0]):
-        spread[place] = chosen
-
-
-def value_kernel(tokens, column, core, across, both, keys, values, norms, x, w, sems):
-    rows, depth = x.shape
-    load(1, 2, tokens, (column, core, across, both), x, w, sems)
-
-    @pl.loop(0, 3)
-    def _(step):
-        here = pl.ds(pl.multiple_of(step * (rows // 3), rows // 3), rows // 3)
-        flat = jnp.dot(x[here, :], w[0].reshape(depth, -1), preferred_element_type=F32)
-        values[here, :] = flat.astype(BF16)
+        for kind, out in ((0, query), (1, keys), (2, values)):
+            out[here, :] = jnp.dot(
+                left, w[kind].reshape(depth, -1), preferred_element_type=F32
+            ).astype(BF16)
         for head in range(2):
             norms[head, here, :] = down_norm(keys[here, pl.ds(head * 128, 128)])
 
@@ -208,38 +244,60 @@
     )
     column = lax.all_gather(weights, "z", axis=1, tiled=True).reshape(3, 16, 32, 256)
     across, core = shift(column, "xl", 1), shift(column, "c", 1)
+    column, core = (
+        pltpu.with_memory_space_constraint(value, pltpu.HBM) for value in (column, core)
+    )
+    picked = call(
+        pick_kernel,
+        "pick",
+        shape((8, 2048), BF16),
+        [SMEM, ANY],
+        1 << 20,
+        1 << 19,
+        [
+            pltpu.VMEM((8, 8, 8, 256), BF16),
+            pltpu.VMEM((8, 2048), F32),
+            pltpu.SemaphoreType.DMA((8,)),
+        ],
+    )(landmark_pos, whole)
+    other_picked = shift(picked, "xl", 1)
+    keep, give = call(
+        partial_kernel,
+        "partial",
+        (shape((8, 128), F32), shape((8, 128), F32)),
+        [VMEM, VMEM, HBM, HBM],
+        2 * 16 * 1024 * 512,
+        1 << 20,
+        [pltpu.VMEM((2, 16, 2, 32, 256), BF16), pltpu.SemaphoreType.DMA((2,))],
+    )(picked, other_picked, column, core)
+    received = shift(give, "xl", 1)
+    spread = call(
+        finish_kernel, "finish", shape((32, 8, 128), BF16), [VMEM] * 2, 1 << 14, 1 << 16
+    )(keep, received)
+    own_marks = lax.all_to_all(spread, CHIPS, 0, 0, tiled=True)
+    across, spread = lax.optimization_barrier((across, spread))
     both = shift(across, "c", 1)
-    whole, column, core, across, both = (
-        pltpu.with_memory_space_constraint(value, pltpu.HBM)
-        for value in (whole, column, core, across, both)
-    )
-    place = pltpu.VMEM((768, 2048), BF16)
-    sems = pltpu.SemaphoreType.DMA((12,))
-    query, keys, spread = call(
-        query_key_kernel,
-        "query_keys",
-        (shape((768, 256), BF16), shape((768, 256), BF16), shape((32, 8, 128), BF16)),
-        [SMEM] + [ANY] * 5,
-        2 * 768 * 2048 * 512,
-        5 << 20,
+    across, both = (
+        pltpu.with_memory_space_constraint(value, pltpu.HBM) for value in (across, both)
+    )
+    query, keys, values, norms = call(
+        project_kernel,
+        "project",
+        (
+            shape((768, 256), BF16),
+            shape((768, 256), BF16),
+            shape((768, 256), BF16),
+            shape((2, 768, 1), F32),
+        ),
+        [ANY] + [HBM] * 4,
+        1 << 16,
+        1 << 16,
         [
-            place,
-            pltpu.VMEM((2, 16, 2, 2, 32, 256), BF16),
-            pltpu.VMEM((4, 768, 128), F32),
-            pltpu.VMEM((8, 128), F32),
-            sems,
+            pltpu.VMEM((768, 2048), BF16),
+            pltpu.VMEM((3, 16, 2, 2, 32, 256), BF16),
+            pltpu.SemaphoreType.DMA((12,)),
         ],
-    )(landmark_pos, whole, column, core, across, both)
-    own_marks = lax.all_to_all(spread, CHIPS, 0, 0, tiled=True)
-    values, norms = call(
-        value_kernel,
-        "values",
-        (shape((768, 256), BF16), shape((2, 768, 1), F32)),
-        [ANY] * 5 + [VMEM],
-        2 * 768 * 2048 * 256,
-        4 << 20,
-        [place, pltpu.VMEM((1, 16, 2, 2, 32, 256), BF16), sems],
-    )(whole, column, core, across, both, keys)
+    )(whole, column, core, across, both)
     own_marks, values = lax.optimization_barrier((own_marks, values))
     other_marks = shift(own_marks, "c", 1)
     marks, give, keep = call(

time: 156 us -> 169 us (1.083)
  waiting for transfers between devices: 39.7 us -> 46.6 us
  local copies, waits for them, and re-layouts: 2.9 us -> 8.34 us
    ppermute x6 -> x8, waiting for transfers between devices: 9.9 us -> 20.9 us  [shift(): lax.ppermute(value, axis, [(i, (i + step) % size) for i in range(size)])]
    unnamed x10 -> x16, local copies, waits for them, and re-layouts: 0.02 us -> 5.52 us
    all_to_all x1, starting transfers between devices: 11.9 us -> 6.81 us  [shards(): own_marks = lax.all_to_all(spread, CHIPS, 0, 0, tiled=True)]
    all_to_all x1, waiting for transfers between devices: 8.98 us -> 5.01 us  [shards(): own_marks = lax.all_to_all(spread, CHIPS, 0, 0, tiled=True)]
    all_to_all x1, starting transfers between devices: 3.86 us -> 6.05 us  [shards(): pieces = lax.all_to_all(chip.reshape(32, 8, 128), CHIPS, 0, 0, tiled=True)]
    ppermute x6 -> x8, starting transfers between devices: 29.5 us -> 30.8 us  [shift(): lax.ppermute(value, axis, [(i, (i + step) % size) for i in range(size)])]
    pallas_call x2 -> x4, Pallas kernels: 9.51 us -> 8.35 us  [the longest x1 5.27 us: shards(): call(project_kernel, 'project', (shape((768, 256), BF16), shape((768, 256...]
  transfers between devices with their start and end apart: 10 -> 12, of which waited for: 8 -> 8; matrix products, arithmetic and copies ran while one was open for 0% -> 0% of each run, Pallas kernels for 7% -> 9%
where the time goes in v4:
time: 169 us; the launch traced here: 167 us
  starting transfers between devices  55.4 us (33%)
  waiting for transfers between devices  46.6 us (28%)
  blocking collectives  36.6 us (22%)
  Pallas kernels  19.7 us (12%)
  local copies, waits for them, and re-layouts  8.34 us (5%)
    all_gather x1, blocking collectives, shards(): lax.all_gather(weights, 'z', axis=1, tiled=True).reshape(3, 16, 32, 256)  36.6 us
    ppermute x8, starting transfers between devices, shift(): lax.ppermute(value, axis, [(i, (i + step) % size) for i in range(size)])  30.8 us
    ppermute x8, waiting for transfers between devices, shift(): lax.ppermute(value, axis, [(i, (i + step) % size) for i in range(size)])  20.9 us
    all_to_all x1, waiting for transfers between devices, shards(): own_mixed = lax.all_to_all(mixed, CHIPS, 0, 0, tiled=True)  11.7 us
    all_to_all x1, waiting for transfers between devices, shards(): pieces = lax.all_to_all(chip.reshape(32, 8, 128), CHIPS, 0, 0, tiled=True)  9.05 us
    all_to_all x1, starting transfers between devices, shards(): lax.all_to_all(jnp.broadcast_to(tokens[None], (8,) + tokens.shape), HEAD,...  7.61 us
    all_to_all x1, starting transfers between devices, shards(): own_marks = lax.all_to_all(spread, CHIPS, 0, 0, tiled=True)  6.81 us
    pallas_call x1, Pallas kernels, shards(): call(inverse_kernel, 'inverse', shape((256, 256), F32), [VMEM], 2 * 6 * 1...  6.12 us
  transfers between devices with their start and end apart: 12, of which 8 were waited for; matrix products, arithmetic and copies ran while one was open for 0% of the time, Pallas kernels for 9%

profile of v4, /device:TPU:1, one launch (start us, length us, event | category | flops | bytes accessed | tf_op | source)
XLA Modules:
  0.0 167.5 jit_solution(7501143360661067693)
XLA Ops:
  0.0 2.8 %broadcast_in_dim.2 = bf16[8,768,256]{2,1,0:T(8,128)(2,1)} broadcast(bf16[768,256]{1,0:T(8,128)(2,1)} %param.3), dimensions={1,2} | broadcast | bytes 3538944 | tf_op jit(solution)/shard_map/broadcast_in_dim | solution.py:243
  2.8 7.6 %all-to-all-start = ((bf16[8,768,256]{2,1,0:T(8,128)(2,1)}), bf16[8,768,256]{2,1,0:T(8,128)(2,1)S(1)}, u32[]{:S(2)}, u32[]{:S(2)}) async-start(bf16[8,768,256]{2,1,0:T(8,128)(2,1)} %broadcast_in_dim.2), calls=%async_computation | async-start | bytes 6291456 | tf_op jit(solution)/shard_map/all_to_all | solution.py:242
  10.4 36.6 %all_gather.3 = bf16[3,512,256]{2,1,0:T(8,128)(2,1)} all-gather(bf16[3,32,256]{2,1,0:T(8,128)(2,1)S(1)} %copy-done.7), channel_id=1, replica_groups=mesh['y'=4,'xh'=2,'z'=16,'xl'=2,'c'=2] {'z'}, dimensions={1}, use_global_device_ids=true | all-gather | bytes 835584 | tf_op jit(solution)/shard_map/all_gather | solution.py:245
  47.0 8.7 %collective-permute-start.1 = (bf16[3,16,32,256]{3,2,1,0:T(8,128)(2,1)}, bf16[3,16,32,256]{3,2,1,0:T(8,128)(2,1)}, u32[]{:S(2)}, u32[]{:S(2)}) collective-permute-start(bf16[3,16,32,256]{3,2,1,0:T(8,128)(2,1)} %bitcast.column), channel_id=1, source_target_pairs={{0,1},{1,0},{2,3},{3,2},{4,5},{5,4},{6,7},{7,6},{8,9},{9,8},{10,11... | collective-permute-start | bytes 2359304 | tf_op jit(solution)/shard_map/ppermute | solution.py:43
  55.7 2.2 %collective-permute-start.3 = (bf16[3,16,32,256]{3,2,1,0:T(8,128)(2,1)}, bf16[3,16,32,256]{3,2,1,0:T(8,128)(2,1)}, u32[]{:S(2)}, u32[]{:S(2)}) collective-permute-start(bf16[3,16,32,256]{3,2,1,0:T(8,128)(2,1)} %bitcast.column), channel_id=1, source_target_pairs={{0,2},{2,0},{1,3},{3,1},{4,6},{6,4},{5,7},{7,5},{8,10},{10,8},{9,1... | collective-permute-start | bytes 2359304 | tf_op jit(solution)/shard_map/ppermute | solution.py:43
  57.9 1.0 pick.1.own
  58.9 3.1 %collective-permute-start = (bf16[8,2048]{1,0:T(8,128)(2,1)S(1)}, bf16[8,2048]{1,0:T(8,128)(2,1)S(1)}, u32[]{:S(2)}, u32[]{:S(2)}) collective-permute-start(bf16[8,2048]{1,0:T(8,128)(2,1)S(1)} %pick.1.own), channel_id=1, source_target_pairs={{0,2},{2,0},{1,3},{3,1},{4,6},{6,4},{5,7},{7,5},{8,10},{10,8},{9,1... | collective-permute-start | bytes 98312 | tf_op jit(solution)/shard_map/ppermute | solution.py:43
  62.0 15.8 %collective-permute-done.other = bf16[8,2048]{1,0:T(8,128)(2,1)S(1)} collective-permute-done((bf16[8,2048]{1,0:T(8,128)(2,1)S(1)}, bf16[8,2048]{1,0:T(8,128)(2,1)S(1)}, u32[]{:S(2)}, u32[]{:S(2)}) %collective-permute-start) | collective-permute-done | bytes 32800 | tf_op jit(solution)/shard_map/ppermute | solution.py:43
  77.8 1.5 partial.1
  79.3 2.2 %collective-permute-start.2 = (f32[8,128]{1,0:T(8,128)S(1)}, f32[8,128]{1,0:T(8,128)S(1)}, u32[]{:S(2)}, u32[]{:S(2)}) collective-permute-start(f32[8,128]{1,0:T(8,128)S(1)} %get-tuple-element.25), channel_id=1, source_target_pairs={{0,2},{2,0},{1,3},{3,1},{4,6},{6,4},{5,7},{7,5},{8,10},{10,8},{9,1... | collective-permute-start | bytes 12296 | tf_op jit(solution)/shard_map/ppermute | solution.py:43
  81.5 2.1 %collective-permute-done.2.received = f32[8,128]{1,0:T(8,128)S(1)} collective-permute-done((f32[8,128]{1,0:T(8,128)S(1)}, f32[8,128]{1,0:T(8,128)S(1)}, u32[]{:S(2)}, u32[]{:S(2)}) %collective-permute-start.2) | collective-permute-done | bytes 4128 | tf_op jit(solution)/shard_map/ppermute | solution.py:43
  84.3 3.7 %collective-permute-start.4 = (bf16[3,16,32,256]{3,2,1,0:T(8,128)(2,1)}, bf16[3,16,32,256]{3,2,1,0:T(8,128)(2,1)}, u32[]{:S(2)}, u32[]{:S(2)}) collective-permute-start(bf16[3,16,32,256]{3,2,1,0:T(8,128)(2,1)} %collective-permute-done.3.across), channel_id=1, source_target_pairs={{0,1},{1,0},{2,3},{3,2},{4,5},{5,4},{6,7},{7,6},{8,9},{9,8},{10,11... | collective-permute-start | bytes 2359304 | tf_op jit(solution)/shard_map/ppermute | solution.py:43
  88.0 6.8 %all-to-all-start.1 = ((bf16[32,8,128]{2,1,0:T(8,128)(2,1)}), bf16[32,8,128]{2,1,0:T(8,128)(2,1)}, u32[]{:S(2)}, u32[]{:S(2)}) async-start(bf16[32,8,128]{2,1,0:T(8,128)(2,1)} %finish.1), calls=%async_computation.1 | async-start | bytes 131072 | tf_op jit(solution)/shard_map/all_to_all | solution.py:277
  94.8 5.3 %project.1 = (bf16[768,256]{1,0:T(8,128)(2,1)S(1)}, bf16[768,256]{1,0:T(8,128)(2,1)S(1)}, bf16[768,256]{1,0:T(8,128)(2,1)S(1)}, f32[2,768,1]{2,1,0:T(8,128)S(1)}) custom-call(bf16[8,768,256]{2,1,0:T(8,128)(2,1)S(1)} %all-to-all-done.tokens, bf16[3,16,32,256]{3,2,1,0:T(8,128)(2,1)} %bitcast.column, bf16[3,16,32,256]{3,2,1,0:T(8,128)(2,1)} %collective-permute-done.1.core, ...), custom_call_target="tpu_custom_call" | custom-call | flops 65536 | bytes 65536 | tf_op jit(solution)/shard_map/project/pallas_call | solution.py:283
  102.5 5.0 %all-to-all-done.1.own = bf16[32,8,128]{2,1,0:T(8,128)(2,1)} async-done(((bf16[32,8,128]{2,1,0:T(8,128)(2,1)}), bf16[32,8,128]{2,1,0:T(8,128)(2,1)}, u32[]{:S(2)}, u32[]{:S(2)}) %all-to-all-start.1) | async-done | bytes 65568 | tf_op jit(solution)/shard_map/all_to_all | solution.py:277
  107.5 3.9 %collective-permute-start.5 = (bf16[32,8,128]{2,1,0:T(8,128)(2,1)}, bf16[32,8,128]{2,1,0:T(8,128)(2,1)S(1)}, u32[]{:S(2)}, u32[]{:S(2)}) collective-permute-start(bf16[32,8,128]{2,1,0:T(8,128)(2,1)} %all-to-all-done.1.own), channel_id=1, source_target_pairs={{0,1},{1,0},{2,3},{3,2},{4,5},{5,4},{6,7},{7,6},{8,9},{9,8},{10,11... | collective-permute-start | bytes 196616 | tf_op jit(solution)/shard_map/ppermute | solution.py:43
  111.4 1.1 collective-permute-done.5.other
  112.5 1.1 copy-done.1
  113.6 1.0 copy-done.3
  114.6 1.0 copy-done.5
  115.6 2.1 %summary.1 = (bf16[2,256,128]{2,1,0:T(8,128)(2,1)S(1)}, f32[256,128]{1,0:T(8,128)S(1)}, f32[256,128]{1,0:T(8,128)S(1)}) custom-call(bf16[32,8,128]{2,1,0:T(8,128)(2,1)} %all-to-all-done.1.own, bf16[32,8,128]{2,1,0:T(8,128)(2,1)S(1)} %collective-permute-done.5.other, bf16[768,256]{1,0:T(8,128)(2,1)S(1)} %copy-done.3, bf16[768,256]{1,0:T(8,128)(2,1)S(1)} %copy-done.5, ...), custom_call_target="tpu_custom_call" | custom-call | flops 201326592 | bytes 2097152 | tf_op jit(solution)/shard_map/summary/pallas_call | solution.py:303
  117.7 2.3 %collective-permute-start.6 = (f32[256,128]{1,0:T(8,128)S(1)}, f32[256,128]{1,0:T(8,128)S(1)}, u32[]{:S(2)}, u32[]{:S(2)}) collective-permute-start(f32[256,128]{1,0:T(8,128)S(1)} %get-tuple-element.33), channel_id=1, source_target_pairs={{0,1},{1,0},{2,3},{3,2},{4,5},{5,4},{6,7},{7,6},{8,9},{9,8},{10,11... | collective-permute-start | bytes 393224 | tf_op jit(solution)/shard_map/ppermute | solution.py:43
  120.0 1.0 collective-permute-done.6
  121.6 6.0 %all-to-all-start.2 = ((f32[32,8,128]{2,1,0:T(8,128)}), f32[32,8,128]{2,1,0:T(8,128)S(1)}, u32[]{:S(2)}, u32[]{:S(2)}) async-start(f32[32,8,128]{2,1,0:T(8,128)} %bitcast.1), calls=%async_computation.2 | async-start | bytes 262144 | tf_op jit(solution)/shard_map/all_to_all | solution.py:325
  127.7 6.1 %inverse.1 = f32[256,256]{1,0:T(8,128)S(1)} custom-call(bf16[2,256,128]{2,1,0:T(8,128)(2,1)S(1)} %get-tuple-element.40.marks_ref.marks), custom_call_target="tpu_custom_call" | custom-call | flops 2415919104 | bytes 524288 | tf_op jit(solution)/shard_map/inverse/pallas_call | solution.py:315
  133.8 9.0 %all-to-all-done.2.pieces = f32[32,8,128]{2,1,0:T(8,128)S(1)} async-done(((f32[32,8,128]{2,1,0:T(8,128)}), f32[32,8,128]{2,1,0:T(8,128)S(1)}, u32[]{:S(2)}, u32[]{:S(2)}) %all-to-all-start.2) | async-done | bytes 131104 | tf_op jit(solution)/shard_map/all_to_all | solution.py:325
  142.8 1.0 mixed.1
  143.8 4.2 %all-to-all-start.3 = ((bf16[32,8,128]{2,1,0:T(8,128)(2,1)}), bf16[32,8,128]{2,1,0:T(8,128)(2,1)S(1)}, u32[]{:S(2)}, u32[]{:S(2)}) async-start(bf16[32,8,128]{2,1,0:T(8,128)(2,1)} %mixed.1), calls=%async_computation.3 | async-start | bytes 131072 | tf_op jit(solution)/shard_map/all_to_all | solution.py:335
  148.1 1.0 query_weights.1.weights
  149.0 11.7 %all-to-all-done.3.own = bf16[32,8,128]{2,1,0:T(8,128)(2,1)S(1)} async-done(((bf16[32,8,128]{2,1,0:T(8,128)(2,1)}), bf16[32,8,128]{2,1,0:T(8,128)(2,1)S(1)}, u32[]{:S(2)}, u32[]{:S(2)}) %all-to-all-start.3) | async-done | bytes 65568 | tf_op jit(solution)/shard_map/all_to_all | solution.py:335
  160.7 4.7 %collective-permute-start.7 = (bf16[32,8,128]{2,1,0:T(8,128)(2,1)S(1)}, bf16[32,8,128]{2,1,0:T(8,128)(2,1)S(1)}, u32[]{:S(2)}, u32[]{:S(2)}) collective-permute-start(bf16[32,8,128]{2,1,0:T(8,128)(2,1)S(1)} %all-to-all-done.3.own), channel_id=1, source_target_pairs={{0,1},{1,0},{2,3},{3,2},{4,5},{5,4},{6,7},{7,6},{8,9},{9,8},{10,11... | collective-permute-start | bytes 196616 | tf_op jit(solution)/shard_map/ppermute | solution.py:43
  166.3 1.1 attended.1
  (20 shorter events, 4.6 us)
Async XLA Ops:
  2.8 7.6 %copy-start.7 = (bf16[3,32,256]{2,1,0:T(8,128)(2,1)S(1)}, bf16[3,32,256]{2,1,0:T(8,128)(2,1)}, u32[]{:S(2)}) copy-start(bf16[3,32,256]{2,1,0:T(8,128)(2,1)} %param.4) | copy-start | bytes 147460
  2.8 55.1 %copy-start.6 = (s32[2,256]{1,0:T(2,128)S(1)}, s32[2,256]{1,0:T(2,128)}, u32[]{:S(2)}) copy-start(s32[2,256]{1,0:T(2,128)} %pos_ref.1) | copy-start | bytes 6148
  2.8 55.1 %all-to-all-start = ((bf16[8,768,256]{2,1,0:T(8,128)(2,1)}), bf16[8,768,256]{2,1,0:T(8,128)(2,1)S(1)}, u32[]{:S(2)}, u32[]{:S(2)}) async-start(bf16[8,768,256]{2,1,0:T(8,128)(2,1)} %broadcast_in_dim.2), calls=%async_computation | async-start | bytes 6291456 | tf_op jit(solution)/shard_map/all_to_all | solution.py:242
  47.0 14.9 %collective-permute-start.1 = (bf16[3,16,32,256]{3,2,1,0:T(8,128)(2,1)}, bf16[3,16,32,256]{3,2,1,0:T(8,128)(2,1)}, u32[]{:S(2)}, u32[]{:S(2)}) collective-permute-start(bf16[3,16,32,256]{3,2,1,0:T(8,128)(2,1)} %bitcast.column), channel_id=1, source_target_pairs={{0,1},{1,0},{2,3},{3,2},{4,5},{5,4},{6,7},{7,6},{8,9},{9,8},{10,11... | collective-permute-start | bytes 2359304 | tf_op jit(solution)/shard_map/ppermute | solution.py:43
  55.7 28.6 %collective-permute-start.3 = (bf16[3,16,32,256]{3,2,1,0:T(8,128)(2,1)}, bf16[3,16,32,256]{3,2,1,0:T(8,128)(2,1)}, u32[]{:S(2)}, u32[]{:S(2)}) collective-permute-start(bf16[3,16,32,256]{3,2,1,0:T(8,128)(2,1)} %bitcast.column), channel_id=1, source_target_pairs={{0,2},{2,0},{1,3},{3,1},{4,6},{6,4},{5,7},{7,5},{8,10},{10,8},{9,1... | collective-permute-start | bytes 2359304 | tf_op jit(solution)/shard_map/ppermute | solution.py:43
  58.9 18.9 %collective-permute-start = (bf16[8,2048]{1,0:T(8,128)(2,1)S(1)}, bf16[8,2048]{1,0:T(8,128)(2,1)S(1)}, u32[]{:S(2)}, u32[]{:S(2)}) collective-permute-start(bf16[8,2048]{1,0:T(8,128)(2,1)S(1)} %pick.1.own), channel_id=1, source_target_pairs={{0,2},{2,0},{1,3},{3,1},{4,6},{6,4},{5,7},{7,5},{8,10},{10,8},{9,1... | collective-permute-start | bytes 98312 | tf_op jit(solution)/shard_map/ppermute | solution.py:43
  79.3 4.4 %collective-permute-start.2 = (f32[8,128]{1,0:T(8,128)S(1)}, f32[8,128]{1,0:T(8,128)S(1)}, u32[]{:S(2)}, u32[]{:S(2)}) collective-permute-start(f32[8,128]{1,0:T(8,128)S(1)} %get-tuple-element.25), channel_id=1, source_target_pairs={{0,2},{2,0},{1,3},{3,1},{4,6},{6,4},{5,7},{7,5},{8,10},{10,8},{9,1... | collective-permute-start | bytes 12296 | tf_op jit(solution)/shard_map/ppermute | solution.py:43
  84.3 10.6 %collective-permute-start.4 = (bf16[3,16,32,256]{3,2,1,0:T(8,128)(2,1)}, bf16[3,16,32,256]{3,2,1,0:T(8,128)(2,1)}, u32[]{:S(2)}, u32[]{:S(2)}) collective-permute-start(bf16[3,16,32,256]{3,2,1,0:T(8,128)(2,1)} %collective-permute-done.3.across), channel_id=1, source_target_pairs={{0,1},{1,0},{2,3},{3,2},{4,5},{5,4},{6,7},{7,6},{8,9},{9,8},{10,11... | collective-permute-start | bytes 2359304 | tf_op jit(solution)/shard_map/ppermute | solution.py:43
  88.0 19.5 %all-to-all-start.1 = ((bf16[32,8,128]{2,1,0:T(8,128)(2,1)}), bf16[32,8,128]{2,1,0:T(8,128)(2,1)}, u32[]{:S(2)}, u32[]{:S(2)}) async-start(bf16[32,8,128]{2,1,0:T(8,128)(2,1)} %finish.1), calls=%async_computation.1 | async-start | bytes 131072 | tf_op jit(solution)/shard_map/all_to_all | solution.py:277
  100.1 0.9 copy-start
  101.0 0.7 copy-start.2
  101.7 0.8 copy-start.4
  107.5 5.0 %collective-permute-start.5 = (bf16[32,8,128]{2,1,0:T(8,128)(2,1)}, bf16[32,8,128]{2,1,0:T(8,128)(2,1)S(1)}, u32[]{:S(2)}, u32[]{:S(2)}) collective-permute-start(bf16[32,8,128]{2,1,0:T(8,128)(2,1)} %all-to-all-done.1.own), channel_id=1, source_target_pairs={{0,1},{1,0},{2,3},{3,2},{4,5},{5,4},{6,7},{7,6},{8,9},{9,8},{10,11... | collective-permute-start | bytes 196616 | tf_op jit(solution)/shard_map/ppermute | solution.py:43
  112.5 1.1 copy-start.1
  113.6 1.0 copy-start.3
  114.6 1.0 copy-start.5
  117.7 3.2 %collective-permute-start.6 = (f32[256,128]{1,0:T(8,128)S(1)}, f32[256,128]{1,0:T(8,128)S(1)}, u32[]{:S(2)}, u32[]{:S(2)}) collective-permute-start(f32[256,128]{1,0:T(8,128)S(1)} %get-tuple-element.33), channel_id=1, source_target_pairs={{0,1},{1,0},{2,3},{3,2},{4,5},{5,4},{6,7},{7,6},{8,9},{9,8},{10,11... | collective-permute-start | bytes 393224 | tf_op jit(solution)/shard_map/ppermute | solution.py:43
  121.6 21.2 %all-to-all-start.2 = ((f32[32,8,128]{2,1,0:T(8,128)}), f32[32,8,128]{2,1,0:T(8,128)S(1)}, u32[]{:S(2)}, u32[]{:S(2)}) async-start(f32[32,8,128]{2,1,0:T(8,128)} %bitcast.1), calls=%async_computation.2 | async-start | bytes 262144 | tf_op jit(solution)/shard_map/all_to_all | solution.py:325
  143.8 16.9 %all-to-all-start.3 = ((bf16[32,8,128]{2,1,0:T(8,128)(2,1)}), bf16[32,8,128]{2,1,0:T(8,128)(2,1)S(1)}, u32[]{:S(2)}, u32[]{:S(2)}) async-start(bf16[32,8,128]{2,1,0:T(8,128)(2,1)} %mixed.1), calls=%async_computation.3 | async-start | bytes 131072 | tf_op jit(solution)/shard_map/all_to_all | solution.py:335
  160.7 5.6 %collective-permute-start.7 = (bf16[32,8,128]{2,1,0:T(8,128)(2,1)S(1)}, bf16[32,8,128]{2,1,0:T(8,128)(2,1)S(1)}, u32[]{:S(2)}, u32[]{:S(2)}) collective-permute-start(bf16[32,8,128]{2,1,0:T(8,128)(2,1)S(1)} %all-to-all-done.3.own), channel_id=1, source_target_pairs={{0,1},{1,0},{2,3},{3,2},{4,5},{5,4},{6,7},{7,6},{8,9},{9,8},{10,11... | collective-permute-start | bytes 196616 | tf_op jit(solution)/shard_map/ppermute | solution.py:43

commit v5 on v4

v5 whole, which is shorter than its diff:
```python
import math

import jax
import jax.numpy as jnp
from jax import lax
from jax.experimental import pallas as pl
from jax.experimental.pallas import tpu as pltpu
from jax.sharding import Mesh
from jax.sharding import PartitionSpec as P

NSTEPS = 6
AXES = ("y", "xh", "z", "xl", "c")
SIZES = (4, 2, 16, 2, 2)
HEAD = ("y", "xh")
SEQ = ("z", "xl", "c")
CHIPS = ("z", "xl")
CORES = ("z", "c")

VMEM = pl.BlockSpec(memory_space=pltpu.VMEM)
SMEM = pl.BlockSpec(memory_space=pltpu.SMEM)
HBM = pl.BlockSpec(memory_space=pltpu.HBM)
ANY = pl.BlockSpec(memory_space=pl.ANY)
BF16 = jnp.bfloat16
F32 = jnp.float32
ROWS = (((1,), (1,)), ((), ()))
COLS = (((0,), (0,)), ((), ()))


def call(kernel, name, outs, ins, flops, nbytes, scratch=(), exps=0, space=VMEM):
    return pl.pallas_call(
        kernel,
        out_shape=outs,
        in_specs=ins,
        out_specs=jax.tree.map(lambda _: space, outs),
        scratch_shapes=list(scratch),
        cost_estimate=pl.CostEstimate(flops=flops, bytes_accessed=nbytes, transcendentals=exps),
        compiler_params=pltpu.CompilerParams(vmem_limit_bytes=16 << 20),
        name=name,
    )


def shift(value, axis, step):
    size = lax.axis_size(axis)
    return lax.ppermute(value, axis, [(i, (i + step) % size) for i in range(size)])


def high(left, right, dims=(((1,), (0,)), ((), ()))):
    return lax.dot_general(
        left, right, dims, precision=lax.Precision.HIGHEST, preferred_element_type=F32
    )


def side_norm(rows):
    rows32 = rows.astype(F32)
    ones = jnp.ones((8, rows.shape[1]), F32)
    return high(ones, rows32 * rows32, ROWS)[:1]


def down_norm(rows):
    rows32 = rows.astype(F32)
    return jnp.sum(rows32 * rows32, 1, keepdims=True)


def gauss(left, right, left_norm, right_norm):
    product = lax.dot_general(left, right, ROWS, preferred_element_type=F32)
    return jnp.exp((left_norm + right_norm - 2.0 * product) * (-0.5 / math.sqrt(left.shape[1])))


def run(copies):
    for copy in copies:
        copy.start()
    for copy in copies:
        copy.wait()


def pick_kernel(pos_ref, tokens, picked, groups, rows, sems):
    group = (lax.axis_index("z") * 2 + lax.axis_index("xl")) * 2 + lax.axis_index("c")
    blocks, count, width = tokens.shape
    places, copies = [], []
    for mark in range(8):
        row = pos_ref[mark // 4, group * 4 + mark % 4] - group * count
        start = pl.multiple_of((row // 8) * 8, 8)
        places.append(row - start)
        copies.append(
            pltpu.make_async_copy(
                tokens.at[:, pl.ds(start, 8), :], groups.at[mark], sems.at[mark]
            )
        )
    run(copies)
    index = lax.broadcasted_iota(jnp.int32, (8, width), 0)
    for mark, place in enumerate(places):
        for block in range(blocks):
            eight = groups[mark, block].astype(F32)
            rows[pl.ds(mark, 1), pl.ds(block * width, width)] = jnp.sum(
                jnp.where(index == place, eight, 0.0), 0, keepdims=True
            )
    picked[...] = rows[...].astype(BF16)


def partial_kernel(own, other, column, core, keep, give, w, sems):
    xl, c = lax.axis_index("xl"), lax.axis_index("c")
    run(
        [
            pltpu.make_async_copy(column.at[pl.ds(0, 2)], w.at[:, :, c], sems.at[0]),
            pltpu.make_async_copy(core.at[pl.ds(0, 2)], w.at[:, :, 1 - c], sems.at[1]),
        ]
    )
    rows = jnp.concatenate([own[...].astype(F32), other[...].astype(F32)], 0)
    low = lax.broadcasted_iota(jnp.int32, (16, 128), 1) < 64
    tiles = []
    for pair in range(8):
        even = rows[:, pair * 256 : pair * 256 + 128]
        odd = rows[:, pair * 256 + 128 : pair * 256 + 256]
        first = jnp.where(low, even, pltpu.roll(odd, 64, 1))
        second = jnp.where(low, pltpu.roll(even, 64, 1), odd)
        tiles.append(jnp.where(xl == 0, first, second))
    left = jnp.concatenate(tiles, 1).astype(BF16)
    results = [
        jnp.dot(left, w[kind].reshape(1024, 256), preferred_element_type=F32) for kind in range(2)
    ]
    number = lax.broadcasted_iota(jnp.int32, (16, 256), 0)
    both = jnp.where(number % 2 == 0, results[0], results[1])
    chosen = jnp.where((number[:, :128] % 8) < 4, both[:, :128], both[:, 128:])
    keep[...] = chosen[:8]
    give[...] = chosen[8:]


def finish_kernel(keep, received, spread):
    chosen = (keep[...] + received[...]).astype(BF16)
    for place in range(spread.shape[0]):
        spread[place] = chosen


def pack_kernel(column, core, packed, sems):
    c = lax.axis_index("c")
    cols = pl.ds(pl.multiple_of(c * 128, 128), 128)
    run(
        [
            pltpu.make_async_copy(column.at[:, :, :, cols], packed.at[c], sems.at[0]),
            pltpu.make_async_copy(core.at[:, :, :, cols], packed.at[1 - c], sems.at[1]),
        ]
    )


def project_kernel(tokens, core_tokens, packed, across, query, keys, values, norms, x, w, sems):
    depth = x.shape[1]
    xl = lax.axis_index("xl")
    copies = []

    def add(source, target):
        copies.append(pltpu.make_async_copy(source, target, sems.at[len(copies)]))

    for part in range(2):
        add(packed.at[part], w.at[:, :, xl, part])
        add(across.at[part], w.at[:, :, 1 - xl, part])
    blocks, rows, width = tokens.shape
    for number, source in enumerate((tokens, core_tokens)):
        for block in range(blocks):
            add(
                source.at[block],
                x.at[pl.ds(number * rows, rows), pl.ds(block * width, width)],
            )
    run(copies)
    weights = [w[kind].reshape(depth, 128) for kind in range(3)]
    pair = jnp.concatenate(weights[:2], 1)

    @pl.loop(0, 6)
    def _(step):
        here = pl.ds(pl.multiple_of(step * 256, 256), 256)
        left = x[here, :]
        both = jnp.dot(left, pair, preferred_element_type=F32).astype(BF16)
        query[here, :] = both[:, :128]
        keys[here, :] = both[:, 128:]
        values[here, :] = jnp.dot(left, weights[2], preferred_element_type=F32).astype(BF16)
        norms[here, :] = down_norm(both[:, 128:])


def summary_kernel(own, other, keys, values, norms, marks, pieces, flat, part):
    xl, c = lax.axis_index("xl"), lax.axis_index("c")
    flat[xl] = own[...].reshape(256, 128).astype(F32)
    flat[1 - xl] = other[...].reshape(256, 128).astype(F32)
    rows = []
    for side in range(2):
        for mark in range(4):
            first = flat[side, pl.ds(mark, 32, stride=8), :]
            second = flat[side, pl.ds(4 + mark, 32, stride=8), :]
            rows.append(jnp.where(c == 0, first, second))
    rows = jnp.concatenate(rows, 0).astype(BF16)
    marks[...] = rows
    weights = gauss(keys[...], rows, norms[...], side_norm(rows)).astype(BF16)
    part[...] = lax.dot_general(values[...], weights, COLS, preferred_element_type=F32)
    for half in range(2):
        for four in range(4):
            pieces[pl.ds(half * 4 + four, 32, stride=8), :] = part[
                pl.ds(four * 32, 32), pl.ds(half * 128, 128)
            ]


def inverse_kernel(marks_ref, inverse_ref):
    marks = marks_ref[...]
    inner = gauss(marks, marks, down_norm(marks), side_norm(marks))
    scale_cols = jnp.max(jnp.sum(jnp.abs(inner), 0, keepdims=True), 1, keepdims=True)
    scale_rows = jnp.max(jnp.sum(jnp.abs(inner), 1, keepdims=True), 0, keepdims=True)
    iterate = inner / (scale_cols * scale_rows)
    for step in range(NSTEPS):
        iterate = 2.0 * iterate - high(high(iterate, inner), iterate)
    inverse_ref[...] = iterate


def mixed_kernel(pieces, inverse, spread):
    summed = jnp.sum(pieces[...], 0)
    left = high(summed, inverse[:, :128], ROWS)
    right = high(summed, inverse[:, 128:], ROWS)
    mixed = left[:4] + right[4:]
    chosen = jnp.concatenate([mixed[:, :128], mixed[:, 128:]], 0).astype(BF16)
    for place in range(spread.shape[0]):
        spread[place] = chosen


def query_weight_kernel(query, marks, weights):
    rows = marks[...]
    weights[...] = gauss(query[...], rows, down_norm(query[...]), side_norm(rows)).astype(BF16)


def give_kernel(spread, weights, mixed, give, flat):
    flat[...] = spread[...].reshape(256, 128).astype(F32)
    halves = [
        jnp.concatenate([flat[pl.ds(half * 4 + four, 32, stride=8), :] for four in range(4)], 0)
        for half in range(2)
    ]
    matrix = jnp.concatenate(halves, 1).astype(BF16)
    mixed[...] = matrix
    give[...] = lax.dot_general(
        weights[768:, :], matrix, ROWS, preferred_element_type=F32
    ).astype(BF16)


def keep_kernel(mixed, weights, keep):
    keep[...] = lax.dot_general(
        weights[:768, :], mixed[...], ROWS, preferred_element_type=F32
    ).astype(BF16)


def join_kernel(keep, received, out):
    c = lax.axis_index("c")
    out[:, pl.ds(pl.multiple_of(c * 128, 128), 128)] = keep[...]
    out[:, pl.ds(pl.multiple_of((1 - c) * 128, 128), 128)] = received[...]


def shape(dims, dtype):
    return jax.ShapeDtypeStruct(dims, dtype)


def shards(tokens, weights, landmark_pos):
    whole = lax.all_to_all(
        jnp.broadcast_to(tokens[None], (8,) + tokens.shape), HEAD, 0, 0, tiled=True
    )
    column = lax.all_gather(weights, "z", axis=1, tiled=True).reshape(3, 16, 32, 256)
    core = shift(column, "c", 1)
    core, later = lax.optimization_barrier((core, whole))
    core_tokens = shift(later, "c", 1)
    packed = call(
        pack_kernel,
        "pack",
        shape((2, 3, 16, 32, 128), BF16),
        [ANY, ANY],
        1 << 10,
        3 << 19,
        [pltpu.SemaphoreType.DMA((2,))],
        space=HBM,
    )(column, core)
    picked = call(
        pick_kernel,
        "pick",
        shape((8, 2048), BF16),
        [SMEM, ANY],
        1 << 20,
        1 << 19,
        [
            pltpu.VMEM((8, 8, 8, 256), BF16),
            pltpu.VMEM((8, 2048), F32),
            pltpu.SemaphoreType.DMA((8,)),
        ],
    )(landmark_pos, whole)
    other_picked = shift(picked, "xl", 1)
    keep, give = call(
        partial_kernel,
        "partial",
        (shape((8, 128), F32), shape((8, 128), F32)),
        [VMEM, VMEM, ANY, ANY],
        2 * 16 * 1024 * 512,
        1 << 20,
        [pltpu.VMEM((2, 16, 2, 32, 256), BF16), pltpu.SemaphoreType.DMA((2,))],
    )(picked, other_picked, column, core)
    received = shift(give, "xl", 1)
    spread = call(
        finish_kernel, "finish", shape((32, 8, 128), BF16), [VMEM] * 2, 1 << 14, 1 << 16
    )(keep, received)
    spread, packed = lax.optimization_barrier((spread, packed))
    own_marks = lax.all_to_all(spread, CORES, 0, 0, tiled=True)
    across = shift(packed, "xl", 1)
    query, keys, values, norms = call(
        project_kernel,
        "project",
        (
            shape((1536, 128), BF16),
            shape((1536, 128), BF16),
            shape((1536, 128), BF16),
            shape((1536, 1), F32),
        ),
        [ANY] * 4,
        2 * 1536 * 2048 * 384,
        8 << 20,
        [
            pltpu.VMEM((1536, 2048), BF16),
            pltpu.VMEM((3, 16, 2, 2, 32, 128), BF16),
            pltpu.SemaphoreType.DMA((20,)),
        ],
    )(whole, core_tokens, packed, across)

    other_marks = shift(own_marks, "xl", 1)
    marks, chip = call(
        summary_kernel,
        "summary",
        (shape((256, 128), BF16), shape((256, 128), F32)),
        [VMEM] * 5,
        2 * 2 * 1536 * 256 * 128,
        2 << 20,
        [pltpu.VMEM((2, 256, 128), F32), pltpu.VMEM((128, 256), F32)],
        1536 * 256,
    )(own_marks, other_marks, keys, values, norms)
    chip, marks, query = lax.optimization_barrier((chip, marks, query))
    inverse = call(
        inverse_kernel,
        "inverse",
        shape((256, 256), F32),
        [VMEM],
        2 * 6 * 12 * 256**3,
        1 << 19,
        (),
        256 * 256,
    )(marks)
    query_weights = call(
        query_weight_kernel,
        "query_weights",
        shape((1536, 256), BF16),
        [VMEM] * 2,
        2 * 1536 * 256 * 128,
        2 << 20,
        (),
        1536 * 256,
    )(query, marks)
    pieces = lax.all_to_all(chip.reshape(32, 8, 128), CHIPS, 0, 0, tiled=True)
    pieces, query_weights = lax.optimization_barrier((pieces, query_weights))
    spread = call(
        mixed_kernel,
        "mixed",
        shape((32, 8, 128), BF16),
        [VMEM] * 2,
        2 * 6 * 16 * 256 * 128,
        1 << 19,
    )(pieces, inverse)
    spread = lax.all_to_all(spread, CHIPS, 0, 0, tiled=True)
    mixed, give = call(
        give_kernel,
        "give",
        (shape((128, 256), BF16), shape((768, 128), BF16)),
        [VMEM] * 2,
        2 * 768 * 256 * 128,
        1 << 19,
        [pltpu.VMEM((256, 128), F32)],
    )(spread, query_weights)
    received = shift(give, "c", 1)
    keep = call(
        keep_kernel,
        "keep",
        shape((768, 128), BF16),
        [VMEM] * 2,
        2 * 768 * 256 * 128,
        1 << 19,
    )(mixed, query_weights)
    return call(
        join_kernel, "join", shape((768, 256), BF16), [VMEM] * 2, 1 << 10, 1 << 19
    )(keep, received)


def solution(mesh):
    fine = Mesh(mesh.devices.reshape(SIZES), AXES)
    return jax.shard_map(
        shards,
        mesh=fine,
        in_specs=(P(SEQ, HEAD), P(None, SEQ, HEAD), P(HEAD, None)),
        out_specs=P(SEQ, HEAD),
        check_vma=False,
    )
```

time: 169 us -> 152 us (0.90)
  blocking collectives: 36.6 us -> 78.2 us
  waiting for transfers between devices: 46.6 us -> 12.7 us
  starting transfers between devices: 55.4 us -> 37.5 us
  local copies, waits for them, and re-layouts: 8.34 us -> 4.65 us
  Pallas kernels: 19.7 us -> 17.8 us
    all_to_all x0 -> x2, blocking collectives: none -> 43.6 us  [the longest x1 25.3 us: shards(): own_marks = lax.all_to_all(spread, CORES, 0, 0, tiled=True)]
    all_to_all x2 -> x0, waiting for transfers between devices: 16.7 us -> none  [the longest x1 11.7 us: shards(): own_mixed = lax.all_to_all(mixed, CHIPS, 0, 0, tiled=True)]
    ppermute x8 -> x7, waiting for transfers between devices: 20.9 us -> 6.15 us  [shift(): lax.ppermute(value, axis, [(i, (i + step) % size) for i in range(size)])]
    all_to_all x2 -> x0, starting transfers between devices: 11 us -> none  [the longest x1 6.81 us: shards(): own_marks = lax.all_to_all(spread, CHIPS, 0, 0, tiled=True)]
    ppermute x8 -> x7, starting transfers between devices: 30.8 us -> 26 us  [shift(): lax.ppermute(value, axis, [(i, (i + step) % size) for i in range(size)])]
    unnamed x16 -> x12, local copies, waits for them, and re-layouts: 5.52 us -> 1.8 us
    all_to_all x1, waiting for transfers between devices: 9.05 us -> 6.57 us  [shards(): pieces = lax.all_to_all(chip.reshape(32, 8, 128), CHIPS, 0, 0, tiled=True)]
    all_to_all x1, starting transfers between devices: 6.05 us -> 3.86 us  [shards(): pieces = lax.all_to_all(chip.reshape(32, 8, 128), CHIPS, 0, 0, tiled=True)]
  transfers between devices with their start and end apart: 12 -> 9, of which waited for: 8 -> 5; matrix products, arithmetic and copies ran while one was open for 0% -> 0% of each run, Pallas kernels for 9% -> 10%
where the time goes in v5:
time: 152 us; the launch traced here: 151 us
  blocking collectives  78.2 us (51%)
  starting transfers between devices  37.5 us (25%)
  Pallas kernels  17.8 us (12%)
  waiting for transfers between devices  12.7 us (8%)
  local copies, waits for them, and re-layouts  4.65 us (3%)
    all_gather x1, blocking collectives, shards(): lax.all_gather(weights, 'z', axis=1, tiled=True).reshape(3, 16, 32, 256)  34.6 us
    ppermute x7, starting transfers between devices, shift(): lax.ppermute(value, axis, [(i, (i + step) % size) for i in range(size)])  26 us
    all_to_all x1, blocking collectives, shards(): own_marks = lax.all_to_all(spread, CORES, 0, 0, tiled=True)  25.3 us
    all_to_all x1, blocking collectives, shards(): spread = lax.all_to_all(spread, CHIPS, 0, 0, tiled=True)  18.3 us
    all_to_all x1, starting transfers between devices, shards(): lax.all_to_all(jnp.broadcast_to(tokens[None], (8,) + tokens.shape), HEAD,...  7.61 us
    all_to_all x1, waiting for transfers between devices, shards(): pieces = lax.all_to_all(chip.reshape(32, 8, 128), CHIPS, 0, 0, tiled=True)  6.57 us
    ppermute x7, waiting for transfers between devices, shift(): lax.ppermute(value, axis, [(i, (i + step) % size) for i in range(size)])  6.15 us
    pallas_call x1, Pallas kernels, shards(): call(inverse_kernel, 'inverse', shape((256, 256), F32), [VMEM], 2 * 6 * 1...  6.12 us
  transfers between devices with their start and end apart: 9, of which 5 were waited for; matrix products, arithmetic and copies ran while one was open for 0% of the time, Pallas kernels for 10%

profile of v5, /device:TPU:1, one launch (start us, length us, event | category | flops | bytes accessed | tf_op | source)
XLA Modules:
  0.0 151.1 jit_solution(15971844214454908183)
XLA Ops:
  0.0 2.9 %broadcast_in_dim.2 = bf16[8,768,256]{2,1,0:T(8,128)(2,1)} broadcast(bf16[768,256]{1,0:T(8,128)(2,1)} %param.3), dimensions={1,2} | broadcast | bytes 3538944 | tf_op jit(solution)/shard_map/broadcast_in_dim | solution.py:256
  2.9 7.6 %all-to-all-start = ((bf16[8,768,256]{2,1,0:T(8,128)(2,1)}), bf16[8,768,256]{2,1,0:T(8,128)(2,1)S(1)}, u32[]{:S(2)}, u32[]{:S(2)}) async-start(bf16[8,768,256]{2,1,0:T(8,128)(2,1)} %broadcast_in_dim.2), calls=%async_computation | async-start | bytes 6291456 | tf_op jit(solution)/shard_map/all_to_all | solution.py:255
  10.5 34.6 %all_gather.3 = bf16[3,512,256]{2,1,0:T(8,128)(2,1)S(1)} all-gather(bf16[3,32,256]{2,1,0:T(8,128)(2,1)S(1)} %copy-done.5), channel_id=1, replica_groups=mesh['y'=4,'xh'=2,'z'=16,'xl'=2,'c'=2] {'z'}, dimensions={1}, use_global_device_ids=true | all-gather | bytes 835584 | tf_op jit(solution)/shard_map/all_gather | solution.py:258
  45.1 8.3 %collective-permute-start.1 = (bf16[3,16,32,256]{3,2,1,0:T(8,128)(2,1)S(1)}, bf16[3,16,32,256]{3,2,1,0:T(8,128)(2,1)S(1)}, u32[]{:S(2)}, u32[]{:S(2)}) collective-permute-start(bf16[3,16,32,256]{3,2,1,0:T(8,128)(2,1)S(1)} %bitcast.2), channel_id=1, source_target_pairs={{0,1},{1,0},{2,3},{3,2},{4,5},{5,4},{6,7},{7,6},{8,9},{9,8},{10,11... | collective-permute-start | bytes 2359304 | tf_op jit(solution)/shard_map/ppermute | solution.py:44
  53.4 0.9 copy-done
  54.3 1.0 collective-permute-done.1.core
  55.3 0.9 copy-done.2
  56.2 0.0 all-to-all-done.tokens
  56.2 2.4 %collective-permute-start.4 = (bf16[8,768,256]{2,1,0:T(8,128)(2,1)S(1)}, bf16[8,768,256]{2,1,0:T(8,128)(2,1)S(1)}, u32[]{:S(2)}, u32[]{:S(2)}) collective-permute-start(bf16[8,768,256]{2,1,0:T(8,128)(2,1)S(1)} %all-to-all-done.tokens), channel_id=1, source_target_pairs={{0,1},{1,0},{2,3},{3,2},{4,5},{5,4},{6,7},{7,6},{8,9},{9,8},{10,11... | collective-permute-start | bytes 9437192 | tf_op jit(solution)/shard_map/ppermute | solution.py:44
  58.6 1.0 pick.1.own
  59.6 2.2 %collective-permute-start = (bf16[8,2048]{1,0:T(8,128)(2,1)S(1)}, bf16[8,2048]{1,0:T(8,128)(2,1)S(1)}, u32[]{:S(2)}, u32[]{:S(2)}) collective-permute-start(bf16[8,2048]{1,0:T(8,128)(2,1)S(1)} %pick.1.own), channel_id=1, source_target_pairs={{0,2},{2,0},{1,3},{3,1},{4,6},{6,4},{5,7},{7,5},{8,10},{10,8},{9,1... | collective-permute-start | bytes 98312 | tf_op jit(solution)/shard_map/ppermute | solution.py:44
  61.8 2.4 %collective-permute-done.other = bf16[8,2048]{1,0:T(8,128)(2,1)S(1)} collective-permute-done((bf16[8,2048]{1,0:T(8,128)(2,1)S(1)}, bf16[8,2048]{1,0:T(8,128)(2,1)S(1)}, u32[]{:S(2)}, u32[]{:S(2)}) %collective-permute-start) | collective-permute-done | bytes 32800 | tf_op jit(solution)/shard_map/ppermute | solution.py:44
  64.2 0.4 partial.1
  64.7 2.2 %collective-permute-start.2 = (f32[8,128]{1,0:T(8,128)S(1)}, f32[8,128]{1,0:T(8,128)S(1)}, u32[]{:S(2)}, u32[]{:S(2)}) collective-permute-start(f32[8,128]{1,0:T(8,128)S(1)} %get-tuple-element.26), channel_id=1, source_target_pairs={{0,2},{2,0},{1,3},{3,1},{4,6},{6,4},{5,7},{7,5},{8,10},{10,8},{9,1... | collective-permute-start | bytes 12296 | tf_op jit(solution)/shard_map/ppermute | solution.py:44
  66.9 0.2 pack.1.packed
  67.1 1.9 %collective-permute-done.2.received = f32[8,128]{1,0:T(8,128)S(1)} collective-permute-done((f32[8,128]{1,0:T(8,128)S(1)}, f32[8,128]{1,0:T(8,128)S(1)}, u32[]{:S(2)}, u32[]{:S(2)}) %collective-permute-start.2) | collective-permute-done | bytes 4128 | tf_op jit(solution)/shard_map/ppermute | solution.py:44
  69.0 2.2 %collective-permute-start.5 = (bf16[2,3,16,32,128]{4,3,2,1,0:T(8,128)(2,1)S(1)}, bf16[2,3,16,32,128]{4,3,2,1,0:T(8,128)(2,1)S(1)}, u32[]{:S(2)}, u32[]{:S(2)}) collective-permute-start(bf16[2,3,16,32,128]{4,3,2,1,0:T(8,128)(2,1)S(1)} %pack.1.packed), channel_id=1, source_target_pairs={{0,2},{2,0},{1,3},{3,1},{4,6},{6,4},{5,7},{7,5},{8,10},{10,8},{9,1... | collective-permute-start | bytes 2359304 | tf_op jit(solution)/shard_map/ppermute | solution.py:44
  71.2 25.3 %all_to_all.20.own = bf16[32,8,128]{2,1,0:T(8,128)(2,1)S(1)} all-to-all(bf16[32,8,128]{2,1,0:T(8,128)(2,1)S(1)} %finish.1), channel_id=1, replica_groups=mesh['y'=4,'xh'=2,'z'=16,'xl'=2,'c'=2] {'z','c'}, dimensions={0} | all-to-all | bytes 131072 | tf_op jit(solution)/shard_map/all_to_all | solution.py:300
  96.5 3.0 %collective-permute-start.3 = (bf16[32,8,128]{2,1,0:T(8,128)(2,1)S(1)}, bf16[32,8,128]{2,1,0:T(8,128)(2,1)S(1)}, u32[]{:S(2)}, u32[]{:S(2)}) collective-permute-start(bf16[32,8,128]{2,1,0:T(8,128)(2,1)S(1)} %all_to_all.20.own), channel_id=1, source_target_pairs={{0,2},{2,0},{1,3},{3,1},{4,6},{6,4},{5,7},{7,5},{8,10},{10,8},{9,1... | collective-permute-start | bytes 196616 | tf_op jit(solution)/shard_map/ppermute | solution.py:44
  99.6 6.1 %project.1 = (bf16[1536,128]{1,0:T(8,128)(2,1)S(1)}, bf16[1536,128]{1,0:T(8,128)(2,1)S(1)}, bf16[1536,128]{1,0:T(8,128)(2,1)S(1)}, f32[1536,1]{1,0:T(8,128)S(1)}) custom-call(bf16[8,768,256]{2,1,0:T(8,128)(2,1)S(1)} %all-to-all-done.tokens, bf16[8,768,256]{2,1,0:T(8,128)(2,1)S(1)} %collective-permute-done.4.core_tokens, ...), custom_call_target="tpu_custom_call" | custom-call | flops 2415919104 | bytes 8388608 | tf_op jit(solution)/shard_map/project/pallas_call | solution.py:302
  105.7 1.7 %summary.1 = (bf16[256,128]{1,0:T(8,128)(2,1)S(1)}, f32[256,128]{1,0:T(8,128)}) custom-call(bf16[32,8,128]{2,1,0:T(8,128)(2,1)S(1)} %all_to_all.20.own, bf16[32,8,128]{2,1,0:T(8,128)(2,1)S(1)} %collective-permute-done.3.other, bf16[1536,128]{1,0:T(8,128)(2,1)S(1)} %get-tuple-element.30.keys, bf16[1536,128]{1,0:T(8,128)(2,1)S(1)} %get-tuple-element.31.values, ...), custom_call_target="tpu_custom_call" | custom-call | flops 201326592 | bytes 2097152 | tf_op jit(solution)/shard_map/summary/pallas_call | solution.py:322
  107.3 3.9 %all-to-all-start.2 = ((f32[32,8,128]{2,1,0:T(8,128)}), f32[32,8,128]{2,1,0:T(8,128)S(1)}, u32[]{:S(2)}, u32[]{:S(2)}) async-start(f32[32,8,128]{2,1,0:T(8,128)} %bitcast.1), calls=%async_computation.2 | async-start | bytes 262144 | tf_op jit(solution)/shard_map/all_to_all | solution.py:353
  111.2 0.8 query_weights.1.weights
  112.0 6.1 %inverse.1 = f32[256,256]{1,0:T(8,128)S(1)} custom-call(bf16[256,128]{1,0:T(8,128)(2,1)S(1)} %get-tuple-element.38.marks.marks_ref), custom_call_target="tpu_custom_call" | custom-call | flops 2415919104 | bytes 524288 | tf_op jit(solution)/shard_map/inverse/pallas_call | solution.py:333
  118.1 6.6 %all-to-all-done.2.pieces = f32[32,8,128]{2,1,0:T(8,128)S(1)} async-done(((f32[32,8,128]{2,1,0:T(8,128)}), f32[32,8,128]{2,1,0:T(8,128)S(1)}, u32[]{:S(2)}, u32[]{:S(2)}) %all-to-all-start.2) | async-done | bytes 131104 | tf_op jit(solution)/shard_map/all_to_all | solution.py:353
  124.7 0.3 mixed.1
  125.0 18.3 %all_to_all.21.spread = bf16[32,8,128]{2,1,0:T(8,128)(2,1)S(1)} all-to-all(bf16[32,8,128]{2,1,0:T(8,128)(2,1)S(1)} %mixed.1), channel_id=1, replica_groups=mesh['y'=4,'xh'=2,'z'=16,'xl'=2,'c'=2] {'z','xl'}, dimensions={0} | all-to-all | bytes 131072 | tf_op jit(solution)/shard_map/all_to_all | solution.py:363
  143.3 0.3 give.1
  143.6 5.6 %collective-permute-start.6 = (bf16[768,128]{1,0:T(8,128)(2,1)S(1)}, bf16[768,128]{1,0:T(8,128)(2,1)S(1)}, u32[]{:S(2)}, u32[]{:S(2)}) collective-permute-start(bf16[768,128]{1,0:T(8,128)(2,1)S(1)} %get-tuple-element.42), channel_id=1, source_target_pairs={{0,1},{1,0},{2,3},{3,2},{4,5},{5,4},{6,7},{7,6},{8,9},{9,8},{10,11... | collective-permute-start | bytes 589832 | tf_op jit(solution)/shard_map/ppermute | solution.py:44
  149.2 0.3 keep.1
  149.4 0.8 collective-permute-done.6.received
  150.2 0.9 join.1
  (14 shorter events, 0.0 us)
Async XLA Ops:
  2.9 7.6 %copy-start.5 = (bf16[3,32,256]{2,1,0:T(8,128)(2,1)S(1)}, bf16[3,32,256]{2,1,0:T(8,128)(2,1)}, u32[]{:S(2)}) copy-start(bf16[3,32,256]{2,1,0:T(8,128)(2,1)} %param.4) | copy-start | bytes 147460
  2.9 55.8 %copy-start.4 = (s32[2,256]{1,0:T(2,128)S(1)}, s32[2,256]{1,0:T(2,128)}, u32[]{:S(2)}) copy-start(s32[2,256]{1,0:T(2,128)} %pos_ref.1) | copy-start | bytes 6148
  2.9 53.3 %all-to-all-start = ((bf16[8,768,256]{2,1,0:T(8,128)(2,1)}), bf16[8,768,256]{2,1,0:T(8,128)(2,1)S(1)}, u32[]{:S(2)}, u32[]{:S(2)}) async-start(bf16[8,768,256]{2,1,0:T(8,128)(2,1)} %broadcast_in_dim.2), calls=%async_computation | async-start | bytes 6291456 | tf_op jit(solution)/shard_map/all_to_all | solution.py:255
  45.1 10.2 %collective-permute-start.1 = (bf16[3,16,32,256]{3,2,1,0:T(8,128)(2,1)S(1)}, bf16[3,16,32,256]{3,2,1,0:T(8,128)(2,1)S(1)}, u32[]{:S(2)}, u32[]{:S(2)}) collective-permute-start(bf16[3,16,32,256]{3,2,1,0:T(8,128)(2,1)S(1)} %bitcast.2), channel_id=1, source_target_pairs={{0,1},{1,0},{2,3},{3,2},{4,5},{5,4},{6,7},{7,6},{8,9},{9,8},{10,11... | collective-permute-start | bytes 2359304 | tf_op jit(solution)/shard_map/ppermute | solution.py:44
  53.4 0.9 copy-start
  55.3 0.9 copy-start.2
  56.2 8.0 %copy-start.1 = (bf16[3,512,256]{2,1,0:T(8,128)(2,1)S(1)}, bf16[3,512,256]{2,1,0:T(8,128)(2,1)}, u32[]{:S(2)}) copy-start(bf16[3,512,256]{2,1,0:T(8,128)(2,1)} %copy-done) | copy-start | bytes 2359300
  56.2 8.0 %copy-start.3 = (bf16[3,16,32,256]{3,2,1,0:T(8,128)(2,1)S(1)}, bf16[3,16,32,256]{3,2,1,0:T(8,128)(2,1)}, u32[]{:S(2)}) copy-start(bf16[3,16,32,256]{3,2,1,0:T(8,128)(2,1)} %copy-done.2) | copy-start | bytes 2359300
  56.2 43.4 %collective-permute-start.4 = (bf16[8,768,256]{2,1,0:T(8,128)(2,1)S(1)}, bf16[8,768,256]{2,1,0:T(8,128)(2,1)S(1)}, u32[]{:S(2)}, u32[]{:S(2)}) collective-permute-start(bf16[8,768,256]{2,1,0:T(8,128)(2,1)S(1)} %all-to-all-done.tokens), channel_id=1, source_target_pairs={{0,1},{1,0},{2,3},{3,2},{4,5},{5,4},{6,7},{7,6},{8,9},{9,8},{10,11... | collective-permute-start | bytes 9437192 | tf_op jit(solution)/shard_map/ppermute | solution.py:44
  59.6 4.7 %collective-permute-start = (bf16[8,2048]{1,0:T(8,128)(2,1)S(1)}, bf16[8,2048]{1,0:T(8,128)(2,1)S(1)}, u32[]{:S(2)}, u32[]{:S(2)}) collective-permute-start(bf16[8,2048]{1,0:T(8,128)(2,1)S(1)} %pick.1.own), channel_id=1, source_target_pairs={{0,2},{2,0},{1,3},{3,1},{4,6},{6,4},{5,7},{7,5},{8,10},{10,8},{9,1... | collective-permute-start | bytes 98312 | tf_op jit(solution)/shard_map/ppermute | solution.py:44
  64.7 4.4 %collective-permute-start.2 = (f32[8,128]{1,0:T(8,128)S(1)}, f32[8,128]{1,0:T(8,128)S(1)}, u32[]{:S(2)}, u32[]{:S(2)}) collective-permute-start(f32[8,128]{1,0:T(8,128)S(1)} %get-tuple-element.26), channel_id=1, source_target_pairs={{0,2},{2,0},{1,3},{3,1},{4,6},{6,4},{5,7},{7,5},{8,10},{10,8},{9,1... | collective-permute-start | bytes 12296 | tf_op jit(solution)/shard_map/ppermute | solution.py:44
  69.0 30.6 %collective-permute-start.5 = (bf16[2,3,16,32,128]{4,3,2,1,0:T(8,128)(2,1)S(1)}, bf16[2,3,16,32,128]{4,3,2,1,0:T(8,128)(2,1)S(1)}, u32[]{:S(2)}, u32[]{:S(2)}) collective-permute-start(bf16[2,3,16,32,128]{4,3,2,1,0:T(8,128)(2,1)S(1)} %pack.1.packed), channel_id=1, source_target_pairs={{0,2},{2,0},{1,3},{3,1},{4,6},{6,4},{5,7},{7,5},{8,10},{10,8},{9,1... | collective-permute-start | bytes 2359304 | tf_op jit(solution)/shard_map/ppermute | solution.py:44
  96.5 9.1 %collective-permute-start.3 = (bf16[32,8,128]{2,1,0:T(8,128)(2,1)S(1)}, bf16[32,8,128]{2,1,0:T(8,128)(2,1)S(1)}, u32[]{:S(2)}, u32[]{:S(2)}) collective-permute-start(bf16[32,8,128]{2,1,0:T(8,128)(2,1)S(1)} %all_to_all.20.own), channel_id=1, source_target_pairs={{0,2},{2,0},{1,3},{3,1},{4,6},{6,4},{5,7},{7,5},{8,10},{10,8},{9,1... | collective-permute-start | bytes 196616 | tf_op jit(solution)/shard_map/ppermute | solution.py:44
  107.3 17.3 %all-to-all-start.2 = ((f32[32,8,128]{2,1,0:T(8,128)}), f32[32,8,128]{2,1,0:T(8,128)S(1)}, u32[]{:S(2)}, u32[]{:S(2)}) async-start(f32[32,8,128]{2,1,0:T(8,128)} %bitcast.1), calls=%async_computation.2 | async-start | bytes 262144 | tf_op jit(solution)/shard_map/all_to_all | solution.py:353
  143.6 6.6 %collective-permute-start.6 = (bf16[768,128]{1,0:T(8,128)(2,1)S(1)}, bf16[768,128]{1,0:T(8,128)(2,1)S(1)}, u32[]{:S(2)}, u32[]{:S(2)}) collective-permute-start(bf16[768,128]{1,0:T(8,128)(2,1)S(1)} %get-tuple-element.42), channel_id=1, source_target_pairs={{0,1},{1,0},{2,3},{3,2},{4,5},{5,4},{6,7},{7,6},{8,9},{9,8},{10,11... | collective-permute-start | bytes 589832 | tf_op jit(solution)/shard_map/ppermute | solution.py:44

commit v6 on v5

--- a/solution.py
+++ b/solution.py
@@ -71,6 +71,10 @@
         copy.start()
     for copy in copies:
         copy.wait()
+
+
+def repeat_kernel(source, target, sems):
+    run([pltpu.make_async_copy(source, target.at[i], sems.at[i]) for i in range(target.shape[0])])
 
 
 def pick_kernel(pos_ref, tokens, picked, groups, rows, sems):
@@ -131,19 +135,21 @@
         spread[place] = chosen
 
 
-def pack_kernel(column, core, packed, sems):
+def pack_kernel(column, core, queries, pairs, sems):
     c = lax.axis_index("c")
     cols = pl.ds(pl.multiple_of(c * 128, 128), 128)
-    run(
-        [
-            pltpu.make_async_copy(column.at[:, :, :, cols], packed.at[c], sems.at[0]),
-            pltpu.make_async_copy(core.at[:, :, :, cols], packed.at[1 - c], sems.at[1]),
-        ]
-    )
-
-
-def project_kernel(tokens, core_tokens, packed, across, query, keys, values, norms, x, w, sems):
-    depth = x.shape[1]
+    copies = []
+    for piece, part in ((column, c), (core, 1 - c)):
+        for first, count, target in ((0, 1, queries), (1, 2, pairs)):
+            copies.append(
+                pltpu.make_async_copy(
+                    piece.at[pl.ds(first, count), :, :, cols], target.at[part], sems.at[len(copies)]
+                )
+            )
+    run(copies)
+
+
+def fill(tokens, core_tokens, packed, across, x, w, sems):
     xl = lax.axis_index("xl")
     copies = []
 
@@ -161,22 +167,46 @@
                 x.at[pl.ds(number * rows, rows), pl.ds(block * width, width)],
             )
     run(copies)
-    weights = [w[kind].reshape(depth, 128) for kind in range(3)]
-    pair = jnp.concatenate(weights[:2], 1)
+
+
+def key_value_kernel(tokens, core_tokens, packed, across, keys, values, x, w, k, v, sems):
+    fill(tokens, core_tokens, packed, across, x, w, sems)
+    depth = x.shape[1]
+    pair = jnp.concatenate([w[kind].reshape(depth, 128) for kind in range(2)], 1)
 
     @pl.loop(0, 6)
     def _(step):
         here = pl.ds(pl.multiple_of(step * 256, 256), 256)
-        left = x[here, :]
-        both = jnp.dot(left, pair, preferred_element_type=F32).astype(BF16)
-        query[here, :] = both[:, :128]
-        keys[here, :] = both[:, 128:]
-        values[here, :] = jnp.dot(left, weights[2], preferred_element_type=F32).astype(BF16)
-        norms[here, :] = down_norm(both[:, 128:])
-
-
-def summary_kernel(own, other, keys, values, norms, marks, pieces, flat, part):
+        both = jnp.dot(x[here, :], pair, preferred_element_type=F32).astype(BF16)
+        k[here, :] = both[:, :128]
+        v[here, :] = both[:, 128:]
+
+    run(
+        [
+            pltpu.make_async_copy(k, keys, sems.at[0]),
+            pltpu.make_async_copy(v, values, sems.at[1]),
+        ]
+    )
+
+
+def query_kernel(tokens, core_tokens, packed, across, query, x, w, sems):
+    fill(tokens, core_tokens, packed, across, x, w, sems)
+    matrix = w[0].reshape(x.shape[1], 128)
+
+    @pl.loop(0, 6)
+    def _(step):
+        here = pl.ds(pl.multiple_of(step * 256, 256), 256)
+        query[here, :] = jnp.dot(x[here, :], matrix, preferred_element_type=F32).astype(BF16)
+
+
+def summary_kernel(own, other, keys_in, values_in, marks, pieces, flat, part, keys, values, sems):
     xl, c = lax.axis_index("xl"), lax.axis_index("c")
+    copies = [
+        pltpu.make_async_copy(keys_in, keys, sems.at[0]),
+        pltpu.make_async_copy(values_in, values, sems.at[1]),
+    ]
+    for copy in copies:
+        copy.start()
     flat[xl] = own[...].reshape(256, 128).astype(F32)
     flat[1 - xl] = other[...].reshape(256, 128).astype(F32)
     rows = []
@@ -187,7 +217,9 @@
             rows.append(jnp.where(c == 0, first, second))
     rows = jnp.concatenate(rows, 0).astype(BF16)
     marks[...] = rows
-    weights = gauss(keys[...], rows, norms[...], side_norm(rows)).astype(BF16)
+    for copy in copies:
+        copy.wait()
+    weights = gauss(keys[...], rows, down_norm(keys[...]), side_norm(rows)).astype(BF16)
     part[...] = lax.dot_general(values[...], weights, COLS, preferred_element_type=F32)
     for half in range(2):
         for four in range(4):
@@ -251,24 +283,26 @@
     return jax.ShapeDtypeStruct(dims, dtype)
 
 
+def in_hbm(*values):
+    return tuple(pltpu.with_memory_space_constraint(value, pltpu.HBM) for value in values)
+
+
 def shards(tokens, weights, landmark_pos):
-    whole = lax.all_to_all(
-        jnp.broadcast_to(tokens[None], (8,) + tokens.shape), HEAD, 0, 0, tiled=True
-    )
+    repeated = call(
+        repeat_kernel,
+        "repeat",
+        shape((8, 768, 256), BF16),
+        [VMEM],
+        1 << 10,
+        3 << 20,
+        [pltpu.SemaphoreType.DMA((8,))],
+        space=HBM,
+    )(tokens)
+    (repeated,) = in_hbm(repeated)
+    whole = lax.all_to_all(repeated, HEAD, 0, 0, tiled=True)
     column = lax.all_gather(weights, "z", axis=1, tiled=True).reshape(3, 16, 32, 256)
     core = shift(column, "c", 1)
-    core, later = lax.optimization_barrier((core, whole))
-    core_tokens = shift(later, "c", 1)
-    packed = call(
-        pack_kernel,
-        "pack",
-        shape((2, 3, 16, 32, 128), BF16),
-        [ANY, ANY],
-        1 << 10,
-        3 << 19,
-        [pltpu.SemaphoreType.DMA((2,))],
-        space=HBM,
-    )(column, core)
+    column, core, whole = in_hbm(column, core, whole)
     picked = call(
         pick_kernel,
         "pick",
@@ -283,6 +317,19 @@
         ],
     )(landmark_pos, whole)
     other_picked = shift(picked, "xl", 1)
+    picked, core = lax.optimization_barrier((picked, core))
+    packed_q, packed_kv = call(
+        pack_kernel,
+        "pack",
+        (shape((2, 1, 16, 32, 128), BF16), shape((2, 2, 16, 32, 128), BF16)),
+        [ANY, ANY],
+        1 << 10,
+        3 << 19,
+        [pltpu.SemaphoreType.DMA((4,))],
+        space=HBM,
+    )(column, core)
+    later, packed_q = lax.optimization_barrier((whole, packed_q))
+    core_tokens = shift(later, "c", 1)
     keep, give = call(
         partial_kernel,
         "partial",
@@ -296,40 +343,53 @@
     spread = call(
         finish_kernel, "finish", shape((32, 8, 128), BF16), [VMEM] * 2, 1 << 14, 1 << 16
     )(keep, received)
-    spread, packed = lax.optimization_barrier((spread, packed))
+    spread, packed_kv = lax.optimization_barrier((spread, packed_kv))
     own_marks = lax.all_to_all(spread, CORES, 0, 0, tiled=True)
-    across = shift(packed, "xl", 1)
-    query, keys, values, norms = call(
-        project_kernel,
-        "project",
-        (
-            shape((1536, 128), BF16),
-            shape((1536, 128), BF16),
-            shape((1536, 128), BF16),
-            shape((1536, 1), F32),
-        ),
+    across_kv = shift(packed_kv, "xl", 1)
+    across_kv, packed_q = lax.optimization_barrier((across_kv, packed_q))
+    across_q = shift(packed_q, "xl", 1)
+    everyone = pltpu.VMEM((1536, 2048), BF16)
+    half = pltpu.VMEM((1536, 128), BF16)
+    sems = pltpu.SemaphoreType.DMA((20,))
+    keys, values = call(
+        key_value_kernel,
+        "key_values",
+        (shape((1536, 128), BF16), shape((1536, 128), BF16)),
         [ANY] * 4,
-        2 * 1536 * 2048 * 384,
+        2 * 1536 * 2048 * 256,
         8 << 20,
-        [
-            pltpu.VMEM((1536, 2048), BF16),
-            pltpu.VMEM((3, 16, 2, 2, 32, 128), BF16),
-            pltpu.SemaphoreType.DMA((20,)),
-        ],
-    )(whole, core_tokens, packed, across)
-
+        [everyone, pltpu.VMEM((2, 16, 2, 2, 32, 128), BF16), half, half, sems],
+        space=HBM,
+    )(whole, core_tokens, packed_kv, across_kv)
+    keys, values = in_hbm(keys, values)
+    own_marks, values = lax.optimization_barrier((own_marks, values))
     other_marks = shift(own_marks, "xl", 1)
     marks, chip = call(
         summary_kernel,
         "summary",
         (shape((256, 128), BF16), shape((256, 128), F32)),
-        [VMEM] * 5,
+        [VMEM, VMEM, HBM, HBM],
         2 * 2 * 1536 * 256 * 128,
         2 << 20,
-        [pltpu.VMEM((2, 256, 128), F32), pltpu.VMEM((128, 256), F32)],
+        [
+            pltpu.VMEM((2, 256, 128), F32),
+            pltpu.VMEM((128, 256), F32),
+            half,
+            half,
+            pltpu.SemaphoreType.DMA((2,)),
+        ],
         1536 * 256,
-    )(own_marks, other_marks, keys, values, norms)
-    chip, marks, query = lax.optimization_barrier((chip, marks, query))
+    )(own_marks, other_marks, keys, values)
+    packed_q, marks = lax.optimization_barrier((packed_q, marks))
+    query = call(
+        query_kernel,
+        "queries",
+        shape((1536, 128), BF16),
+        [ANY] * 4,
+        2 * 1536 * 2048 * 128,
+        7 << 20,
+        [everyone, pltpu.VMEM((1, 16, 2, 2, 32, 128), BF16), sems],
+    )(whole, core_tokens, packed_q, across_q)
     inverse = call(
         inverse_kernel,
         "inverse",

time: 152 us -> 162 us (1.066)
  starting transfers between devices: 37.5 us -> 56.8 us
  blocking collectives: 78.2 us -> 59.1 us
  Pallas kernels: 17.8 us -> 29.8 us
    all_to_all x1 -> x0, blocking collectives: 25.3 us -> none  [shards(): own_marks = lax.all_to_all(spread, CORES, 0, 0, tiled=True)]
    all_to_all x1 -> x2, starting transfers between devices: 7.61 us -> 22.8 us  [the longest x1 15.2 us: shards(): own_marks = lax.all_to_all(spread, CORES, 0, 0, tiled=True)]
    pallas_call x2 -> x4, Pallas kernels: 6.23 us -> 14.6 us  [the longest x1 6.05 us: shards(): call(key_value_kernel, 'key_values', (shape((1536, 128), BF16), shape((15...]
    all_to_all x1 -> x2, waiting for transfers between devices: 0.01 us -> 5.48 us  [the longest x1 5.48 us: shards(): own_marks = lax.all_to_all(spread, CORES, 0, 0, tiled=True)]
    all_to_all x1, blocking collectives: 18.3 us -> 23.8 us  [shards(): spread = lax.all_to_all(spread, CHIPS, 0, 0, tiled=True)]
    all_to_all x1, waiting for transfers between devices: 6.57 us -> 1.13 us  [shards(): pieces = lax.all_to_all(chip.reshape(32, 8, 128), CHIPS, 0, 0, tiled=True)]
    all_to_all x1, starting transfers between devices: 3.86 us -> 7.17 us  [shards(): pieces = lax.all_to_all(chip.reshape(32, 8, 128), CHIPS, 0, 0, tiled=True)]
    broadcast_in_dim x1 -> x0, local copies, waits for them, and re-layouts: 2.85 us -> none  [shards(): jnp.broadcast_to(tokens[None], (8,) + tokens.shape)]
  transfers between devices with their start and end apart: 9 -> 11, of which waited for: 5 -> 6; matrix products, arithmetic and copies ran while one was open for 0% -> 0% of each run, Pallas kernels for 10% -> 16%
where the time goes in v6:
time: 162 us
  blocking collectives  59.1 us (36%)
  starting transfers between devices  56.8 us (35%)
  Pallas kernels  29.8 us (18%)
  waiting for transfers between devices  12.2 us (8%)
  local copies, waits for them, and re-layouts  3.39 us (2%)
    all_gather x1, blocking collectives, shards(): lax.all_gather(weights, 'z', axis=1, tiled=True).reshape(3, 16, 32, 256)  35.3 us
    ppermute x8, starting transfers between devices, shift(): lax.ppermute(value, axis, [(i, (i + step) % size) for i in range(size)])  26.8 us
    all_to_all x1, blocking collectives, shards(): spread = lax.all_to_all(spread, CHIPS, 0, 0, tiled=True)  23.8 us
    all_to_all x1, starting transfers between devices, shards(): own_marks = lax.all_to_all(spread, CORES, 0, 0, tiled=True)  15.2 us
    all_to_all x1, starting transfers between devices, shards(): whole = lax.all_to_all(repeated, HEAD, 0, 0, tiled=True)  7.62 us
    all_to_all x1, starting transfers between devices, shards(): pieces = lax.all_to_all(chip.reshape(32, 8, 128), CHIPS, 0, 0, tiled=True)  7.17 us
    pallas_call x1, Pallas kernels, shards(): call(inverse_kernel, 'inverse', shape((256, 256), F32), [VMEM], 2 * 6 * 1...  6.12 us
    pallas_call x1, Pallas kernels, shards(): call(key_value_kernel, 'key_values', (shape((1536, 128), BF16), shape((15...  6.05 us
  transfers between devices with their start and end apart: 11, of which 6 were waited for; matrix products, arithmetic and copies ran while one was open for 0% of the time, Pallas kernels for 16%

profile of v6, /device:TPU:1, one launch (start us, length us, event | category | flops | bytes accessed | tf_op | source)
XLA Modules:
  0.0 161.6 jit_solution(7144582584023144270)
XLA Ops:
  0.0 1.0 copy-done
  1.0 1.7 %repeat.1 = bf16[8,768,256]{2,1,0:T(8,128)(2,1)} custom-call(bf16[768,256]{1,0:T(8,128)(2,1)S(1)} %copy-done), custom_call_target="tpu_custom_call" | custom-call | flops 1024 | bytes 3145728 | tf_op jit(solution)/shard_map/repeat/pallas_call | solution.py:291
  2.8 7.6 %all-to-all-start = ((bf16[8,768,256]{2,1,0:T(8,128)(2,1)}), bf16[8,768,256]{2,1,0:T(8,128)(2,1)}, u32[]{:S(2)}, u32[]{:S(2)}) async-start(bf16[8,768,256]{2,1,0:T(8,128)(2,1)} %repeat.1), calls=%async_computation | async-start | bytes 6291456 | tf_op jit(solution)/shard_map/all_to_all | solution.py:302
  10.4 35.3 %all_gather.3 = bf16[3,512,256]{2,1,0:T(8,128)(2,1)S(1)} all-gather(bf16[3,32,256]{2,1,0:T(8,128)(2,1)S(1)} %copy-done.6), channel_id=1, replica_groups=mesh['y'=4,'xh'=2,'z'=16,'xl'=2,'c'=2] {'z'}, dimensions={1}, use_global_device_ids=true | all-gather | bytes 835584 | tf_op jit(solution)/shard_map/all_gather | solution.py:303
  45.7 7.6 %collective-permute-start = (bf16[3,16,32,256]{3,2,1,0:T(8,128)(2,1)S(1)}, bf16[3,16,32,256]{3,2,1,0:T(8,128)(2,1)S(1)}, u32[]{:S(2)}, u32[]{:S(2)}) collective-permute-start(bf16[3,16,32,256]{3,2,1,0:T(8,128)(2,1)S(1)} %bitcast.2), channel_id=1, source_target_pairs={{0,1},{1,0},{2,3},{3,2},{4,5},{5,4},{6,7},{7,6},{8,9},{9,8},{10,11... | collective-permute-start | bytes 2359304 | tf_op jit(solution)/shard_map/ppermute | solution.py:44
  53.4 1.7 %pick.1.own = bf16[8,2048]{1,0:T(8,128)(2,1)S(1)} custom-call(s32[2,256]{1,0:T(2,128)S(1)} %copy-done.3, bf16[8,768,256]{2,1,0:T(8,128)(2,1)} %all-to-all-done.tokens), custom_call_target="tpu_custom_call" | custom-call | flops 1048576 | bytes 524288 | tf_op jit(solution)/shard_map/pick/pallas_call | solution.py:306
  55.2 0.9 copy-done.5
  56.1 1.2 pack.1
  57.3 2.3 %collective-permute-start.3 = (bf16[8,768,256]{2,1,0:T(8,128)(2,1)}, bf16[8,768,256]{2,1,0:T(8,128)(2,1)}, u32[]{:S(2)}, u32[]{:S(2)}) collective-permute-start(bf16[8,768,256]{2,1,0:T(8,128)(2,1)} %all-to-all-done.tokens), channel_id=1, source_target_pairs={{0,1},{1,0},{2,3},{3,2},{4,5},{5,4},{6,7},{7,6},{8,9},{9,8},{10,11... | collective-permute-start | bytes 9437192 | tf_op jit(solution)/shard_map/ppermute | solution.py:44
  59.6 2.2 %collective-permute-start.1 = (bf16[8,2048]{1,0:T(8,128)(2,1)S(1)}, bf16[8,2048]{1,0:T(8,128)(2,1)S(1)}, u32[]{:S(2)}, u32[]{:S(2)}) collective-permute-start(bf16[8,2048]{1,0:T(8,128)(2,1)S(1)} %pick.1.own), channel_id=1, source_target_pairs={{0,2},{2,0},{1,3},{3,1},{4,6},{6,4},{5,7},{7,5},{8,10},{10,8},{9,1... | collective-permute-start | bytes 98312 | tf_op jit(solution)/shard_map/ppermute | solution.py:44
  61.8 2.5 %collective-permute-done.1.other = bf16[8,2048]{1,0:T(8,128)(2,1)S(1)} collective-permute-done((bf16[8,2048]{1,0:T(8,128)(2,1)S(1)}, bf16[8,2048]{1,0:T(8,128)(2,1)S(1)}, u32[]{:S(2)}, u32[]{:S(2)}) %collective-permute-start.1) | collective-permute-done | bytes 32800 | tf_op jit(solution)/shard_map/ppermute | solution.py:44
  64.3 1.5 partial.1
  65.8 2.2 %collective-permute-start.2 = (f32[8,128]{1,0:T(8,128)S(1)}, f32[8,128]{1,0:T(8,128)S(1)}, u32[]{:S(2)}, u32[]{:S(2)}) collective-permute-start(f32[8,128]{1,0:T(8,128)S(1)} %get-tuple-element.32), channel_id=1, source_target_pairs={{0,2},{2,0},{1,3},{3,1},{4,6},{6,4},{5,7},{7,5},{8,10},{10,8},{9,1... | collective-permute-start | bytes 12296 | tf_op jit(solution)/shard_map/ppermute | solution.py:44
  68.0 2.2 %collective-permute-done.2.received = f32[8,128]{1,0:T(8,128)S(1)} collective-permute-done((f32[8,128]{1,0:T(8,128)S(1)}, f32[8,128]{1,0:T(8,128)S(1)}, u32[]{:S(2)}, u32[]{:S(2)}) %collective-permute-start.2) | collective-permute-done | bytes 4128 | tf_op jit(solution)/shard_map/ppermute | solution.py:44
  70.8 2.1 %collective-permute-start.4 = (bf16[2,2,16,32,128]{4,3,2,1,0:T(8,128)(2,1)S(1)}, bf16[2,2,16,32,128]{4,3,2,1,0:T(8,128)(2,1)S(1)}, u32[]{:S(2)}, u32[]{:S(2)}) collective-permute-start(bf16[2,2,16,32,128]{4,3,2,1,0:T(8,128)(2,1)S(1)} %get-tuple-element.37.packed), channel_id=1, source_target_pairs={{0,2},{2,0},{1,3},{3,1},{4,6},{6,4},{5,7},{7,5},{8,10},{10,8},{9,1... | collective-permute-start | bytes 1572872 | tf_op jit(solution)/shard_map/ppermute | solution.py:44
  72.9 15.2 %all-to-all-start.1 = ((bf16[32,8,128]{2,1,0:T(8,128)(2,1)}), bf16[32,8,128]{2,1,0:T(8,128)(2,1)S(1)}, u32[]{:S(2)}, u32[]{:S(2)}) async-start(bf16[32,8,128]{2,1,0:T(8,128)(2,1)} %finish.1), calls=%async_computation.1 | async-start | bytes 131072 | tf_op jit(solution)/shard_map/all_to_all | solution.py:347
  88.2 6.0 %key_values.1 = (bf16[1536,128]{1,0:T(8,128)(2,1)S(1)}, bf16[1536,128]{1,0:T(8,128)(2,1)S(1)}) custom-call(bf16[8,768,256]{2,1,0:T(8,128)(2,1)} %all-to-all-done.tokens, bf16[8,768,256]{2,1,0:T(8,128)(2,1)} %collective-permute-done.3.core_tokens, bf16[2,2,16,32,128]{4,3,2,1,0:T(8,128)(2,1)S(1)} %get-tuple-element.37.packed, ...), custom_call_target="tpu_custom_call" | custom-call | flops 1610612736 | bytes 8388608 | tf_op jit(solution)/shard_map/key_values/pallas_call | solution.py:354
  94.2 0.7 copy-done.1
  95.0 0.8 copy-done.2
  95.7 5.5 %all-to-all-done.1.own = bf16[32,8,128]{2,1,0:T(8,128)(2,1)S(1)} async-done(((bf16[32,8,128]{2,1,0:T(8,128)(2,1)}), bf16[32,8,128]{2,1,0:T(8,128)(2,1)S(1)}, u32[]{:S(2)}, u32[]{:S(2)}) %all-to-all-start.1) | async-done | bytes 65568 | tf_op jit(solution)/shard_map/all_to_all | solution.py:347
  101.2 3.0 %collective-permute-start.5 = (bf16[32,8,128]{2,1,0:T(8,128)(2,1)S(1)}, bf16[32,8,128]{2,1,0:T(8,128)(2,1)S(1)}, u32[]{:S(2)}, u32[]{:S(2)}) collective-permute-start(bf16[32,8,128]{2,1,0:T(8,128)(2,1)S(1)} %all-to-all-done.1.own), channel_id=1, source_target_pairs={{0,2},{2,0},{1,3},{3,1},{4,6},{6,4},{5,7},{7,5},{8,10},{10,8},{9,1... | collective-permute-start | bytes 196616 | tf_op jit(solution)/shard_map/ppermute | solution.py:44
  104.3 2.2 %collective-permute-start.6 = (bf16[2,1,16,32,128]{4,3,2,1,0:T(8,128)(2,1)S(1)}, bf16[2,1,16,32,128]{4,3,2,1,0:T(8,128)(2,1)S(1)}, u32[]{:S(2)}, u32[]{:S(2)}) collective-permute-start(bf16[2,1,16,32,128]{4,3,2,1,0:T(8,128)(2,1)S(1)} %get-tuple-element.47.packed), channel_id=1, source_target_pairs={{0,2},{2,0},{1,3},{3,1},{4,6},{6,4},{5,7},{7,5},{8,10},{10,8},{9,1... | collective-permute-start | bytes 786440 | tf_op jit(solution)/shard_map/ppermute | solution.py:44
  106.5 2.8 %summary.1 = (bf16[256,128]{1,0:T(8,128)(2,1)S(1)}, f32[256,128]{1,0:T(8,128)}) custom-call(bf16[32,8,128]{2,1,0:T(8,128)(2,1)S(1)} %all-to-all-done.1.own, bf16[32,8,128]{2,1,0:T(8,128)(2,1)S(1)} %collective-permute-done.5.other, bf16[1536,128]{1,0:T(8,128)(2,1)} %copy-done.1, bf16[1536,128]{1,0:T(8,128)(2,1)} %copy-done.2), custom_call_target="tpu_custom_call" | custom-call | flops 201326592 | bytes 2097152 | tf_op jit(solution)/shard_map/summary/pallas_call | solution.py:367
  109.3 7.2 %all-to-all-start.2 = ((f32[32,8,128]{2,1,0:T(8,128)}), f32[32,8,128]{2,1,0:T(8,128)S(1)}, u32[]{:S(2)}, u32[]{:S(2)}) async-start(f32[32,8,128]{2,1,0:T(8,128)} %bitcast.1), calls=%async_computation.2 | async-start | bytes 262144 | tf_op jit(solution)/shard_map/all_to_all | solution.py:413
  116.5 5.6 %queries.1.query = bf16[1536,128]{1,0:T(8,128)(2,1)S(1)} custom-call(bf16[8,768,256]{2,1,0:T(8,128)(2,1)} %all-to-all-done.tokens, bf16[8,768,256]{2,1,0:T(8,128)(2,1)} %collective-permute-done.3.core_tokens, bf16[2,1,16,32,128]{4,3,2,1,0:T(8,128)(2,1)S(1)} %get-tuple-element.47.packed, bf16[2,1,16,32,128]{4,3,2,1,0:T(8,128)(2,1)S(1)} %collective-permute-done.6.across), custom_call_target="tpu_custom_call" | custom-call | flops 805306368 | bytes 7340032 | tf_op jit(solution)/shard_map/queries/pallas_call | solution.py:384
  122.1 0.8 query_weights.1.weights
  122.9 6.1 %inverse.1 = f32[256,256]{1,0:T(8,128)S(1)} custom-call(bf16[256,128]{1,0:T(8,128)(2,1)S(1)} %get-tuple-element.48.marks.marks_ref), custom_call_target="tpu_custom_call" | custom-call | flops 2415919104 | bytes 524288 | tf_op jit(solution)/shard_map/inverse/pallas_call | solution.py:393
  129.0 1.1 all-to-all-done.2.pieces
  130.5 23.8 %all_to_all.20.spread = bf16[32,8,128]{2,1,0:T(8,128)(2,1)S(1)} all-to-all(bf16[32,8,128]{2,1,0:T(8,128)(2,1)S(1)} %mixed.1), channel_id=1, replica_groups=mesh['y'=4,'xh'=2,'z'=16,'xl'=2,'c'=2] {'z','xl'}, dimensions={0} | all-to-all | bytes 131072 | tf_op jit(solution)/shard_map/all_to_all | solution.py:423
  154.5 5.2 %collective-permute-start.7 = (bf16[768,128]{1,0:T(8,128)(2,1)S(1)}, bf16[768,128]{1,0:T(8,128)(2,1)S(1)}, u32[]{:S(2)}, u32[]{:S(2)}) collective-permute-start(bf16[768,128]{1,0:T(8,128)(2,1)S(1)} %get-tuple-element.52), channel_id=1, source_target_pairs={{0,1},{1,0},{2,3},{3,2},{4,5},{5,4},{6,7},{7,6},{8,9},{9,8},{10,11... | collective-permute-start | bytes 589832 | tf_op jit(solution)/shard_map/ppermute | solution.py:44
  160.0 0.8 collective-permute-done.7.received
  160.7 0.9 join.1
  (20 shorter events, 1.6 us)
Async XLA Ops:
  0.0 1.0 copy-start
  2.7 7.7 %copy-start.6 = (bf16[3,32,256]{2,1,0:T(8,128)(2,1)S(1)}, bf16[3,32,256]{2,1,0:T(8,128)(2,1)}, u32[]{:S(2)}) copy-start(bf16[3,32,256]{2,1,0:T(8,128)(2,1)} %param.4) | copy-start | bytes 147460
  2.8 50.6 %copy-start.3 = (s32[2,256]{1,0:T(2,128)S(1)}, s32[2,256]{1,0:T(2,128)}, u32[]{:S(2)}) copy-start(s32[2,256]{1,0:T(2,128)} %pos_ref.1) | copy-start | bytes 6148
  2.8 50.6 %all-to-all-start = ((bf16[8,768,256]{2,1,0:T(8,128)(2,1)}), bf16[8,768,256]{2,1,0:T(8,128)(2,1)}, u32[]{:S(2)}, u32[]{:S(2)}) async-start(bf16[8,768,256]{2,1,0:T(8,128)(2,1)} %repeat.1), calls=%async_computation | async-start | bytes 6291456 | tf_op jit(solution)/shard_map/all_to_all | solution.py:302
  45.7 9.5 %copy-start.4 = (bf16[3,512,256]{2,1,0:T(8,128)(2,1)}, bf16[3,512,256]{2,1,0:T(8,128)(2,1)S(1)}, u32[]{:S(2)}) copy-start(bf16[3,512,256]{2,1,0:T(8,128)(2,1)S(1)} %all_gather.3) | copy-start | bytes 2359300
  45.7 9.5 %collective-permute-start = (bf16[3,16,32,256]{3,2,1,0:T(8,128)(2,1)S(1)}, bf16[3,16,32,256]{3,2,1,0:T(8,128)(2,1)S(1)}, u32[]{:S(2)}, u32[]{:S(2)}) collective-permute-start(bf16[3,16,32,256]{3,2,1,0:T(8,128)(2,1)S(1)} %bitcast.2), channel_id=1, source_target_pairs={{0,1},{1,0},{2,3},{3,2},{4,5},{5,4},{6,7},{7,6},{8,9},{9,8},{10,11... | collective-permute-start | bytes 2359304 | tf_op jit(solution)/shard_map/ppermute | solution.py:44
  55.2 0.9 copy-start.5
  57.3 30.8 %collective-permute-start.3 = (bf16[8,768,256]{2,1,0:T(8,128)(2,1)}, bf16[8,768,256]{2,1,0:T(8,128)(2,1)}, u32[]{:S(2)}, u32[]{:S(2)}) collective-permute-start(bf16[8,768,256]{2,1,0:T(8,128)(2,1)} %all-to-all-done.tokens), channel_id=1, source_target_pairs={{0,1},{1,0},{2,3},{3,2},{4,5},{5,4},{6,7},{7,6},{8,9},{9,8},{10,11... | collective-permute-start | bytes 9437192 | tf_op jit(solution)/shard_map/ppermute | solution.py:44
  59.6 4.7 %collective-permute-start.1 = (bf16[8,2048]{1,0:T(8,128)(2,1)S(1)}, bf16[8,2048]{1,0:T(8,128)(2,1)S(1)}, u32[]{:S(2)}, u32[]{:S(2)}) collective-permute-start(bf16[8,2048]{1,0:T(8,128)(2,1)S(1)} %pick.1.own), channel_id=1, source_target_pairs={{0,2},{2,0},{1,3},{3,1},{4,6},{6,4},{5,7},{7,5},{8,10},{10,8},{9,1... | collective-permute-start | bytes 98312 | tf_op jit(solution)/shard_map/ppermute | solution.py:44
  65.8 4.4 %collective-permute-start.2 = (f32[8,128]{1,0:T(8,128)S(1)}, f32[8,128]{1,0:T(8,128)S(1)}, u32[]{:S(2)}, u32[]{:S(2)}) collective-permute-start(f32[8,128]{1,0:T(8,128)S(1)} %get-tuple-element.32), channel_id=1, source_target_pairs={{0,2},{2,0},{1,3},{3,1},{4,6},{6,4},{5,7},{7,5},{8,10},{10,8},{9,1... | collective-permute-start | bytes 12296 | tf_op jit(solution)/shard_map/ppermute | solution.py:44
  70.8 17.4 %collective-permute-start.4 = (bf16[2,2,16,32,128]{4,3,2,1,0:T(8,128)(2,1)S(1)}, bf16[2,2,16,32,128]{4,3,2,1,0:T(8,128)(2,1)S(1)}, u32[]{:S(2)}, u32[]{:S(2)}) collective-permute-start(bf16[2,2,16,32,128]{4,3,2,1,0:T(8,128)(2,1)S(1)} %get-tuple-element.37.packed), channel_id=1, source_target_pairs={{0,2},{2,0},{1,3},{3,1},{4,6},{6,4},{5,7},{7,5},{8,10},{10,8},{9,1... | collective-permute-start | bytes 1572872 | tf_op jit(solution)/shard_map/ppermute | solution.py:44
  72.9 28.3 %all-to-all-start.1 = ((bf16[32,8,128]{2,1,0:T(8,128)(2,1)}), bf16[32,8,128]{2,1,0:T(8,128)(2,1)S(1)}, u32[]{:S(2)}, u32[]{:S(2)}) async-start(bf16[32,8,128]{2,1,0:T(8,128)(2,1)} %finish.1), calls=%async_computation.1 | async-start | bytes 131072 | tf_op jit(solution)/shard_map/all_to_all | solution.py:347
  94.2 0.7 copy-start.1
  95.0 0.8 copy-start.2
  101.2 5.3 %collective-permute-start.5 = (bf16[32,8,128]{2,1,0:T(8,128)(2,1)S(1)}, bf16[32,8,128]{2,1,0:T(8,128)(2,1)S(1)}, u32[]{:S(2)}, u32[]{:S(2)}) collective-permute-start(bf16[32,8,128]{2,1,0:T(8,128)(2,1)S(1)} %all-to-all-done.1.own), channel_id=1, source_target_pairs={{0,2},{2,0},{1,3},{3,1},{4,6},{6,4},{5,7},{7,5},{8,10},{10,8},{9,1... | collective-permute-start | bytes 196616 | tf_op jit(solution)/shard_map/ppermute | solution.py:44
  104.3 12.2 %collective-permute-start.6 = (bf16[2,1,16,32,128]{4,3,2,1,0:T(8,128)(2,1)S(1)}, bf16[2,1,16,32,128]{4,3,2,1,0:T(8,128)(2,1)S(1)}, u32[]{:S(2)}, u32[]{:S(2)}) collective-permute-start(bf16[2,1,16,32,128]{4,3,2,1,0:T(8,128)(2,1)S(1)} %get-tuple-element.47.packed), channel_id=1, source_target_pairs={{0,2},{2,0},{1,3},{3,1},{4,6},{6,4},{5,7},{7,5},{8,10},{10,8},{9,1... | collective-permute-start | bytes 786440 | tf_op jit(solution)/shard_map/ppermute | solution.py:44
  109.3 20.9 %all-to-all-start.2 = ((f32[32,8,128]{2,1,0:T(8,128)}), f32[32,8,128]{2,1,0:T(8,128)S(1)}, u32[]{:S(2)}, u32[]{:S(2)}) async-start(f32[32,8,128]{2,1,0:T(8,128)} %bitcast.1), calls=%async_computation.2 | async-start | bytes 262144 | tf_op jit(solution)/shard_map/all_to_all | solution.py:413
  154.5 6.2 %collective-permute-start.7 = (bf16[768,128]{1,0:T(8,128)(2,1)S(1)}, bf16[768,128]{1,0:T(8,128)(2,1)S(1)}, u32[]{:S(2)}, u32[]{:S(2)}) collective-permute-start(bf16[768,128]{1,0:T(8,128)(2,1)S(1)} %get-tuple-element.52), channel_id=1, source_target_pairs={{0,1},{1,0},{2,3},{3,2},{4,5},{5,4},{6,7},{7,6},{8,9},{9,8},{10,11... | collective-permute-start | bytes 589832 | tf_op jit(solution)/shard_map/ppermute | solution.py:44

commit v7 on v5

--- a/solution.py
+++ b/solution.py
@@ -142,37 +142,36 @@
     )
 
 
-def project_kernel(tokens, core_tokens, packed, across, query, keys, values, norms, x, w, sems):
-    depth = x.shape[1]
+def project_kernel(tokens, core_tokens, packed, across, query, keys, values, norms, w, sems):
     xl = lax.axis_index("xl")
     copies = []
-
-    def add(source, target):
-        copies.append(pltpu.make_async_copy(source, target, sems.at[len(copies)]))
-
     for part in range(2):
-        add(packed.at[part], w.at[:, :, xl, part])
-        add(across.at[part], w.at[:, :, 1 - xl, part])
-    blocks, rows, width = tokens.shape
-    for number, source in enumerate((tokens, core_tokens)):
-        for block in range(blocks):
-            add(
-                source.at[block],
-                x.at[pl.ds(number * rows, rows), pl.ds(block * width, width)],
+        for source, row in ((packed, xl), (across, 1 - xl)):
+            copies.append(
+                pltpu.make_async_copy(
+                    source.at[part], w.at[:, :, row, part], sems.at[len(copies)]
+                )
             )
     run(copies)
-    weights = [w[kind].reshape(depth, 128) for kind in range(3)]
+    blocks, rows, width = tokens.shape
+    weights = [w[kind].reshape(blocks * width, 128) for kind in range(3)]
     pair = jnp.concatenate(weights[:2], 1)
-
-    @pl.loop(0, 6)
-    def _(step):
-        here = pl.ds(pl.multiple_of(step * 256, 256), 256)
-        left = x[here, :]
-        both = jnp.dot(left, pair, preferred_element_type=F32).astype(BF16)
-        query[here, :] = both[:, :128]
-        keys[here, :] = both[:, 128:]
-        values[here, :] = jnp.dot(left, weights[2], preferred_element_type=F32).astype(BF16)
-        norms[here, :] = down_norm(both[:, 128:])
+    for number, source in enumerate((tokens, core_tokens)):
+
+        @pl.loop(0, 3)
+        def _(step):
+            start = pl.multiple_of(step * 256, 256)
+            here = pl.ds(number * rows + start, 256)
+            left = jnp.concatenate(
+                [source[block, pl.ds(start, 256), :] for block in range(blocks)], 1
+            )
+            both = jnp.dot(left, pair, preferred_element_type=F32).astype(BF16)
+            query[here, :] = both[:, :128]
+            keys[here, :] = both[:, 128:]
+            values[here, :] = jnp.dot(
+                left, weights[2], preferred_element_type=F32
+            ).astype(BF16)
+            norms[here, :] = down_norm(both[:, 128:])
 
 
 def summary_kernel(own, other, keys, values, norms, marks, pieces, flat, part):
@@ -196,14 +195,27 @@
             ]
 
 
+def parts(value):
+    upper = value.astype(BF16)
+    return upper, (value - upper.astype(F32)).astype(BF16)
+
+
+def three(left, right):
+    upper = jnp.dot(left[0], right[0], preferred_element_type=F32)
+    cross = jnp.dot(left[0], right[1], preferred_element_type=F32)
+    return upper + (cross + jnp.dot(left[1], right[0], preferred_element_type=F32))
+
+
 def inverse_kernel(marks_ref, inverse_ref):
     marks = marks_ref[...]
     inner = gauss(marks, marks, down_norm(marks), side_norm(marks))
     scale_cols = jnp.max(jnp.sum(jnp.abs(inner), 0, keepdims=True), 1, keepdims=True)
     scale_rows = jnp.max(jnp.sum(jnp.abs(inner), 1, keepdims=True), 0, keepdims=True)
     iterate = inner / (scale_cols * scale_rows)
+    inner = parts(inner)
     for step in range(NSTEPS):
-        iterate = 2.0 * iterate - high(high(iterate, inner), iterate)
+        now = parts(iterate)
+        iterate = 2.0 * iterate - three(parts(three(now, inner)), now)
     inverse_ref[...] = iterate
 
 
@@ -308,14 +320,10 @@
             shape((1536, 128), BF16),
             shape((1536, 1), F32),
         ),
-        [ANY] * 4,
+        [VMEM, VMEM, ANY, ANY],
         2 * 1536 * 2048 * 384,
         8 << 20,
-        [
-            pltpu.VMEM((1536, 2048), BF16),
-            pltpu.VMEM((3, 16, 2, 2, 32, 128), BF16),
-            pltpu.SemaphoreType.DMA((20,)),
-        ],
+        [pltpu.VMEM((3, 16, 2, 2, 32, 128), BF16), pltpu.SemaphoreType.DMA((4,))],
     )(whole, core_tokens, packed, across)
 
     other_marks = shift(own_marks, "xl", 1)
@@ -329,7 +337,7 @@
         [pltpu.VMEM((2, 256, 128), F32), pltpu.VMEM((128, 256), F32)],
         1536 * 256,
     )(own_marks, other_marks, keys, values, norms)
-    chip, marks, query = lax.optimization_barrier((chip, marks, query))
+    chip, marks = lax.optimization_barrier((chip, marks))
     inverse = call(
         inverse_kernel,
         "inverse",
@@ -340,6 +348,17 @@
         (),
         256 * 256,
     )(marks)
+    pieces = lax.all_to_all(chip.reshape(32, 8, 128), CHIPS, 0, 0, tiled=True)
+    spread = call(
+        mixed_kernel,
+        "mixed",
+        shape((32, 8, 128), BF16),
+        [VMEM] * 2,
+        2 * 6 * 16 * 256 * 128,
+        1 << 19,
+    )(pieces, inverse)
+    spread, marks = lax.optimization_barrier((spread, marks))
+    spread = lax.all_to_all(spread, CHIPS, 0, 0, tiled=True)
     query_weights = call(
         query_weight_kernel,
         "query_weights",
@@ -350,17 +369,7 @@
         (),
         1536 * 256,
     )(query, marks)
-    pieces = lax.all_to_all(chip.reshape(32, 8, 128), CHIPS, 0, 0, tiled=True)
-    pieces, query_weights = lax.optimization_barrier((pieces, query_weights))
-    spread = call(
-        mixed_kernel,
-        "mixed",
-        shape((32, 8, 128), BF16),
-        [VMEM] * 2,
-        2 * 6 * 16 * 256 * 128,
-        1 << 19,
-    )(pieces, inverse)
-    spread = lax.all_to_all(spread, CHIPS, 0, 0, tiled=True)
+    spread, query_weights = lax.optimization_barrier((spread, query_weights))
     mixed, give = call(
         give_kernel,
         "give",

time: 152 us -> 151 us (level)
  blocking collectives: 78.2 us -> 59.9 us
  waiting for transfers between devices: 12.7 us -> 27.8 us
  starting transfers between devices: 37.5 us -> 42.6 us
  Pallas kernels: 17.8 us -> 14.9 us
    all_to_all x1 -> x0, blocking collectives: 18.3 us -> none  [shards(): spread = lax.all_to_all(spread, CHIPS, 0, 0, tiled=True)]
    all_to_all x0 -> x1, waiting for transfers between devices: none -> 11.8 us  [shards(): spread = lax.all_to_all(spread, CHIPS, 0, 0, tiled=True)]
    all_to_all x0 -> x1, starting transfers between devices: none -> 4.61 us  [shards(): spread = lax.all_to_all(spread, CHIPS, 0, 0, tiled=True)]
    all_to_all x1, waiting for transfers between devices: 6.57 us -> 9.84 us  [shards(): pieces = lax.all_to_all(chip.reshape(32, 8, 128), CHIPS, 0, 0, tiled=True)]
    pallas_call x1, Pallas kernels: 6.12 us -> 3.62 us  [shards(): call(inverse_kernel, 'inverse', shape((256, 256), F32), [VMEM], 2 * 6 * 1...]
  transfers between devices with their start and end apart: 9 -> 10, of which waited for: 5 -> 6; matrix products, arithmetic and copies ran while one was open for 0% -> 0% of each run, Pallas kernels for 10% -> 7%
where the time goes in v7:
time: 151 us; the launch traced here: 150 us
  blocking collectives  59.9 us (40%)
  starting transfers between devices  42.6 us (28%)
  waiting for transfers between devices  27.8 us (18%)
  Pallas kernels  14.9 us (10%)
  local copies, waits for them, and re-layouts  4.63 us (3%)
    all_gather x1, blocking collectives, shards(): lax.all_gather(weights, 'z', axis=1, tiled=True).reshape(3, 16, 32, 256)  34.6 us
    ppermute x7, starting transfers between devices, shift(): lax.ppermute(value, axis, [(i, (i + step) % size) for i in range(size)])  26.5 us
    all_to_all x1, blocking collectives, shards(): own_marks = lax.all_to_all(spread, CORES, 0, 0, tiled=True)  25.3 us
    all_to_all x1, waiting for transfers between devices, shards(): spread = lax.all_to_all(spread, CHIPS, 0, 0, tiled=True)  11.8 us
    all_to_all x1, waiting for transfers between devices, shards(): pieces = lax.all_to_all(chip.reshape(32, 8, 128), CHIPS, 0, 0, tiled=True)  9.84 us
    all_to_all x1, starting transfers between devices, shards(): lax.all_to_all(jnp.broadcast_to(tokens[None], (8,) + tokens.shape), HEAD,...  7.61 us
    ppermute x7, waiting for transfers between devices, shift(): lax.ppermute(value, axis, [(i, (i + step) % size) for i in range(size)])  6.17 us
    pallas_call x1, Pallas kernels, shards(): call(project_kernel, 'project', (shape((1536, 128), BF16), shape((1536, 1...  5 us
  transfers between devices with their start and end apart: 10, of which 6 were waited for; matrix products, arithmetic and copies ran while one was open for 0% of the time, Pallas kernels for 7%

profile of v7, /device:TPU:1, one launch (start us, length us, event | category | flops | bytes accessed | tf_op | source)
XLA Modules:
  0.0 150.1 jit_solution(16484019742721701301)
XLA Ops:
  0.0 2.8 %broadcast_in_dim.2 = bf16[8,768,256]{2,1,0:T(8,128)(2,1)} broadcast(bf16[768,256]{1,0:T(8,128)(2,1)} %param.3), dimensions={1,2} | broadcast | bytes 3538944 | tf_op jit(solution)/shard_map/broadcast_in_dim | solution.py:268
  2.8 7.6 %all-to-all-start = ((bf16[8,768,256]{2,1,0:T(8,128)(2,1)}), bf16[8,768,256]{2,1,0:T(8,128)(2,1)S(1)}, u32[]{:S(2)}, u32[]{:S(2)}) async-start(bf16[8,768,256]{2,1,0:T(8,128)(2,1)} %broadcast_in_dim.2), calls=%async_computation | async-start | bytes 6291456 | tf_op jit(solution)/shard_map/all_to_all | solution.py:267
  10.5 34.6 %all_gather.3 = bf16[3,512,256]{2,1,0:T(8,128)(2,1)S(1)} all-gather(bf16[3,32,256]{2,1,0:T(8,128)(2,1)S(1)} %copy-done.5), channel_id=1, replica_groups=mesh['y'=4,'xh'=2,'z'=16,'xl'=2,'c'=2] {'z'}, dimensions={1}, use_global_device_ids=true | all-gather | bytes 835584 | tf_op jit(solution)/shard_map/all_gather | solution.py:270
  45.1 8.3 %collective-permute-start.1 = (bf16[3,16,32,256]{3,2,1,0:T(8,128)(2,1)S(1)}, bf16[3,16,32,256]{3,2,1,0:T(8,128)(2,1)S(1)}, u32[]{:S(2)}, u32[]{:S(2)}) collective-permute-start(bf16[3,16,32,256]{3,2,1,0:T(8,128)(2,1)S(1)} %bitcast.2), channel_id=1, source_target_pairs={{0,1},{1,0},{2,3},{3,2},{4,5},{5,4},{6,7},{7,6},{8,9},{9,8},{10,11... | collective-permute-start | bytes 2359304 | tf_op jit(solution)/shard_map/ppermute | solution.py:44
  53.4 0.9 copy-done
  54.3 1.0 collective-permute-done.1.core
  55.3 0.9 copy-done.2
  56.2 2.4 %collective-permute-start.4 = (bf16[8,768,256]{2,1,0:T(8,128)(2,1)S(1)}, bf16[8,768,256]{2,1,0:T(8,128)(2,1)S(1)}, u32[]{:S(2)}, u32[]{:S(2)}) collective-permute-start(bf16[8,768,256]{2,1,0:T(8,128)(2,1)S(1)} %all-to-all-done.tokens), channel_id=1, source_target_pairs={{0,1},{1,0},{2,3},{3,2},{4,5},{5,4},{6,7},{7,6},{8,9},{9,8},{10,11... | collective-permute-start | bytes 9437192 | tf_op jit(solution)/shard_map/ppermute | solution.py:44
  58.6 1.0 pick.1.own
  59.6 2.2 %collective-permute-start = (bf16[8,2048]{1,0:T(8,128)(2,1)S(1)}, bf16[8,2048]{1,0:T(8,128)(2,1)S(1)}, u32[]{:S(2)}, u32[]{:S(2)}) collective-permute-start(bf16[8,2048]{1,0:T(8,128)(2,1)S(1)} %pick.1.own), channel_id=1, source_target_pairs={{0,2},{2,0},{1,3},{3,1},{4,6},{6,4},{5,7},{7,5},{8,10},{10,8},{9,1... | collective-permute-start | bytes 98312 | tf_op jit(solution)/shard_map/ppermute | solution.py:44
  61.8 2.4 %collective-permute-done.other = bf16[8,2048]{1,0:T(8,128)(2,1)S(1)} collective-permute-done((bf16[8,2048]{1,0:T(8,128)(2,1)S(1)}, bf16[8,2048]{1,0:T(8,128)(2,1)S(1)}, u32[]{:S(2)}, u32[]{:S(2)}) %collective-permute-start) | collective-permute-done | bytes 32800 | tf_op jit(solution)/shard_map/ppermute | solution.py:44
  64.2 0.4 partial.1
  64.6 2.2 %collective-permute-start.2 = (f32[8,128]{1,0:T(8,128)S(1)}, f32[8,128]{1,0:T(8,128)S(1)}, u32[]{:S(2)}, u32[]{:S(2)}) collective-permute-start(f32[8,128]{1,0:T(8,128)S(1)} %get-tuple-element.27), channel_id=1, source_target_pairs={{0,2},{2,0},{1,3},{3,1},{4,6},{6,4},{5,7},{7,5},{8,10},{10,8},{9,1... | collective-permute-start | bytes 12296 | tf_op jit(solution)/shard_map/ppermute | solution.py:44
  66.9 0.2 pack.1.packed
  67.0 1.9 %collective-permute-done.2.received = f32[8,128]{1,0:T(8,128)S(1)} collective-permute-done((f32[8,128]{1,0:T(8,128)S(1)}, f32[8,128]{1,0:T(8,128)S(1)}, u32[]{:S(2)}, u32[]{:S(2)}) %collective-permute-start.2) | collective-permute-done | bytes 4128 | tf_op jit(solution)/shard_map/ppermute | solution.py:44
  69.0 2.2 %collective-permute-start.5 = (bf16[2,3,16,32,128]{4,3,2,1,0:T(8,128)(2,1)S(1)}, bf16[2,3,16,32,128]{4,3,2,1,0:T(8,128)(2,1)S(1)}, u32[]{:S(2)}, u32[]{:S(2)}) collective-permute-start(bf16[2,3,16,32,128]{4,3,2,1,0:T(8,128)(2,1)S(1)} %pack.1.packed), channel_id=1, source_target_pairs={{0,2},{2,0},{1,3},{3,1},{4,6},{6,4},{5,7},{7,5},{8,10},{10,8},{9,1... | collective-permute-start | bytes 2359304 | tf_op jit(solution)/shard_map/ppermute | solution.py:44
  71.2 25.3 %all_to_all.20.own = bf16[32,8,128]{2,1,0:T(8,128)(2,1)S(1)} all-to-all(bf16[32,8,128]{2,1,0:T(8,128)(2,1)S(1)} %finish.1), channel_id=1, replica_groups=mesh['y'=4,'xh'=2,'z'=16,'xl'=2,'c'=2] {'z','c'}, dimensions={0} | all-to-all | bytes 131072 | tf_op jit(solution)/shard_map/all_to_all | solution.py:312
  96.5 3.0 %collective-permute-start.3 = (bf16[32,8,128]{2,1,0:T(8,128)(2,1)S(1)}, bf16[32,8,128]{2,1,0:T(8,128)(2,1)S(1)}, u32[]{:S(2)}, u32[]{:S(2)}) collective-permute-start(bf16[32,8,128]{2,1,0:T(8,128)(2,1)S(1)} %all_to_all.20.own), channel_id=1, source_target_pairs={{0,2},{2,0},{1,3},{3,1},{4,6},{6,4},{5,7},{7,5},{8,10},{10,8},{9,1... | collective-permute-start | bytes 196616 | tf_op jit(solution)/shard_map/ppermute | solution.py:44
  99.6 5.0 %project.1 = (bf16[1536,128]{1,0:T(8,128)(2,1)S(1)}, bf16[1536,128]{1,0:T(8,128)(2,1)S(1)}, bf16[1536,128]{1,0:T(8,128)(2,1)S(1)}, f32[1536,1]{1,0:T(8,128)S(1)}) custom-call(bf16[8,768,256]{2,1,0:T(8,128)(2,1)S(1)} %all-to-all-done.tokens, bf16[8,768,256]{2,1,0:T(8,128)(2,1)S(1)} %collective-permute-done.4.core_tokens, ...), custom_call_target="tpu_custom_call" | custom-call | flops 2415919104 | bytes 8388608 | tf_op jit(solution)/shard_map/project/pallas_call | solution.py:314
  104.6 1.7 %summary.1 = (bf16[256,128]{1,0:T(8,128)(2,1)S(1)}, f32[256,128]{1,0:T(8,128)}) custom-call(bf16[32,8,128]{2,1,0:T(8,128)(2,1)S(1)} %all_to_all.20.own, bf16[32,8,128]{2,1,0:T(8,128)(2,1)S(1)} %collective-permute-done.3.other, bf16[1536,128]{1,0:T(8,128)(2,1)S(1)} %get-tuple-element.31.keys, bf16[1536,128]{1,0:T(8,128)(2,1)S(1)} %get-tuple-element.32.values, ...), custom_call_target="tpu_custom_call" | custom-call | flops 201326592 | bytes 2097152 | tf_op jit(solution)/shard_map/summary/pallas_call | solution.py:330
  106.3 3.9 %all-to-all-start.2 = ((f32[32,8,128]{2,1,0:T(8,128)}), f32[32,8,128]{2,1,0:T(8,128)S(1)}, u32[]{:S(2)}, u32[]{:S(2)}) async-start(f32[32,8,128]{2,1,0:T(8,128)} %bitcast.1), calls=%async_computation.2 | async-start | bytes 262144 | tf_op jit(solution)/shard_map/all_to_all | solution.py:351
  110.1 3.6 %inverse.1 = f32[256,256]{1,0:T(8,128)S(1)} custom-call(bf16[256,128]{1,0:T(8,128)(2,1)S(1)} %get-tuple-element.40.marks_ref.marks), custom_call_target="tpu_custom_call" | custom-call | flops 2415919104 | bytes 524288 | tf_op jit(solution)/shard_map/inverse/pallas_call | solution.py:341
  113.8 9.8 %all-to-all-done.2.pieces = f32[32,8,128]{2,1,0:T(8,128)S(1)} async-done(((f32[32,8,128]{2,1,0:T(8,128)}), f32[32,8,128]{2,1,0:T(8,128)S(1)}, u32[]{:S(2)}, u32[]{:S(2)}) %all-to-all-start.2) | async-done | bytes 131104 | tf_op jit(solution)/shard_map/all_to_all | solution.py:351
  123.6 1.0 mixed.1
  124.6 4.6 %all-to-all-start.3 = ((bf16[32,8,128]{2,1,0:T(8,128)(2,1)}), bf16[32,8,128]{2,1,0:T(8,128)(2,1)S(1)}, u32[]{:S(2)}, u32[]{:S(2)}) async-start(bf16[32,8,128]{2,1,0:T(8,128)(2,1)} %mixed.1), calls=%async_computation.3 | async-start | bytes 131072 | tf_op jit(solution)/shard_map/all_to_all | solution.py:361
  129.2 0.8 query_weights.1.weights
  130.0 11.8 %all-to-all-done.3.spread = bf16[32,8,128]{2,1,0:T(8,128)(2,1)S(1)} async-done(((bf16[32,8,128]{2,1,0:T(8,128)(2,1)}), bf16[32,8,128]{2,1,0:T(8,128)(2,1)S(1)}, u32[]{:S(2)}, u32[]{:S(2)}) %all-to-all-start.3) | async-done | bytes 65568 | tf_op jit(solution)/shard_map/all_to_all | solution.py:361
  141.8 0.3 give.1
  142.1 6.1 %collective-permute-start.6 = (bf16[768,128]{1,0:T(8,128)(2,1)S(1)}, bf16[768,128]{1,0:T(8,128)(2,1)S(1)}, u32[]{:S(2)}, u32[]{:S(2)}) collective-permute-start(bf16[768,128]{1,0:T(8,128)(2,1)S(1)} %get-tuple-element.44), channel_id=1, source_target_pairs={{0,1},{1,0},{2,3},{3,2},{4,5},{5,4},{6,7},{7,6},{8,9},{9,8},{10,11... | collective-permute-start | bytes 589832 | tf_op jit(solution)/shard_map/ppermute | solution.py:44
  148.2 0.2 keep.1
  148.4 0.8 collective-permute-done.6.received
  149.2 0.9 join.1
  (15 shorter events, 0.0 us)
Async XLA Ops:
  2.8 7.6 %copy-start.5 = (bf16[3,32,256]{2,1,0:T(8,128)(2,1)S(1)}, bf16[3,32,256]{2,1,0:T(8,128)(2,1)}, u32[]{:S(2)}) copy-start(bf16[3,32,256]{2,1,0:T(8,128)(2,1)} %param.4) | copy-start | bytes 147460
  2.8 55.8 %copy-start.4 = (s32[2,256]{1,0:T(2,128)S(1)}, s32[2,256]{1,0:T(2,128)}, u32[]{:S(2)}) copy-start(s32[2,256]{1,0:T(2,128)} %pos_ref.1) | copy-start | bytes 6148
  2.8 53.3 %all-to-all-start = ((bf16[8,768,256]{2,1,0:T(8,128)(2,1)}), bf16[8,768,256]{2,1,0:T(8,128)(2,1)S(1)}, u32[]{:S(2)}, u32[]{:S(2)}) async-start(bf16[8,768,256]{2,1,0:T(8,128)(2,1)} %broadcast_in_dim.2), calls=%async_computation | async-start | bytes 6291456 | tf_op jit(solution)/shard_map/all_to_all | solution.py:267
  45.1 10.2 %collective-permute-start.1 = (bf16[3,16,32,256]{3,2,1,0:T(8,128)(2,1)S(1)}, bf16[3,16,32,256]{3,2,1,0:T(8,128)(2,1)S(1)}, u32[]{:S(2)}, u32[]{:S(2)}) collective-permute-start(bf16[3,16,32,256]{3,2,1,0:T(8,128)(2,1)S(1)} %bitcast.2), channel_id=1, source_target_pairs={{0,1},{1,0},{2,3},{3,2},{4,5},{5,4},{6,7},{7,6},{8,9},{9,8},{10,11... | collective-permute-start | bytes 2359304 | tf_op jit(solution)/shard_map/ppermute | solution.py:44
  53.4 0.9 copy-start
  55.3 0.9 copy-start.2
  56.2 8.0 %copy-start.1 = (bf16[3,512,256]{2,1,0:T(8,128)(2,1)S(1)}, bf16[3,512,256]{2,1,0:T(8,128)(2,1)}, u32[]{:S(2)}) copy-start(bf16[3,512,256]{2,1,0:T(8,128)(2,1)} %copy-done) | copy-start | bytes 2359300
  56.2 8.0 %copy-start.3 = (bf16[3,16,32,256]{3,2,1,0:T(8,128)(2,1)S(1)}, bf16[3,16,32,256]{3,2,1,0:T(8,128)(2,1)}, u32[]{:S(2)}) copy-start(bf16[3,16,32,256]{3,2,1,0:T(8,128)(2,1)} %copy-done.2) | copy-start | bytes 2359300
  56.2 43.4 %collective-permute-start.4 = (bf16[8,768,256]{2,1,0:T(8,128)(2,1)S(1)}, bf16[8,768,256]{2,1,0:T(8,128)(2,1)S(1)}, u32[]{:S(2)}, u32[]{:S(2)}) collective-permute-start(bf16[8,768,256]{2,1,0:T(8,128)(2,1)S(1)} %all-to-all-done.tokens), channel_id=1, source_target_pairs={{0,1},{1,0},{2,3},{3,2},{4,5},{5,4},{6,7},{7,6},{8,9},{9,8},{10,11... | collective-permute-start | bytes 9437192 | tf_op jit(solution)/shard_map/ppermute | solution.py:44
  59.6 4.7 %collective-permute-start = (bf16[8,2048]{1,0:T(8,128)(2,1)S(1)}, bf16[8,2048]{1,0:T(8,128)(2,1)S(1)}, u32[]{:S(2)}, u32[]{:S(2)}) collective-permute-start(bf16[8,2048]{1,0:T(8,128)(2,1)S(1)} %pick.1.own), channel_id=1, source_target_pairs={{0,2},{2,0},{1,3},{3,1},{4,6},{6,4},{5,7},{7,5},{8,10},{10,8},{9,1... | collective-permute-start | bytes 98312 | tf_op jit(solution)/shard_map/ppermute | solution.py:44
  64.6 4.4 %collective-permute-start.2 = (f32[8,128]{1,0:T(8,128)S(1)}, f32[8,128]{1,0:T(8,128)S(1)}, u32[]{:S(2)}, u32[]{:S(2)}) collective-permute-start(f32[8,128]{1,0:T(8,128)S(1)} %get-tuple-element.27), channel_id=1, source_target_pairs={{0,2},{2,0},{1,3},{3,1},{4,6},{6,4},{5,7},{7,5},{8,10},{10,8},{9,1... | collective-permute-start | bytes 12296 | tf_op jit(solution)/shard_map/ppermute | solution.py:44
  69.0 30.6 %collective-permute-start.5 = (bf16[2,3,16,32,128]{4,3,2,1,0:T(8,128)(2,1)S(1)}, bf16[2,3,16,32,128]{4,3,2,1,0:T(8,128)(2,1)S(1)}, u32[]{:S(2)}, u32[]{:S(2)}) collective-permute-start(bf16[2,3,16,32,128]{4,3,2,1,0:T(8,128)(2,1)S(1)} %pack.1.packed), channel_id=1, source_target_pairs={{0,2},{2,0},{1,3},{3,1},{4,6},{6,4},{5,7},{7,5},{8,10},{10,8},{9,1... | collective-permute-start | bytes 2359304 | tf_op jit(solution)/shard_map/ppermute | solution.py:44
  96.5 8.1 %collective-permute-start.3 = (bf16[32,8,128]{2,1,0:T(8,128)(2,1)S(1)}, bf16[32,8,128]{2,1,0:T(8,128)(2,1)S(1)}, u32[]{:S(2)}, u32[]{:S(2)}) collective-permute-start(bf16[32,8,128]{2,1,0:T(8,128)(2,1)S(1)} %all_to_all.20.own), channel_id=1, source_target_pairs={{0,2},{2,0},{1,3},{3,1},{4,6},{6,4},{5,7},{7,5},{8,10},{10,8},{9,1... | collective-permute-start | bytes 196616 | tf_op jit(solution)/shard_map/ppermute | solution.py:44
  106.3 17.3 %all-to-all-start.2 = ((f32[32,8,128]{2,1,0:T(8,128)}), f32[32,8,128]{2,1,0:T(8,128)S(1)}, u32[]{:S(2)}, u32[]{:S(2)}) async-start(f32[32,8,128]{2,1,0:T(8,128)} %bitcast.1), calls=%async_computation.2 | async-start | bytes 262144 | tf_op jit(solution)/shard_map/all_to_all | solution.py:351
  124.6 17.2 %all-to-all-start.3 = ((bf16[32,8,128]{2,1,0:T(8,128)(2,1)}), bf16[32,8,128]{2,1,0:T(8,128)(2,1)S(1)}, u32[]{:S(2)}, u32[]{:S(2)}) async-start(bf16[32,8,128]{2,1,0:T(8,128)(2,1)} %mixed.1), calls=%async_computation.3 | async-start | bytes 131072 | tf_op jit(solution)/shard_map/all_to_all | solution.py:361
  142.1 7.2 %collective-permute-start.6 = (bf16[768,128]{1,0:T(8,128)(2,1)S(1)}, bf16[768,128]{1,0:T(8,128)(2,1)S(1)}, u32[]{:S(2)}, u32[]{:S(2)}) collective-permute-start(bf16[768,128]{1,0:T(8,128)(2,1)S(1)} %get-tuple-element.44), channel_id=1, source_target_pairs={{0,1},{1,0},{2,3},{3,2},{4,5},{5,4},{6,7},{7,6},{8,9},{9,8},{10,11... | collective-permute-start | bytes 589832 | tf_op jit(solution)/shard_map/ppermute | solution.py:44

commit v8 on v7

--- a/solution.py
+++ b/solution.py
@@ -14,7 +14,6 @@
 HEAD = ("y", "xh")
 SEQ = ("z", "xl", "c")
 CHIPS = ("z", "xl")
-CORES = ("z", "c")
 
 VMEM = pl.BlockSpec(memory_space=pltpu.VMEM)
 SMEM = pl.BlockSpec(memory_space=pltpu.SMEM)
@@ -97,23 +96,32 @@
     picked[...] = rows[...].astype(BF16)
 
 
-def partial_kernel(own, other, column, core, keep, give, w, sems):
+def partial_kernel(own, other, column, across, keep, give, w, sems):
     xl, c = lax.axis_index("xl"), lax.axis_index("c")
     run(
         [
-            pltpu.make_async_copy(column.at[pl.ds(0, 2)], w.at[:, :, c], sems.at[0]),
-            pltpu.make_async_copy(core.at[pl.ds(0, 2)], w.at[:, :, 1 - c], sems.at[1]),
+            pltpu.make_async_copy(column.at[pl.ds(0, 2)], w.at[:, :, xl], sems.at[0]),
+            pltpu.make_async_copy(across.at[pl.ds(0, 2)], w.at[:, :, 1 - xl], sems.at[1]),
         ]
     )
     rows = jnp.concatenate([own[...].astype(F32), other[...].astype(F32)], 0)
-    low = lax.broadcasted_iota(jnp.int32, (16, 128), 1) < 64
+    quarter = lax.broadcasted_iota(jnp.int32, (16, 128), 1) // 32
     tiles = []
     for pair in range(8):
         even = rows[:, pair * 256 : pair * 256 + 128]
         odd = rows[:, pair * 256 + 128 : pair * 256 + 256]
-        first = jnp.where(low, even, pltpu.roll(odd, 64, 1))
-        second = jnp.where(low, pltpu.roll(even, 64, 1), odd)
-        tiles.append(jnp.where(xl == 0, first, second))
+        even1, odd1 = pltpu.roll(even, 96, 1), pltpu.roll(odd, 32, 1)
+        first = (even, even1, pltpu.roll(odd, 64, 1), odd1)
+        second = (even1, pltpu.roll(even, 64, 1), odd1, odd)
+        zero, one = (
+            jnp.where(
+                quarter < 2,
+                jnp.where(quarter == 0, four[0], four[1]),
+                jnp.where(quarter == 2, four[2], four[3]),
+            )
+            for four in (first, second)
+        )
+        tiles.append(jnp.where(c == 0, zero, one))
     left = jnp.concatenate(tiles, 1).astype(BF16)
     results = [
         jnp.dot(left, w[kind].reshape(1024, 256), preferred_element_type=F32) for kind in range(2)
@@ -131,25 +139,28 @@
         spread[place] = chosen
 
 
-def pack_kernel(column, core, packed, sems):
-    c = lax.axis_index("c")
-    cols = pl.ds(pl.multiple_of(c * 128, 128), 128)
-    run(
-        [
-            pltpu.make_async_copy(column.at[:, :, :, cols], packed.at[c], sems.at[0]),
-            pltpu.make_async_copy(core.at[:, :, :, cols], packed.at[1 - c], sems.at[1]),
-        ]
-    )
-
-
-def project_kernel(tokens, core_tokens, packed, across, query, keys, values, norms, w, sems):
-    xl = lax.axis_index("xl")
+def pack_kernel(column, across, packed, given, sems):
+    xl, c = lax.axis_index("xl"), lax.axis_index("c")
     copies = []
-    for part in range(2):
-        for source, row in ((packed, xl), (across, 1 - xl)):
+    for target, head in ((packed, c), (given, 1 - c)):
+        cols = pl.ds(pl.multiple_of(head * 128, 128), 128)
+        for piece, side in ((column, xl), (across, 1 - xl)):
             copies.append(
                 pltpu.make_async_copy(
-                    source.at[part], w.at[:, :, row, part], sems.at[len(copies)]
+                    piece.at[:, :, :, cols], target.at[side], sems.at[len(copies)]
+                )
+            )
+    run(copies)
+
+
+def project_kernel(tokens, core_tokens, packed, received, query, keys, values, norms, w, sems):
+    c = lax.axis_index("c")
+    copies = []
+    for row in range(2):
+        for source, part in ((packed, c), (received, 1 - c)):
+            copies.append(
+                pltpu.make_async_copy(
+                    source.at[row], w.at[:, :, row, part], sems.at[len(copies)]
                 )
             )
     run(copies)
@@ -175,9 +186,9 @@
 
 
 def summary_kernel(own, other, keys, values, norms, marks, pieces, flat, part):
-    xl, c = lax.axis_index("xl"), lax.axis_index("c")
-    flat[xl] = own[...].reshape(256, 128).astype(F32)
-    flat[1 - xl] = other[...].reshape(256, 128).astype(F32)
+    c = lax.axis_index("c")
+    flat[c] = own[...].reshape(256, 128).astype(F32)
+    flat[1 - c] = other[...].reshape(256, 128).astype(F32)
     rows = []
     for side in range(2):
         for mark in range(4):
@@ -268,19 +279,8 @@
         jnp.broadcast_to(tokens[None], (8,) + tokens.shape), HEAD, 0, 0, tiled=True
     )
     column = lax.all_gather(weights, "z", axis=1, tiled=True).reshape(3, 16, 32, 256)
-    core = shift(column, "c", 1)
-    core, later = lax.optimization_barrier((core, whole))
-    core_tokens = shift(later, "c", 1)
-    packed = call(
-        pack_kernel,
-        "pack",
-        shape((2, 3, 16, 32, 128), BF16),
-        [ANY, ANY],
-        1 << 10,
-        3 << 19,
-        [pltpu.SemaphoreType.DMA((2,))],
-        space=HBM,
-    )(column, core)
+    landmark_pos, column = lax.optimization_barrier((landmark_pos, column))
+    across = shift(column, "xl", 1)
     picked = call(
         pick_kernel,
         "pick",
@@ -294,7 +294,7 @@
             pltpu.SemaphoreType.DMA((8,)),
         ],
     )(landmark_pos, whole)
-    other_picked = shift(picked, "xl", 1)
+    other_picked = shift(picked, "c", 1)
     keep, give = call(
         partial_kernel,
         "partial",
@@ -303,14 +303,25 @@
         2 * 16 * 1024 * 512,
         1 << 20,
         [pltpu.VMEM((2, 16, 2, 32, 256), BF16), pltpu.SemaphoreType.DMA((2,))],
-    )(picked, other_picked, column, core)
-    received = shift(give, "xl", 1)
+    )(picked, other_picked, column, across)
+    received = shift(give, "c", 1)
+    column, across, whole, received = lax.optimization_barrier((column, across, whole, received))
+    core_tokens = shift(whole, "c", 1)
+    packed, given = call(
+        pack_kernel,
+        "pack",
+        (shape((2, 3, 16, 32, 128), BF16), shape((2, 3, 16, 32, 128), BF16)),
+        [ANY, ANY],
+        1 << 10,
+        3 << 19,
+        [pltpu.SemaphoreType.DMA((4,))],
+        space=HBM,
+    )(column, across)
+    core_weights = shift(given, "c", 1)
     spread = call(
         finish_kernel, "finish", shape((32, 8, 128), BF16), [VMEM] * 2, 1 << 14, 1 << 16
     )(keep, received)
-    spread, packed = lax.optimization_barrier((spread, packed))
-    own_marks = lax.all_to_all(spread, CORES, 0, 0, tiled=True)
-    across = shift(packed, "xl", 1)
+    own_marks = lax.all_to_all(spread, CHIPS, 0, 0, tiled=True)
     query, keys, values, norms = call(
         project_kernel,
         "project",
@@ -324,9 +335,9 @@
         2 * 1536 * 2048 * 384,
         8 << 20,
         [pltpu.VMEM((3, 16, 2, 2, 32, 128), BF16), pltpu.SemaphoreType.DMA((4,))],
-    )(whole, core_tokens, packed, across)
-
-    other_marks = shift(own_marks, "xl", 1)
+    )(whole, core_tokens, packed, core_weights)
+
+    other_marks = shift(own_marks, "c", 1)
     marks, chip = call(
         summary_kernel,
         "summary",

time: 151 us -> 157 us (1.040)
  starting transfers between devices: 42.6 us -> 48.7 us
  Pallas kernels: 14.9 us -> 17.3 us
  local copies, waits for them, and re-layouts: 4.63 us -> 2.85 us
    ppermute x7, starting transfers between devices: 26.5 us -> 33.4 us  [shift(): lax.ppermute(value, axis, [(i, (i + step) % size) for i in range(size)])]
    all_to_all x1, waiting for transfers between devices: 9.84 us -> 12.4 us  [shards(): pieces = lax.all_to_all(chip.reshape(32, 8, 128), CHIPS, 0, 0, tiled=True)]
    all_to_all x1, blocking collectives: 25.3 us -> 22.8 us  [shards(): own_marks = lax.all_to_all(spread, CHIPS, 0, 0, tiled=True)]
    ppermute x7, waiting for transfers between devices: 6.17 us -> 3.93 us  [shift(): lax.ppermute(value, axis, [(i, (i + step) % size) for i in range(size)])]
    all_gather x1, blocking collectives: 34.6 us -> 36.6 us  [shards(): lax.all_gather(weights, 'z', axis=1, tiled=True).reshape(3, 16, 32, 256)]
    unnamed x12 -> x4, local copies, waits for them, and re-layouts: 1.79 us -> 0.01 us
  transfers between devices with their start and end apart: 10 -> 10, of which waited for: 6 -> 5; matrix products, arithmetic and copies ran while one was open for 0% -> 0% of each run, Pallas kernels for 7% -> 8%
where the time goes in v8:
time: 157 us; the launch traced here: 156 us
  blocking collectives  59.4 us (38%)
  starting transfers between devices  48.7 us (31%)
  waiting for transfers between devices  28.1 us (18%)
  Pallas kernels  17.3 us (11%)
  local copies, waits for them, and re-layouts  2.85 us (2%)
    all_gather x1, blocking collectives, shards(): lax.all_gather(weights, 'z', axis=1, tiled=True).reshape(3, 16, 32, 256)  36.6 us
    ppermute x7, starting transfers between devices, shift(): lax.ppermute(value, axis, [(i, (i + step) % size) for i in range(size)])  33.4 us
    all_to_all x1, blocking collectives, shards(): own_marks = lax.all_to_all(spread, CHIPS, 0, 0, tiled=True)  22.8 us
    all_to_all x1, waiting for transfers between devices, shards(): pieces = lax.all_to_all(chip.reshape(32, 8, 128), CHIPS, 0, 0, tiled=True)  12.4 us
    all_to_all x1, waiting for transfers between devices, shards(): spread = lax.all_to_all(spread, CHIPS, 0, 0, tiled=True)  11.7 us
    all_to_all x1, starting transfers between devices, shards(): lax.all_to_all(jnp.broadcast_to(tokens[None], (8,) + tokens.shape), HEAD,...  7.61 us
    pallas_call x1, Pallas kernels, shards(): call(project_kernel, 'project', (shape((1536, 128), BF16), shape((1536, 1...  4.99 us
    ppermute x7, waiting for transfers between devices, shift(): lax.ppermute(value, axis, [(i, (i + step) % size) for i in range(size)])  3.93 us
  transfers between devices with their start and end apart: 10, of which 5 were waited for; matrix products, arithmetic and copies ran while one was open for 0% of the time, Pallas kernels for 8%

profile of v8, /device:TPU:1, one launch (start us, length us, event | category | flops | bytes accessed | tf_op | source)
XLA Modules:
  0.0 156.5 jit_solution(4792594053506354580)
XLA Ops:
  0.0 2.8 %broadcast_in_dim.2 = bf16[8,768,256]{2,1,0:T(8,128)(2,1)} broadcast(bf16[768,256]{1,0:T(8,128)(2,1)} %param.3), dimensions={1,2} | broadcast | bytes 3538944 | tf_op jit(solution)/shard_map/broadcast_in_dim | solution.py:279
  2.8 7.6 %all-to-all-start = ((bf16[8,768,256]{2,1,0:T(8,128)(2,1)}), bf16[8,768,256]{2,1,0:T(8,128)(2,1)S(1)}, u32[]{:S(2)}, u32[]{:S(2)}) async-start(bf16[8,768,256]{2,1,0:T(8,128)(2,1)} %broadcast_in_dim.2), calls=%async_computation | async-start | bytes 6291456 | tf_op jit(solution)/shard_map/all_to_all | solution.py:278
  10.5 36.6 %all_gather.3 = bf16[3,512,256]{2,1,0:T(8,128)(2,1)} all-gather(bf16[3,32,256]{2,1,0:T(8,128)(2,1)S(1)} %copy-done.1), channel_id=1, replica_groups=mesh['y'=4,'xh'=2,'z'=16,'xl'=2,'c'=2] {'z'}, dimensions={1}, use_global_device_ids=true | all-gather | bytes 835584 | tf_op jit(solution)/shard_map/all_gather | solution.py:281
  47.0 2.2 %collective-permute-start.1 = (bf16[3,16,32,256]{3,2,1,0:T(8,128)(2,1)}, bf16[3,16,32,256]{3,2,1,0:T(8,128)(2,1)}, u32[]{:S(2)}, u32[]{:S(2)}) collective-permute-start(bf16[3,16,32,256]{3,2,1,0:T(8,128)(2,1)} %bitcast.column), channel_id=1, source_target_pairs={{0,2},{2,0},{1,3},{3,1},{4,6},{6,4},{5,7},{7,5},{8,10},{10,8},{9,1... | collective-permute-start | bytes 2359304 | tf_op jit(solution)/shard_map/ppermute | solution.py:43
  49.3 0.0 all-to-all-done.tokens
  49.3 1.0 pick.1.own
  50.2 8.9 %collective-permute-start = (bf16[8,2048]{1,0:T(8,128)(2,1)S(1)}, bf16[8,2048]{1,0:T(8,128)(2,1)S(1)}, u32[]{:S(2)}, u32[]{:S(2)}) collective-permute-start(bf16[8,2048]{1,0:T(8,128)(2,1)S(1)} %pick.1.own), channel_id=1, source_target_pairs={{0,1},{1,0},{2,3},{3,2},{4,5},{5,4},{6,7},{7,6},{8,9},{9,8},{10,11... | collective-permute-start | bytes 98312 | tf_op jit(solution)/shard_map/ppermute | solution.py:43
  59.2 2.3 %collective-permute-done.1.across = bf16[3,16,32,256]{3,2,1,0:T(8,128)(2,1)} collective-permute-done((bf16[3,16,32,256]{3,2,1,0:T(8,128)(2,1)}, bf16[3,16,32,256]{3,2,1,0:T(8,128)(2,1)}, u32[]{:S(2)}, u32[]{:S(2)}) %collective-permute-start.1) | collective-permute-done | bytes 786464 | tf_op jit(solution)/shard_map/ppermute | solution.py:43
  61.5 0.0 collective-permute-done.other
  61.5 1.5 partial.1
  63.0 9.6 %collective-permute-start.2 = (f32[8,128]{1,0:T(8,128)S(1)}, f32[8,128]{1,0:T(8,128)S(1)}, u32[]{:S(2)}, u32[]{:S(2)}) collective-permute-start(f32[8,128]{1,0:T(8,128)S(1)} %get-tuple-element.32), channel_id=1, source_target_pairs={{0,1},{1,0},{2,3},{3,2},{4,5},{5,4},{6,7},{7,6},{8,9},{9,8},{10,11... | collective-permute-start | bytes 12296 | tf_op jit(solution)/shard_map/ppermute | solution.py:43
  72.6 0.8 collective-permute-done.2.received
  73.4 2.2 %collective-permute-start.4 = (bf16[8,768,256]{2,1,0:T(8,128)(2,1)S(1)}, bf16[8,768,256]{2,1,0:T(8,128)(2,1)S(1)}, u32[]{:S(2)}, u32[]{:S(2)}) collective-permute-start(bf16[8,768,256]{2,1,0:T(8,128)(2,1)S(1)} %all-to-all-done.tokens), channel_id=1, source_target_pairs={{0,1},{1,0},{2,3},{3,2},{4,5},{5,4},{6,7},{7,6},{8,9},{9,8},{10,11... | collective-permute-start | bytes 9437192 | tf_op jit(solution)/shard_map/ppermute | solution.py:43
  75.7 1.4 pack.1
  77.1 2.1 %collective-permute-start.5 = (bf16[2,3,16,32,128]{4,3,2,1,0:T(8,128)(2,1)S(1)}, bf16[2,3,16,32,128]{4,3,2,1,0:T(8,128)(2,1)S(1)}, u32[]{:S(2)}, u32[]{:S(2)}) collective-permute-start(bf16[2,3,16,32,128]{4,3,2,1,0:T(8,128)(2,1)S(1)} %get-tuple-element.38), channel_id=1, source_target_pairs={{0,1},{1,0},{2,3},{3,2},{4,5},{5,4},{6,7},{7,6},{8,9},{9,8},{10,11... | collective-permute-start | bytes 2359304 | tf_op jit(solution)/shard_map/ppermute | solution.py:43
  79.2 22.8 %all_to_all.20.own = bf16[32,8,128]{2,1,0:T(8,128)(2,1)S(1)} all-to-all(bf16[32,8,128]{2,1,0:T(8,128)(2,1)S(1)} %finish.1), channel_id=1, replica_groups=mesh['y'=4,'xh'=2,'z'=16,'xl'=2,'c'=2] {'z','xl'}, dimensions={0} | all-to-all | bytes 131072 | tf_op jit(solution)/shard_map/all_to_all | solution.py:324
  102.0 4.0 %collective-permute-start.3 = (bf16[32,8,128]{2,1,0:T(8,128)(2,1)S(1)}, bf16[32,8,128]{2,1,0:T(8,128)(2,1)S(1)}, u32[]{:S(2)}, u32[]{:S(2)}) collective-permute-start(bf16[32,8,128]{2,1,0:T(8,128)(2,1)S(1)} %all_to_all.20.own), channel_id=1, source_target_pairs={{0,1},{1,0},{2,3},{3,2},{4,5},{5,4},{6,7},{7,6},{8,9},{9,8},{10,11... | collective-permute-start | bytes 196616 | tf_op jit(solution)/shard_map/ppermute | solution.py:43
  105.9 0.0 collective-permute-done.5.received
  106.0 5.0 %project.1 = (bf16[1536,128]{1,0:T(8,128)(2,1)S(1)}, bf16[1536,128]{1,0:T(8,128)(2,1)S(1)}, bf16[1536,128]{1,0:T(8,128)(2,1)S(1)}, f32[1536,1]{1,0:T(8,128)S(1)}) custom-call(bf16[8,768,256]{2,1,0:T(8,128)(2,1)S(1)} %all-to-all-done.tokens, bf16[8,768,256]{2,1,0:T(8,128)(2,1)S(1)} %collective-permute-done.4.core_tokens, ...), custom_call_target="tpu_custom_call" | custom-call | flops 2415919104 | bytes 8388608 | tf_op jit(solution)/shard_map/project/pallas_call | solution.py:325
  111.0 1.7 %summary.1 = (bf16[256,128]{1,0:T(8,128)(2,1)S(1)}, f32[256,128]{1,0:T(8,128)}) custom-call(bf16[32,8,128]{2,1,0:T(8,128)(2,1)S(1)} %all_to_all.20.own, bf16[32,8,128]{2,1,0:T(8,128)(2,1)S(1)} %collective-permute-done.3.other, bf16[1536,128]{1,0:T(8,128)(2,1)S(1)} %get-tuple-element.39.keys, bf16[1536,128]{1,0:T(8,128)(2,1)S(1)} %get-tuple-element.40.values, ...), custom_call_target="tpu_custom_call" | custom-call | flops 201326592 | bytes 2097152 | tf_op jit(solution)/shard_map/summary/pallas_call | solution.py:341
  112.6 3.9 %all-to-all-start.2 = ((f32[32,8,128]{2,1,0:T(8,128)}), f32[32,8,128]{2,1,0:T(8,128)S(1)}, u32[]{:S(2)}, u32[]{:S(2)}) async-start(f32[32,8,128]{2,1,0:T(8,128)} %bitcast.1), calls=%async_computation.2 | async-start | bytes 262144 | tf_op jit(solution)/shard_map/all_to_all | solution.py:362
  116.5 3.6 %inverse.1 = f32[256,256]{1,0:T(8,128)S(1)} custom-call(bf16[256,128]{1,0:T(8,128)(2,1)S(1)} %get-tuple-element.48.marks_ref.marks), custom_call_target="tpu_custom_call" | custom-call | flops 2415919104 | bytes 524288 | tf_op jit(solution)/shard_map/inverse/pallas_call | solution.py:352
  120.1 12.4 %all-to-all-done.2.pieces = f32[32,8,128]{2,1,0:T(8,128)S(1)} async-done(((f32[32,8,128]{2,1,0:T(8,128)}), f32[32,8,128]{2,1,0:T(8,128)S(1)}, u32[]{:S(2)}, u32[]{:S(2)}) %all-to-all-start.2) | async-done | bytes 131104 | tf_op jit(solution)/shard_map/all_to_all | solution.py:362
  132.5 1.0 mixed.1
  133.5 3.9 %all-to-all-start.3 = ((bf16[32,8,128]{2,1,0:T(8,128)(2,1)}), bf16[32,8,128]{2,1,0:T(8,128)(2,1)S(1)}, u32[]{:S(2)}, u32[]{:S(2)}) async-start(bf16[32,8,128]{2,1,0:T(8,128)(2,1)} %mixed.1), calls=%async_computation.3 | async-start | bytes 131072 | tf_op jit(solution)/shard_map/all_to_all | solution.py:372
  137.4 0.8 query_weights.1.weights
  138.2 11.7 %all-to-all-done.3.spread = bf16[32,8,128]{2,1,0:T(8,128)(2,1)S(1)} async-done(((bf16[32,8,128]{2,1,0:T(8,128)(2,1)}), bf16[32,8,128]{2,1,0:T(8,128)(2,1)S(1)}, u32[]{:S(2)}, u32[]{:S(2)}) %all-to-all-start.3) | async-done | bytes 65568 | tf_op jit(solution)/shard_map/all_to_all | solution.py:372
  149.9 0.3 give.1
  150.2 4.4 %collective-permute-start.6 = (bf16[768,128]{1,0:T(8,128)(2,1)S(1)}, bf16[768,128]{1,0:T(8,128)(2,1)S(1)}, u32[]{:S(2)}, u32[]{:S(2)}) collective-permute-start(bf16[768,128]{1,0:T(8,128)(2,1)S(1)} %get-tuple-element.52), channel_id=1, source_target_pairs={{0,1},{1,0},{2,3},{3,2},{4,5},{5,4},{6,7},{7,6},{8,9},{9,8},{10,11... | collective-permute-start | bytes 589832 | tf_op jit(solution)/shard_map/ppermute | solution.py:43
  154.6 0.2 keep.1
  154.8 0.8 collective-permute-done.6.received
  155.6 0.9 join.1
  (7 shorter events, 0.0 us)
Async XLA Ops:
  2.8 7.6 %copy-start.1 = (bf16[3,32,256]{2,1,0:T(8,128)(2,1)S(1)}, bf16[3,32,256]{2,1,0:T(8,128)(2,1)}, u32[]{:S(2)}) copy-start(bf16[3,32,256]{2,1,0:T(8,128)(2,1)} %param.4) | copy-start | bytes 147460
  2.8 46.4 %copy-start = (s32[2,256]{1,0:T(2,128)S(1)}, s32[2,256]{1,0:T(2,128)}, u32[]{:S(2)}) copy-start(s32[2,256]{1,0:T(2,128)} %pos_ref) | copy-start | bytes 6148
  2.8 46.4 %all-to-all-start = ((bf16[8,768,256]{2,1,0:T(8,128)(2,1)}), bf16[8,768,256]{2,1,0:T(8,128)(2,1)S(1)}, u32[]{:S(2)}, u32[]{:S(2)}) async-start(bf16[8,768,256]{2,1,0:T(8,128)(2,1)} %broadcast_in_dim.2), calls=%async_computation | async-start | bytes 6291456 | tf_op jit(solution)/shard_map/all_to_all | solution.py:278
  47.0 14.5 %collective-permute-start.1 = (bf16[3,16,32,256]{3,2,1,0:T(8,128)(2,1)}, bf16[3,16,32,256]{3,2,1,0:T(8,128)(2,1)}, u32[]{:S(2)}, u32[]{:S(2)}) collective-permute-start(bf16[3,16,32,256]{3,2,1,0:T(8,128)(2,1)} %bitcast.column), channel_id=1, source_target_pairs={{0,2},{2,0},{1,3},{3,1},{4,6},{6,4},{5,7},{7,5},{8,10},{10,8},{9,1... | collective-permute-start | bytes 2359304 | tf_op jit(solution)/shard_map/ppermute | solution.py:43
  50.2 11.3 %collective-permute-start = (bf16[8,2048]{1,0:T(8,128)(2,1)S(1)}, bf16[8,2048]{1,0:T(8,128)(2,1)S(1)}, u32[]{:S(2)}, u32[]{:S(2)}) collective-permute-start(bf16[8,2048]{1,0:T(8,128)(2,1)S(1)} %pick.1.own), channel_id=1, source_target_pairs={{0,1},{1,0},{2,3},{3,2},{4,5},{5,4},{6,7},{7,6},{8,9},{9,8},{10,11... | collective-permute-start | bytes 98312 | tf_op jit(solution)/shard_map/ppermute | solution.py:43
  63.0 10.4 %collective-permute-start.2 = (f32[8,128]{1,0:T(8,128)S(1)}, f32[8,128]{1,0:T(8,128)S(1)}, u32[]{:S(2)}, u32[]{:S(2)}) collective-permute-start(f32[8,128]{1,0:T(8,128)S(1)} %get-tuple-element.32), channel_id=1, source_target_pairs={{0,1},{1,0},{2,3},{3,2},{4,5},{5,4},{6,7},{7,6},{8,9},{9,8},{10,11... | collective-permute-start | bytes 12296 | tf_op jit(solution)/shard_map/ppermute | solution.py:43
  73.4 32.5 %collective-permute-start.4 = (bf16[8,768,256]{2,1,0:T(8,128)(2,1)S(1)}, bf16[8,768,256]{2,1,0:T(8,128)(2,1)S(1)}, u32[]{:S(2)}, u32[]{:S(2)}) collective-permute-start(bf16[8,768,256]{2,1,0:T(8,128)(2,1)S(1)} %all-to-all-done.tokens), channel_id=1, source_target_pairs={{0,1},{1,0},{2,3},{3,2},{4,5},{5,4},{6,7},{7,6},{8,9},{9,8},{10,11... | collective-permute-start | bytes 9437192 | tf_op jit(solution)/shard_map/ppermute | solution.py:43
  77.1 28.9 %collective-permute-start.5 = (bf16[2,3,16,32,128]{4,3,2,1,0:T(8,128)(2,1)S(1)}, bf16[2,3,16,32,128]{4,3,2,1,0:T(8,128)(2,1)S(1)}, u32[]{:S(2)}, u32[]{:S(2)}) collective-permute-start(bf16[2,3,16,32,128]{4,3,2,1,0:T(8,128)(2,1)S(1)} %get-tuple-element.38), channel_id=1, source_target_pairs={{0,1},{1,0},{2,3},{3,2},{4,5},{5,4},{6,7},{7,6},{8,9},{9,8},{10,11... | collective-permute-start | bytes 2359304 | tf_op jit(solution)/shard_map/ppermute | solution.py:43
  102.0 9.0 %collective-permute-start.3 = (bf16[32,8,128]{2,1,0:T(8,128)(2,1)S(1)}, bf16[32,8,128]{2,1,0:T(8,128)(2,1)S(1)}, u32[]{:S(2)}, u32[]{:S(2)}) collective-permute-start(bf16[32,8,128]{2,1,0:T(8,128)(2,1)S(1)} %all_to_all.20.own), channel_id=1, source_target_pairs={{0,1},{1,0},{2,3},{3,2},{4,5},{5,4},{6,7},{7,6},{8,9},{9,8},{10,11... | collective-permute-start | bytes 196616 | tf_op jit(solution)/shard_map/ppermute | solution.py:43
  112.6 19.9 %all-to-all-start.2 = ((f32[32,8,128]{2,1,0:T(8,128)}), f32[32,8,128]{2,1,0:T(8,128)S(1)}, u32[]{:S(2)}, u32[]{:S(2)}) async-start(f32[32,8,128]{2,1,0:T(8,128)} %bitcast.1), calls=%async_computation.2 | async-start | bytes 262144 | tf_op jit(solution)/shard_map/all_to_all | solution.py:362
  133.5 16.4 %all-to-all-start.3 = ((bf16[32,8,128]{2,1,0:T(8,128)(2,1)}), bf16[32,8,128]{2,1,0:T(8,128)(2,1)S(1)}, u32[]{:S(2)}, u32[]{:S(2)}) async-start(bf16[32,8,128]{2,1,0:T(8,128)(2,1)} %mixed.1), calls=%async_computation.3 | async-start | bytes 131072 | tf_op jit(solution)/shard_map/all_to_all | solution.py:372
  150.2 5.5 %collective-permute-start.6 = (bf16[768,128]{1,0:T(8,128)(2,1)S(1)}, bf16[768,128]{1,0:T(8,128)(2,1)S(1)}, u32[]{:S(2)}, u32[]{:S(2)}) collective-permute-start(bf16[768,128]{1,0:T(8,128)(2,1)S(1)} %get-tuple-element.52), channel_id=1, source_target_pairs={{0,1},{1,0},{2,3},{3,2},{4,5},{5,4},{6,7},{7,6},{8,9},{9,8},{10,11... | collective-permute-start | bytes 589832 | tf_op jit(solution)/shard_map/ppermute | solution.py:43

commit v9 on v7

--- a/solution.py
+++ b/solution.py
@@ -97,14 +97,21 @@
     picked[...] = rows[...].astype(BF16)
 
 
-def partial_kernel(own, other, column, core, keep, give, w, sems):
+def partial_kernel(own, other, column, core, keep, give, packed, w, sems):
     xl, c = lax.axis_index("xl"), lax.axis_index("c")
+    cols = pl.ds(pl.multiple_of(c * 128, 128), 128)
+    packs = [
+        pltpu.make_async_copy(column.at[:, :, :, cols], packed.at[c], sems.at[2]),
+        pltpu.make_async_copy(core.at[:, :, :, cols], packed.at[1 - c], sems.at[3]),
+    ]
     run(
         [
             pltpu.make_async_copy(column.at[pl.ds(0, 2)], w.at[:, :, c], sems.at[0]),
             pltpu.make_async_copy(core.at[pl.ds(0, 2)], w.at[:, :, 1 - c], sems.at[1]),
         ]
     )
+    for copy in packs:
+        copy.start()
     rows = jnp.concatenate([own[...].astype(F32), other[...].astype(F32)], 0)
     low = lax.broadcasted_iota(jnp.int32, (16, 128), 1) < 64
     tiles = []
@@ -123,23 +130,14 @@
     chosen = jnp.where((number[:, :128] % 8) < 4, both[:, :128], both[:, 128:])
     keep[...] = chosen[:8]
     give[...] = chosen[8:]
+    for copy in packs:
+        copy.wait()
 
 
 def finish_kernel(keep, received, spread):
     chosen = (keep[...] + received[...]).astype(BF16)
     for place in range(spread.shape[0]):
         spread[place] = chosen
-
-
-def pack_kernel(column, core, packed, sems):
-    c = lax.axis_index("c")
-    cols = pl.ds(pl.multiple_of(c * 128, 128), 128)
-    run(
-        [
-            pltpu.make_async_copy(column.at[:, :, :, cols], packed.at[c], sems.at[0]),
-            pltpu.make_async_copy(core.at[:, :, :, cols], packed.at[1 - c], sems.at[1]),
-        ]
-    )
 
 
 def project_kernel(tokens, core_tokens, packed, across, query, keys, values, norms, w, sems):
@@ -271,16 +269,6 @@
     core = shift(column, "c", 1)
     core, later = lax.optimization_barrier((core, whole))
     core_tokens = shift(later, "c", 1)
-    packed = call(
-        pack_kernel,
-        "pack",
-        shape((2, 3, 16, 32, 128), BF16),
-        [ANY, ANY],
-        1 << 10,
-        3 << 19,
-        [pltpu.SemaphoreType.DMA((2,))],
-        space=HBM,
-    )(column, core)
     picked = call(
         pick_kernel,
         "pick",
@@ -295,22 +283,21 @@
         ],
     )(landmark_pos, whole)
     other_picked = shift(picked, "xl", 1)
-    keep, give = call(
+    keep, give, packed = call(
         partial_kernel,
         "partial",
-        (shape((8, 128), F32), shape((8, 128), F32)),
+        (shape((8, 128), F32), shape((8, 128), F32), shape((2, 3, 16, 32, 128), BF16)),
         [VMEM, VMEM, ANY, ANY],
-        2 * 16 * 1024 * 512,
+        1 << 36,
         1 << 20,
-        [pltpu.VMEM((2, 16, 2, 32, 256), BF16), pltpu.SemaphoreType.DMA((2,))],
+        [pltpu.VMEM((2, 16, 2, 32, 256), BF16), pltpu.SemaphoreType.DMA((4,))],
     )(picked, other_picked, column, core)
     received = shift(give, "xl", 1)
+    across = shift(packed, "xl", 1)
     spread = call(
-        finish_kernel, "finish", shape((32, 8, 128), BF16), [VMEM] * 2, 1 << 14, 1 << 16
+        finish_kernel, "finish", shape((32, 8, 128), BF16), [VMEM] * 2, 1 << 34, 1 << 16
     )(keep, received)
-    spread, packed = lax.optimization_barrier((spread, packed))
     own_marks = lax.all_to_all(spread, CORES, 0, 0, tiled=True)
-    across = shift(packed, "xl", 1)
     query, keys, values, norms = call(
         project_kernel,
         "project",

time: 151 us -> 148 us (0.980)
  waiting for transfers between devices: 27.8 us -> 22.4 us
  Pallas kernels: 14.9 us -> 16.8 us
  blocking collectives: 59.9 us -> 61.8 us
  local copies, waits for them, and re-layouts: 4.63 us -> 2.85 us
    ppermute x7, waiting for transfers between devices: 6.17 us -> 1.01 us  [shift(): lax.ppermute(value, axis, [(i, (i + step) % size) for i in range(size)])]
    pallas_call x1, Pallas kernels: 0.41 us -> 2.38 us  [shards(): call(partial_kernel, 'partial', (shape((8, 128), F32), shape((8, 128), F3...]
    all_gather x1, blocking collectives: 34.6 us -> 36.6 us  [shards(): lax.all_gather(weights, 'z', axis=1, tiled=True).reshape(3, 16, 32, 256)]
    unnamed x12 -> x4, local copies, waits for them, and re-layouts: 1.79 us -> 0.01 us
  transfers between devices with their start and end apart: 10 -> 10, of which waited for: 6 -> 4; matrix products, arithmetic and copies ran while one was open for 0% -> 0% of each run, Pallas kernels for 7% -> 9%
where the time goes in v9:
time: 148 us; the launch traced here: 147 us
  blocking collectives  61.8 us (42%)
  starting transfers between devices  43.1 us (29%)
  waiting for transfers between devices  22.4 us (15%)
  Pallas kernels  16.8 us (11%)
  local copies, waits for them, and re-layouts  2.85 us (2%)
    all_gather x1, blocking collectives, shards(): lax.all_gather(weights, 'z', axis=1, tiled=True).reshape(3, 16, 32, 256)  36.6 us
    ppermute x7, starting transfers between devices, shift(): lax.ppermute(value, axis, [(i, (i + step) % size) for i in range(size)])  26.1 us
    all_to_all x1, blocking collectives, shards(): own_marks = lax.all_to_all(spread, CORES, 0, 0, tiled=True)  25.2 us
    all_to_all x1, waiting for transfers between devices, shards(): spread = lax.all_to_all(spread, CHIPS, 0, 0, tiled=True)  11.8 us
    all_to_all x1, waiting for transfers between devices, shards(): pieces = lax.all_to_all(chip.reshape(32, 8, 128), CHIPS, 0, 0, tiled=True)  9.63 us
    all_to_all x1, starting transfers between devices, shards(): lax.all_to_all(jnp.broadcast_to(tokens[None], (8,) + tokens.shape), HEAD,...  7.61 us
    all_to_all x1, starting transfers between devices, shards(): spread = lax.all_to_all(spread, CHIPS, 0, 0, tiled=True)  5.44 us
    pallas_call x1, Pallas kernels, shards(): call(project_kernel, 'project', (shape((1536, 128), BF16), shape((1536, 1...  5 us
  transfers between devices with their start and end apart: 10, of which 4 were waited for; matrix products, arithmetic and copies ran while one was open for 0% of the time, Pallas kernels for 9%

profile of v9, /device:TPU:1, one launch (start us, length us, event | category | flops | bytes accessed | tf_op | source)
XLA Modules:
  0.0 147.2 jit_solution(4283150742540430484)
XLA Ops:
  0.0 2.8 %broadcast_in_dim.2 = bf16[8,768,256]{2,1,0:T(8,128)(2,1)} broadcast(bf16[768,256]{1,0:T(8,128)(2,1)} %param.3), dimensions={1,2} | broadcast | bytes 3538944 | tf_op jit(solution)/shard_map/broadcast_in_dim | solution.py:266
  2.8 7.6 %all-to-all-start = ((bf16[8,768,256]{2,1,0:T(8,128)(2,1)}), bf16[8,768,256]{2,1,0:T(8,128)(2,1)S(1)}, u32[]{:S(2)}, u32[]{:S(2)}) async-start(bf16[8,768,256]{2,1,0:T(8,128)(2,1)} %broadcast_in_dim.2), calls=%async_computation | async-start | bytes 6291456 | tf_op jit(solution)/shard_map/all_to_all | solution.py:265
  10.5 36.6 %all_gather.3 = bf16[3,512,256]{2,1,0:T(8,128)(2,1)} all-gather(bf16[3,32,256]{2,1,0:T(8,128)(2,1)S(1)} %copy-done.1), channel_id=1, replica_groups=mesh['y'=4,'xh'=2,'z'=16,'xl'=2,'c'=2] {'z'}, dimensions={1}, use_global_device_ids=true | all-gather | bytes 835584 | tf_op jit(solution)/shard_map/all_gather | solution.py:268
  47.0 8.7 %collective-permute-start.1 = (bf16[3,16,32,256]{3,2,1,0:T(8,128)(2,1)}, bf16[3,16,32,256]{3,2,1,0:T(8,128)(2,1)}, u32[]{:S(2)}, u32[]{:S(2)}) collective-permute-start(bf16[3,16,32,256]{3,2,1,0:T(8,128)(2,1)} %bitcast.column), channel_id=1, source_target_pairs={{0,1},{1,0},{2,3},{3,2},{4,5},{5,4},{6,7},{7,6},{8,9},{9,8},{10,11... | collective-permute-start | bytes 2359304 | tf_op jit(solution)/shard_map/ppermute | solution.py:44
  55.7 0.0 all-to-all-done.tokens
  55.7 1.0 pick.1.own
  56.7 2.2 %collective-permute-start = (bf16[8,2048]{1,0:T(8,128)(2,1)S(1)}, bf16[8,2048]{1,0:T(8,128)(2,1)S(1)}, u32[]{:S(2)}, u32[]{:S(2)}) collective-permute-start(bf16[8,2048]{1,0:T(8,128)(2,1)S(1)} %pick.1.own), channel_id=1, source_target_pairs={{0,2},{2,0},{1,3},{3,1},{4,6},{6,4},{5,7},{7,5},{8,10},{10,8},{9,1... | collective-permute-start | bytes 98312 | tf_op jit(solution)/shard_map/ppermute | solution.py:44
  58.9 0.0 collective-permute-done.1.core
  58.9 2.2 %collective-permute-start.4 = (bf16[8,768,256]{2,1,0:T(8,128)(2,1)S(1)}, bf16[8,768,256]{2,1,0:T(8,128)(2,1)S(1)}, u32[]{:S(2)}, u32[]{:S(2)}) collective-permute-start(bf16[8,768,256]{2,1,0:T(8,128)(2,1)S(1)} %all-to-all-done.tokens), channel_id=1, source_target_pairs={{0,1},{1,0},{2,3},{3,2},{4,5},{5,4},{6,7},{7,6},{8,9},{9,8},{10,11... | collective-permute-start | bytes 9437192 | tf_op jit(solution)/shard_map/ppermute | solution.py:44
  61.1 0.2 collective-permute-done.other
  61.3 2.4 %partial.1 = (f32[8,128]{1,0:T(8,128)S(1)}, f32[8,128]{1,0:T(8,128)S(1)}, bf16[2,3,16,32,128]{4,3,2,1,0:T(8,128)(2,1)S(1)}) custom-call(bf16[8,2048]{1,0:T(8,128)(2,1)S(1)} %pick.1.own, bf16[8,2048]{1,0:T(8,128)(2,1)S(1)} %collective-permute-done.other, bf16[3,16,32,256]{3,2,1,0:T(8,128)(2,1)} %bitcast.column, ...), custom_call_target="tpu_custom_call" | custom-call | flops 68719476736 | bytes 1048576 | tf_op jit(solution)/shard_map/partial/pallas_call | solution.py:286
  63.7 2.9 %collective-permute-start.2 = (f32[8,128]{1,0:T(8,128)S(1)}, f32[8,128]{1,0:T(8,128)S(1)}, u32[]{:S(2)}, u32[]{:S(2)}) collective-permute-start(f32[8,128]{1,0:T(8,128)S(1)} %get-tuple-element.26), channel_id=1, source_target_pairs={{0,2},{2,0},{1,3},{3,1},{4,6},{6,4},{5,7},{7,5},{8,10},{10,8},{9,1... | collective-permute-start | bytes 12296 | tf_op jit(solution)/shard_map/ppermute | solution.py:44
  66.6 2.4 %collective-permute-start.5 = (bf16[2,3,16,32,128]{4,3,2,1,0:T(8,128)(2,1)S(1)}, bf16[2,3,16,32,128]{4,3,2,1,0:T(8,128)(2,1)S(1)}, u32[]{:S(2)}, u32[]{:S(2)}) collective-permute-start(bf16[2,3,16,32,128]{4,3,2,1,0:T(8,128)(2,1)S(1)} %get-tuple-element.28.packed), channel_id=1, source_target_pairs={{0,2},{2,0},{1,3},{3,1},{4,6},{6,4},{5,7},{7,5},{8,10},{10,8},{9,1... | collective-permute-start | bytes 2359304 | tf_op jit(solution)/shard_map/ppermute | solution.py:44
  69.0 0.0 collective-permute-done.2.received
  69.1 25.2 %all_to_all.20.own = bf16[32,8,128]{2,1,0:T(8,128)(2,1)S(1)} all-to-all(bf16[32,8,128]{2,1,0:T(8,128)(2,1)S(1)} %finish.1), channel_id=1, replica_groups=mesh['y'=4,'xh'=2,'z'=16,'xl'=2,'c'=2] {'z','c'}, dimensions={0} | all-to-all | bytes 131072 | tf_op jit(solution)/shard_map/all_to_all | solution.py:300
  94.3 2.2 %collective-permute-start.3 = (bf16[32,8,128]{2,1,0:T(8,128)(2,1)S(1)}, bf16[32,8,128]{2,1,0:T(8,128)(2,1)S(1)}, u32[]{:S(2)}, u32[]{:S(2)}) collective-permute-start(bf16[32,8,128]{2,1,0:T(8,128)(2,1)S(1)} %all_to_all.20.own), channel_id=1, source_target_pairs={{0,2},{2,0},{1,3},{3,1},{4,6},{6,4},{5,7},{7,5},{8,10},{10,8},{9,1... | collective-permute-start | bytes 196616 | tf_op jit(solution)/shard_map/ppermute | solution.py:44
  96.5 0.0 collective-permute-done.5.across
  96.5 0.0 collective-permute-done.4.core_tokens
  96.5 5.0 %project.1 = (bf16[1536,128]{1,0:T(8,128)(2,1)S(1)}, bf16[1536,128]{1,0:T(8,128)(2,1)S(1)}, bf16[1536,128]{1,0:T(8,128)(2,1)S(1)}, f32[1536,1]{1,0:T(8,128)S(1)}) custom-call(bf16[8,768,256]{2,1,0:T(8,128)(2,1)S(1)} %all-to-all-done.tokens, bf16[8,768,256]{2,1,0:T(8,128)(2,1)S(1)} %collective-permute-done.4.core_tokens, ...), custom_call_target="tpu_custom_call" | custom-call | flops 2415919104 | bytes 8388608 | tf_op jit(solution)/shard_map/project/pallas_call | solution.py:301
  101.5 1.7 %summary.1 = (bf16[256,128]{1,0:T(8,128)(2,1)S(1)}, f32[256,128]{1,0:T(8,128)}) custom-call(bf16[32,8,128]{2,1,0:T(8,128)(2,1)S(1)} %all_to_all.20.own, bf16[32,8,128]{2,1,0:T(8,128)(2,1)S(1)} %collective-permute-done.3.other, bf16[1536,128]{1,0:T(8,128)(2,1)S(1)} %get-tuple-element.29.keys, bf16[1536,128]{1,0:T(8,128)(2,1)S(1)} %get-tuple-element.30.values, ...), custom_call_target="tpu_custom_call" | custom-call | flops 201326592 | bytes 2097152 | tf_op jit(solution)/shard_map/summary/pallas_call | solution.py:317
  103.2 4.0 %all-to-all-start.2 = ((f32[32,8,128]{2,1,0:T(8,128)}), f32[32,8,128]{2,1,0:T(8,128)S(1)}, u32[]{:S(2)}, u32[]{:S(2)}) async-start(f32[32,8,128]{2,1,0:T(8,128)} %bitcast.1), calls=%async_computation.2 | async-start | bytes 262144 | tf_op jit(solution)/shard_map/all_to_all | solution.py:338
  107.2 3.6 %inverse.1 = f32[256,256]{1,0:T(8,128)S(1)} custom-call(bf16[256,128]{1,0:T(8,128)(2,1)S(1)} %get-tuple-element.38.marks_ref.marks), custom_call_target="tpu_custom_call" | custom-call | flops 2415919104 | bytes 524288 | tf_op jit(solution)/shard_map/inverse/pallas_call | solution.py:328
  110.8 9.6 %all-to-all-done.2.pieces = f32[32,8,128]{2,1,0:T(8,128)S(1)} async-done(((f32[32,8,128]{2,1,0:T(8,128)}), f32[32,8,128]{2,1,0:T(8,128)S(1)}, u32[]{:S(2)}, u32[]{:S(2)}) %all-to-all-start.2) | async-done | bytes 131104 | tf_op jit(solution)/shard_map/all_to_all | solution.py:338
  120.5 1.0 mixed.1
  121.4 5.4 %all-to-all-start.3 = ((bf16[32,8,128]{2,1,0:T(8,128)(2,1)}), bf16[32,8,128]{2,1,0:T(8,128)(2,1)S(1)}, u32[]{:S(2)}, u32[]{:S(2)}) async-start(bf16[32,8,128]{2,1,0:T(8,128)(2,1)} %mixed.1), calls=%async_computation.3 | async-start | bytes 131072 | tf_op jit(solution)/shard_map/all_to_all | solution.py:348
  126.9 0.8 query_weights.1.weights
  127.7 11.8 %all-to-all-done.3.spread = bf16[32,8,128]{2,1,0:T(8,128)(2,1)S(1)} async-done(((bf16[32,8,128]{2,1,0:T(8,128)(2,1)}), bf16[32,8,128]{2,1,0:T(8,128)(2,1)S(1)}, u32[]{:S(2)}, u32[]{:S(2)}) %all-to-all-start.3) | async-done | bytes 65568 | tf_op jit(solution)/shard_map/all_to_all | solution.py:348
  139.5 0.3 give.1
  139.7 5.5 %collective-permute-start.6 = (bf16[768,128]{1,0:T(8,128)(2,1)S(1)}, bf16[768,128]{1,0:T(8,128)(2,1)S(1)}, u32[]{:S(2)}, u32[]{:S(2)}) collective-permute-start(bf16[768,128]{1,0:T(8,128)(2,1)S(1)} %get-tuple-element.42), channel_id=1, source_target_pairs={{0,1},{1,0},{2,3},{3,2},{4,5},{5,4},{6,7},{7,6},{8,9},{9,8},{10,11... | collective-permute-start | bytes 589832 | tf_op jit(solution)/shard_map/ppermute | solution.py:44
  145.3 0.3 keep.1
  145.5 0.8 collective-permute-done.6.received
  146.3 0.9 join.1
  (6 shorter events, 0.0 us)
Async XLA Ops:
  2.8 7.6 %copy-start.1 = (bf16[3,32,256]{2,1,0:T(8,128)(2,1)S(1)}, bf16[3,32,256]{2,1,0:T(8,128)(2,1)}, u32[]{:S(2)}) copy-start(bf16[3,32,256]{2,1,0:T(8,128)(2,1)} %param.4) | copy-start | bytes 147460
  2.8 52.9 %copy-start = (s32[2,256]{1,0:T(2,128)S(1)}, s32[2,256]{1,0:T(2,128)}, u32[]{:S(2)}) copy-start(s32[2,256]{1,0:T(2,128)} %pos_ref.1) | copy-start | bytes 6148
  2.8 52.9 %all-to-all-start = ((bf16[8,768,256]{2,1,0:T(8,128)(2,1)}), bf16[8,768,256]{2,1,0:T(8,128)(2,1)S(1)}, u32[]{:S(2)}, u32[]{:S(2)}) async-start(bf16[8,768,256]{2,1,0:T(8,128)(2,1)} %broadcast_in_dim.2), calls=%async_computation | async-start | bytes 6291456 | tf_op jit(solution)/shard_map/all_to_all | solution.py:265
  47.0 11.9 %collective-permute-start.1 = (bf16[3,16,32,256]{3,2,1,0:T(8,128)(2,1)}, bf16[3,16,32,256]{3,2,1,0:T(8,128)(2,1)}, u32[]{:S(2)}, u32[]{:S(2)}) collective-permute-start(bf16[3,16,32,256]{3,2,1,0:T(8,128)(2,1)} %bitcast.column), channel_id=1, source_target_pairs={{0,1},{1,0},{2,3},{3,2},{4,5},{5,4},{6,7},{7,6},{8,9},{9,8},{10,11... | collective-permute-start | bytes 2359304 | tf_op jit(solution)/shard_map/ppermute | solution.py:44
  56.7 4.7 %collective-permute-start = (bf16[8,2048]{1,0:T(8,128)(2,1)S(1)}, bf16[8,2048]{1,0:T(8,128)(2,1)S(1)}, u32[]{:S(2)}, u32[]{:S(2)}) collective-permute-start(bf16[8,2048]{1,0:T(8,128)(2,1)S(1)} %pick.1.own), channel_id=1, source_target_pairs={{0,2},{2,0},{1,3},{3,1},{4,6},{6,4},{5,7},{7,5},{8,10},{10,8},{9,1... | collective-permute-start | bytes 98312 | tf_op jit(solution)/shard_map/ppermute | solution.py:44
  58.9 37.6 %collective-permute-start.4 = (bf16[8,768,256]{2,1,0:T(8,128)(2,1)S(1)}, bf16[8,768,256]{2,1,0:T(8,128)(2,1)S(1)}, u32[]{:S(2)}, u32[]{:S(2)}) collective-permute-start(bf16[8,768,256]{2,1,0:T(8,128)(2,1)S(1)} %all-to-all-done.tokens), channel_id=1, source_target_pairs={{0,1},{1,0},{2,3},{3,2},{4,5},{5,4},{6,7},{7,6},{8,9},{9,8},{10,11... | collective-permute-start | bytes 9437192 | tf_op jit(solution)/shard_map/ppermute | solution.py:44
  63.7 5.3 %collective-permute-start.2 = (f32[8,128]{1,0:T(8,128)S(1)}, f32[8,128]{1,0:T(8,128)S(1)}, u32[]{:S(2)}, u32[]{:S(2)}) collective-permute-start(f32[8,128]{1,0:T(8,128)S(1)} %get-tuple-element.26), channel_id=1, source_target_pairs={{0,2},{2,0},{1,3},{3,1},{4,6},{6,4},{5,7},{7,5},{8,10},{10,8},{9,1... | collective-permute-start | bytes 12296 | tf_op jit(solution)/shard_map/ppermute | solution.py:44
  66.6 29.9 %collective-permute-start.5 = (bf16[2,3,16,32,128]{4,3,2,1,0:T(8,128)(2,1)S(1)}, bf16[2,3,16,32,128]{4,3,2,1,0:T(8,128)(2,1)S(1)}, u32[]{:S(2)}, u32[]{:S(2)}) collective-permute-start(bf16[2,3,16,32,128]{4,3,2,1,0:T(8,128)(2,1)S(1)} %get-tuple-element.28.packed), channel_id=1, source_target_pairs={{0,2},{2,0},{1,3},{3,1},{4,6},{6,4},{5,7},{7,5},{8,10},{10,8},{9,1... | collective-permute-start | bytes 2359304 | tf_op jit(solution)/shard_map/ppermute | solution.py:44
  94.3 7.3 %collective-permute-start.3 = (bf16[32,8,128]{2,1,0:T(8,128)(2,1)S(1)}, bf16[32,8,128]{2,1,0:T(8,128)(2,1)S(1)}, u32[]{:S(2)}, u32[]{:S(2)}) collective-permute-start(bf16[32,8,128]{2,1,0:T(8,128)(2,1)S(1)} %all_to_all.20.own), channel_id=1, source_target_pairs={{0,2},{2,0},{1,3},{3,1},{4,6},{6,4},{5,7},{7,5},{8,10},{10,8},{9,1... | collective-permute-start | bytes 196616 | tf_op jit(solution)/shard_map/ppermute | solution.py:44
  103.2 17.2 %all-to-all-start.2 = ((f32[32,8,128]{2,1,0:T(8,128)}), f32[32,8,128]{2,1,0:T(8,128)S(1)}, u32[]{:S(2)}, u32[]{:S(2)}) async-start(f32[32,8,128]{2,1,0:T(8,128)} %bitcast.1), calls=%async_computation.2 | async-start | bytes 262144 | tf_op jit(solution)/shard_map/all_to_all | solution.py:338
  121.4 18.0 %all-to-all-start.3 = ((bf16[32,8,128]{2,1,0:T(8,128)(2,1)}), bf16[32,8,128]{2,1,0:T(8,128)(2,1)S(1)}, u32[]{:S(2)}, u32[]{:S(2)}) async-start(bf16[32,8,128]{2,1,0:T(8,128)(2,1)} %mixed.1), calls=%async_computation.3 | async-start | bytes 131072 | tf_op jit(solution)/shard_map/all_to_all | solution.py:348
  139.7 6.6 %collective-permute-start.6 = (bf16[768,128]{1,0:T(8,128)(2,1)S(1)}, bf16[768,128]{1,0:T(8,128)(2,1)S(1)}, u32[]{:S(2)}, u32[]{:S(2)}) collective-permute-start(bf16[768,128]{1,0:T(8,128)(2,1)S(1)} %get-tuple-element.42), channel_id=1, source_target_pairs={{0,1},{1,0},{2,3},{3,2},{4,5},{5,4},{6,7},{7,6},{8,9},{9,8},{10,11... | collective-permute-start | bytes 589832 | tf_op jit(solution)/shard_map/ppermute | solution.py:44

commit v10 on v9

--- a/solution.py
+++ b/solution.py
@@ -71,6 +71,10 @@
         copy.start()
     for copy in copies:
         copy.wait()
+
+
+def stage_kernel(source, target, sems):
+    run([pltpu.make_async_copy(source.at[i], target.at[i], sems.at[i]) for i in range(3)])
 
 
 def pick_kernel(pos_ref, tokens, picked, groups, rows, sems):
@@ -97,21 +101,21 @@
     picked[...] = rows[...].astype(BF16)
 
 
-def partial_kernel(own, other, column, core, keep, give, packed, w, sems):
-    xl, c = lax.axis_index("xl"), lax.axis_index("c")
+def prepare_kernel(column, core, w, packed, sems):
+    c = lax.axis_index("c")
     cols = pl.ds(pl.multiple_of(c * 128, 128), 128)
-    packs = [
-        pltpu.make_async_copy(column.at[:, :, :, cols], packed.at[c], sems.at[2]),
-        pltpu.make_async_copy(core.at[:, :, :, cols], packed.at[1 - c], sems.at[3]),
-    ]
     run(
         [
             pltpu.make_async_copy(column.at[pl.ds(0, 2)], w.at[:, :, c], sems.at[0]),
             pltpu.make_async_copy(core.at[pl.ds(0, 2)], w.at[:, :, 1 - c], sems.at[1]),
+            pltpu.make_async_copy(column.at[:, :, :, cols], packed.at[c], sems.at[2]),
+            pltpu.make_async_copy(core.at[:, :, :, cols], packed.at[1 - c], sems.at[3]),
         ]
     )
-    for copy in packs:
-        copy.start()
+
+
+def partial_kernel(own, other, w, keep, give):
+    xl = lax.axis_index("xl")
     rows = jnp.concatenate([own[...].astype(F32), other[...].astype(F32)], 0)
     low = lax.broadcasted_iota(jnp.int32, (16, 128), 1) < 64
     tiles = []
@@ -130,8 +134,6 @@
     chosen = jnp.where((number[:, :128] % 8) < 4, both[:, :128], both[:, 128:])
     keep[...] = chosen[:8]
     give[...] = chosen[8:]
-    for copy in packs:
-        copy.wait()
 
 
 def finish_kernel(keep, received, spread):
@@ -261,14 +263,39 @@
     return jax.ShapeDtypeStruct(dims, dtype)
 
 
+def in_hbm(*values):
+    return tuple(pltpu.with_memory_space_constraint(value, pltpu.HBM) for value in values)
+
+
 def shards(tokens, weights, landmark_pos):
     whole = lax.all_to_all(
         jnp.broadcast_to(tokens[None], (8,) + tokens.shape), HEAD, 0, 0, tiled=True
     )
     column = lax.all_gather(weights, "z", axis=1, tiled=True).reshape(3, 16, 32, 256)
+    column = call(
+        stage_kernel,
+        "stage",
+        shape((3, 16, 32, 256), BF16),
+        [VMEM],
+        1 << 10,
+        3 << 19,
+        [pltpu.SemaphoreType.DMA((3,))],
+        space=HBM,
+    )(column)
     core = shift(column, "c", 1)
+    column, core = in_hbm(column, core)
     core, later = lax.optimization_barrier((core, whole))
     core_tokens = shift(later, "c", 1)
+    wide, packed = call(
+        prepare_kernel,
+        "prepare",
+        (shape((2, 16, 2, 32, 256), BF16), shape((2, 3, 16, 32, 128), BF16)),
+        [ANY, ANY],
+        1 << 10,
+        3 << 20,
+        [pltpu.SemaphoreType.DMA((4,))],
+    )(column, core)
+    landmark_pos, wide = lax.optimization_barrier((landmark_pos, wide))
     picked = call(
         pick_kernel,
         "pick",
@@ -283,15 +310,15 @@
         ],
     )(landmark_pos, whole)
     other_picked = shift(picked, "xl", 1)
-    keep, give, packed = call(
+    keep, give = call(
         partial_kernel,
         "partial",
-        (shape((8, 128), F32), shape((8, 128), F32), shape((2, 3, 16, 32, 128), BF16)),
-        [VMEM, VMEM, ANY, ANY],
+        (shape((8, 128), F32), shape((8, 128), F32)),
+        [VMEM, VMEM, VMEM],
         1 << 36,
         1 << 20,
-        [pltpu.VMEM((2, 16, 2, 32, 256), BF16), pltpu.SemaphoreType.DMA((4,))],
-    )(picked, other_picked, column, core)
+    )(picked, other_picked, wide)
+    packed, give = lax.optimization_barrier((packed, give))
     received = shift(give, "xl", 1)
     across = shift(packed, "xl", 1)
     spread = call(

time: 148 us -> 147 us (level)
  blocking collectives: 61.8 us -> 59.9 us
  waiting for transfers between devices: 22.4 us -> 24.2 us
    pallas_call x1, Pallas kernels: 2.38 us -> 0.28 us  [shards(): call(partial_kernel, 'partial', (shape((8, 128), F32), shape((8, 128), F3...]
    all_gather x1, blocking collectives: 36.6 us -> 34.6 us  [shards(): lax.all_gather(weights, 'z', axis=1, tiled=True).reshape(3, 16, 32, 256)]
    ppermute x7, waiting for transfers between devices: 1.01 us -> 2.82 us  [shift(): lax.ppermute(value, axis, [(i, (i + step) % size) for i in range(size)])]
    pallas_call x0 -> x2, Pallas kernels: none -> 1.55 us  [the longest x1 1.46 us: shards(): call(prepare_kernel, 'prepare', (shape((2, 16, 2, 32, 256), BF16), shape(...]
  transfers between devices with their start and end apart: 10 -> 10, of which waited for: 4 -> 4; matrix products, arithmetic and copies ran while one was open for 0% -> 0% of each run, Pallas kernels for 9% -> 7%
where the time goes in v10:
time: 147 us
  blocking collectives  59.9 us (41%)
  starting transfers between devices  43.2 us (29%)
  waiting for transfers between devices  24.2 us (16%)
  Pallas kernels  16.2 us (11%)
  local copies, waits for them, and re-layouts  2.87 us (2%)
    all_gather x1, blocking collectives, shards(): lax.all_gather(weights, 'z', axis=1, tiled=True).reshape(3, 16, 32, 256)  34.6 us
    ppermute x7, starting transfers between devices, shift(): lax.ppermute(value, axis, [(i, (i + step) % size) for i in range(size)])  26.1 us
    all_to_all x1, blocking collectives, shards(): own_marks = lax.all_to_all(spread, CORES, 0, 0, tiled=True)  25.2 us
    all_to_all x1, waiting for transfers between devices, shards(): spread = lax.all_to_all(spread, CHIPS, 0, 0, tiled=True)  11.8 us
    all_to_all x1, waiting for transfers between devices, shards(): pieces = lax.all_to_all(chip.reshape(32, 8, 128), CHIPS, 0, 0, tiled=True)  9.63 us
    all_to_all x1, starting transfers between devices, shards(): lax.all_to_all(jnp.broadcast_to(tokens[None], (8,) + tokens.shape), HEAD,...  7.61 us
    all_to_all x1, starting transfers between devices, shards(): spread = lax.all_to_all(spread, CHIPS, 0, 0, tiled=True)  5.44 us
    pallas_call x1, Pallas kernels, shards(): call(project_kernel, 'project', (shape((1536, 128), BF16), shape((1536, 1...  5 us
  transfers between devices with their start and end apart: 10, of which 4 were waited for; matrix products, arithmetic and copies ran while one was open for 0% of the time, Pallas kernels for 7%

profile of v10, /device:TPU:1, one launch (start us, length us, event | category | flops | bytes accessed | tf_op | source)
XLA Modules:
  0.0 146.5 jit_solution(10045782415837776444)
XLA Ops:
  0.0 2.9 %broadcast_in_dim.2 = bf16[8,768,256]{2,1,0:T(8,128)(2,1)} broadcast(bf16[768,256]{1,0:T(8,128)(2,1)} %param.3), dimensions={1,2} | broadcast | bytes 3538944 | tf_op jit(solution)/shard_map/broadcast_in_dim | solution.py:272
  2.9 7.6 %all-to-all-start = ((bf16[8,768,256]{2,1,0:T(8,128)(2,1)}), bf16[8,768,256]{2,1,0:T(8,128)(2,1)S(1)}, u32[]{:S(2)}, u32[]{:S(2)}) async-start(bf16[8,768,256]{2,1,0:T(8,128)(2,1)} %broadcast_in_dim.2), calls=%async_computation | async-start | bytes 6291456 | tf_op jit(solution)/shard_map/all_to_all | solution.py:271
  10.5 0.0 copy-start.1
  10.5 34.6 %all_gather.3 = bf16[3,512,256]{2,1,0:T(8,128)(2,1)S(1)} all-gather(bf16[3,32,256]{2,1,0:T(8,128)(2,1)S(1)} %copy-done.2), channel_id=1, replica_groups=mesh['y'=4,'xh'=2,'z'=16,'xl'=2,'c'=2] {'z'}, dimensions={1}, use_global_device_ids=true | all-gather | bytes 835584 | tf_op jit(solution)/shard_map/all_gather | solution.py:274
  45.1 0.1 stage.1.column
  45.2 8.3 %collective-permute-start = (bf16[3,16,32,256]{3,2,1,0:T(8,128)(2,1)S(1)}, bf16[3,16,32,256]{3,2,1,0:T(8,128)(2,1)}, u32[]{:S(2)}, u32[]{:S(2)}) collective-permute-start(bf16[3,16,32,256]{3,2,1,0:T(8,128)(2,1)S(1)} %stage.1.column), channel_id=1, source_target_pairs={{0,1},{1,0},{2,3},{3,2},{4,5},{5,4},{6,7},{7,6},{8,9},{9,8},{10,11... | collective-permute-start | bytes 2359304 | tf_op jit(solution)/shard_map/ppermute | solution.py:44
  53.5 2.0 %collective-permute-done.core = bf16[3,16,32,256]{3,2,1,0:T(8,128)(2,1)} collective-permute-done((bf16[3,16,32,256]{3,2,1,0:T(8,128)(2,1)S(1)}, bf16[3,16,32,256]{3,2,1,0:T(8,128)(2,1)}, u32[]{:S(2)}, u32[]{:S(2)}) %collective-permute-start) | collective-permute-done | bytes 786464 | tf_op jit(solution)/shard_map/ppermute | solution.py:44
  55.6 1.5 prepare.1
  57.0 1.0 pick.1.own
  58.0 2.2 %collective-permute-start.1 = (bf16[8,2048]{1,0:T(8,128)(2,1)S(1)}, bf16[8,2048]{1,0:T(8,128)(2,1)S(1)}, u32[]{:S(2)}, u32[]{:S(2)}) collective-permute-start(bf16[8,2048]{1,0:T(8,128)(2,1)S(1)} %pick.1.own), channel_id=1, source_target_pairs={{0,2},{2,0},{1,3},{3,1},{4,6},{6,4},{5,7},{7,5},{8,10},{10,8},{9,1... | collective-permute-start | bytes 98312 | tf_op jit(solution)/shard_map/ppermute | solution.py:44
  60.2 2.6 %collective-permute-start.4 = (bf16[8,768,256]{2,1,0:T(8,128)(2,1)S(1)}, bf16[8,768,256]{2,1,0:T(8,128)(2,1)S(1)}, u32[]{:S(2)}, u32[]{:S(2)}) collective-permute-start(bf16[8,768,256]{2,1,0:T(8,128)(2,1)S(1)} %all-to-all-done.tokens), channel_id=1, source_target_pairs={{0,1},{1,0},{2,3},{3,2},{4,5},{5,4},{6,7},{7,6},{8,9},{9,8},{10,11... | collective-permute-start | bytes 9437192 | tf_op jit(solution)/shard_map/ppermute | solution.py:44
  62.8 0.0 collective-permute-done.1.other
  62.8 0.3 partial.1
  63.1 3.1 %collective-permute-start.2 = (f32[8,128]{1,0:T(8,128)S(1)}, f32[8,128]{1,0:T(8,128)S(1)}, u32[]{:S(2)}, u32[]{:S(2)}) collective-permute-start(f32[8,128]{1,0:T(8,128)S(1)} %get-tuple-element.36), channel_id=1, source_target_pairs={{0,2},{2,0},{1,3},{3,1},{4,6},{6,4},{5,7},{7,5},{8,10},{10,8},{9,1... | collective-permute-start | bytes 12296 | tf_op jit(solution)/shard_map/ppermute | solution.py:44
  66.2 2.2 %collective-permute-start.5 = (bf16[2,3,16,32,128]{4,3,2,1,0:T(8,128)(2,1)S(1)}, bf16[2,3,16,32,128]{4,3,2,1,0:T(8,128)(2,1)S(1)}, u32[]{:S(2)}, u32[]{:S(2)}) collective-permute-start(bf16[2,3,16,32,128]{4,3,2,1,0:T(8,128)(2,1)S(1)} %get-tuple-element.38.packed), channel_id=1, source_target_pairs={{0,2},{2,0},{1,3},{3,1},{4,6},{6,4},{5,7},{7,5},{8,10},{10,8},{9,1... | collective-permute-start | bytes 2359304 | tf_op jit(solution)/shard_map/ppermute | solution.py:44
  68.4 0.0 collective-permute-done.2.received
  68.4 25.2 %all_to_all.20.own = bf16[32,8,128]{2,1,0:T(8,128)(2,1)S(1)} all-to-all(bf16[32,8,128]{2,1,0:T(8,128)(2,1)S(1)} %finish.1), channel_id=1, replica_groups=mesh['y'=4,'xh'=2,'z'=16,'xl'=2,'c'=2] {'z','c'}, dimensions={0} | all-to-all | bytes 131072 | tf_op jit(solution)/shard_map/all_to_all | solution.py:327
  93.7 2.2 %collective-permute-start.3 = (bf16[32,8,128]{2,1,0:T(8,128)(2,1)S(1)}, bf16[32,8,128]{2,1,0:T(8,128)(2,1)S(1)}, u32[]{:S(2)}, u32[]{:S(2)}) collective-permute-start(bf16[32,8,128]{2,1,0:T(8,128)(2,1)S(1)} %all_to_all.20.own), channel_id=1, source_target_pairs={{0,2},{2,0},{1,3},{3,1},{4,6},{6,4},{5,7},{7,5},{8,10},{10,8},{9,1... | collective-permute-start | bytes 196616 | tf_op jit(solution)/shard_map/ppermute | solution.py:44
  95.9 5.0 %project.1 = (bf16[1536,128]{1,0:T(8,128)(2,1)S(1)}, bf16[1536,128]{1,0:T(8,128)(2,1)S(1)}, bf16[1536,128]{1,0:T(8,128)(2,1)S(1)}, f32[1536,1]{1,0:T(8,128)S(1)}) custom-call(bf16[8,768,256]{2,1,0:T(8,128)(2,1)S(1)} %all-to-all-done.tokens, bf16[8,768,256]{2,1,0:T(8,128)(2,1)S(1)} %collective-permute-done.4.core_tokens, ...), custom_call_target="tpu_custom_call" | custom-call | flops 2415919104 | bytes 8388608 | tf_op jit(solution)/shard_map/project/pallas_call | solution.py:328
  100.9 1.7 %summary.1 = (bf16[256,128]{1,0:T(8,128)(2,1)S(1)}, f32[256,128]{1,0:T(8,128)}) custom-call(bf16[32,8,128]{2,1,0:T(8,128)(2,1)S(1)} %all_to_all.20.own, bf16[32,8,128]{2,1,0:T(8,128)(2,1)S(1)} %collective-permute-done.3.other, bf16[1536,128]{1,0:T(8,128)(2,1)S(1)} %get-tuple-element.39.keys, bf16[1536,128]{1,0:T(8,128)(2,1)S(1)} %get-tuple-element.40.values, ...), custom_call_target="tpu_custom_call" | custom-call | flops 201326592 | bytes 2097152 | tf_op jit(solution)/shard_map/summary/pallas_call | solution.py:344
  102.6 4.0 %all-to-all-start.2 = ((f32[32,8,128]{2,1,0:T(8,128)}), f32[32,8,128]{2,1,0:T(8,128)S(1)}, u32[]{:S(2)}, u32[]{:S(2)}) async-start(f32[32,8,128]{2,1,0:T(8,128)} %bitcast.1), calls=%async_computation.2 | async-start | bytes 262144 | tf_op jit(solution)/shard_map/all_to_all | solution.py:365
  106.6 3.6 %inverse.1 = f32[256,256]{1,0:T(8,128)S(1)} custom-call(bf16[256,128]{1,0:T(8,128)(2,1)S(1)} %get-tuple-element.48.marks_ref.marks), custom_call_target="tpu_custom_call" | custom-call | flops 2415919104 | bytes 524288 | tf_op jit(solution)/shard_map/inverse/pallas_call | solution.py:355
  110.2 9.6 %all-to-all-done.2.pieces = f32[32,8,128]{2,1,0:T(8,128)S(1)} async-done(((f32[32,8,128]{2,1,0:T(8,128)}), f32[32,8,128]{2,1,0:T(8,128)S(1)}, u32[]{:S(2)}, u32[]{:S(2)}) %all-to-all-start.2) | async-done | bytes 131104 | tf_op jit(solution)/shard_map/all_to_all | solution.py:365
  119.8 1.0 mixed.1
  120.8 5.4 %all-to-all-start.3 = ((bf16[32,8,128]{2,1,0:T(8,128)(2,1)}), bf16[32,8,128]{2,1,0:T(8,128)(2,1)S(1)}, u32[]{:S(2)}, u32[]{:S(2)}) async-start(bf16[32,8,128]{2,1,0:T(8,128)(2,1)} %mixed.1), calls=%async_computation.3 | async-start | bytes 131072 | tf_op jit(solution)/shard_map/all_to_all | solution.py:375
  126.3 0.8 query_weights.1.weights
  127.0 11.8 %all-to-all-done.3.spread = bf16[32,8,128]{2,1,0:T(8,128)(2,1)S(1)} async-done(((bf16[32,8,128]{2,1,0:T(8,128)(2,1)}), bf16[32,8,128]{2,1,0:T(8,128)(2,1)S(1)}, u32[]{:S(2)}, u32[]{:S(2)}) %all-to-all-start.3) | async-done | bytes 65568 | tf_op jit(solution)/shard_map/all_to_all | solution.py:375
  138.8 0.3 give.1
  139.1 5.5 %collective-permute-start.6 = (bf16[768,128]{1,0:T(8,128)(2,1)S(1)}, bf16[768,128]{1,0:T(8,128)(2,1)S(1)}, u32[]{:S(2)}, u32[]{:S(2)}) collective-permute-start(bf16[768,128]{1,0:T(8,128)(2,1)S(1)} %get-tuple-element.52), channel_id=1, source_target_pairs={{0,1},{1,0},{2,3},{3,2},{4,5},{5,4},{6,7},{7,6},{8,9},{9,8},{10,11... | collective-permute-start | bytes 589832 | tf_op jit(solution)/shard_map/ppermute | solution.py:44
  144.6 0.2 keep.1
  144.9 0.8 collective-permute-done.6.received
  145.7 0.9 join.1
  (10 shorter events, 0.0 us)
Async XLA Ops:
  2.9 7.6 %copy-start.2 = (bf16[3,32,256]{2,1,0:T(8,128)(2,1)S(1)}, bf16[3,32,256]{2,1,0:T(8,128)(2,1)}, u32[]{:S(2)}) copy-start(bf16[3,32,256]{2,1,0:T(8,128)(2,1)} %param.4) | copy-start | bytes 147460
  2.9 52.7 %all-to-all-start = ((bf16[8,768,256]{2,1,0:T(8,128)(2,1)}), bf16[8,768,256]{2,1,0:T(8,128)(2,1)S(1)}, u32[]{:S(2)}, u32[]{:S(2)}) async-start(bf16[8,768,256]{2,1,0:T(8,128)(2,1)} %broadcast_in_dim.2), calls=%async_computation | async-start | bytes 6291456 | tf_op jit(solution)/shard_map/all_to_all | solution.py:271
  10.5 46.6 %copy-start.1 = (s32[2,256]{1,0:T(2,128)S(1)}, s32[2,256]{1,0:T(2,128)}, u32[]{:S(2)}) copy-start(s32[2,256]{1,0:T(2,128)} %pos_ref) | copy-start | bytes 6148
  45.2 8.4 %copy-start = (bf16[3,16,32,256]{3,2,1,0:T(8,128)(2,1)}, bf16[3,16,32,256]{3,2,1,0:T(8,128)(2,1)S(1)}, u32[]{:S(2)}) copy-start(bf16[3,16,32,256]{3,2,1,0:T(8,128)(2,1)S(1)} %stage.1.column) | copy-start | bytes 2359300
  45.2 10.4 %collective-permute-start = (bf16[3,16,32,256]{3,2,1,0:T(8,128)(2,1)S(1)}, bf16[3,16,32,256]{3,2,1,0:T(8,128)(2,1)}, u32[]{:S(2)}, u32[]{:S(2)}) collective-permute-start(bf16[3,16,32,256]{3,2,1,0:T(8,128)(2,1)S(1)} %stage.1.column), channel_id=1, source_target_pairs={{0,1},{1,0},{2,3},{3,2},{4,5},{5,4},{6,7},{7,6},{8,9},{9,8},{10,11... | collective-permute-start | bytes 2359304 | tf_op jit(solution)/shard_map/ppermute | solution.py:44
  58.0 4.8 %collective-permute-start.1 = (bf16[8,2048]{1,0:T(8,128)(2,1)S(1)}, bf16[8,2048]{1,0:T(8,128)(2,1)S(1)}, u32[]{:S(2)}, u32[]{:S(2)}) collective-permute-start(bf16[8,2048]{1,0:T(8,128)(2,1)S(1)} %pick.1.own), channel_id=1, source_target_pairs={{0,2},{2,0},{1,3},{3,1},{4,6},{6,4},{5,7},{7,5},{8,10},{10,8},{9,1... | collective-permute-start | bytes 98312 | tf_op jit(solution)/shard_map/ppermute | solution.py:44
  60.2 35.7 %collective-permute-start.4 = (bf16[8,768,256]{2,1,0:T(8,128)(2,1)S(1)}, bf16[8,768,256]{2,1,0:T(8,128)(2,1)S(1)}, u32[]{:S(2)}, u32[]{:S(2)}) collective-permute-start(bf16[8,768,256]{2,1,0:T(8,128)(2,1)S(1)} %all-to-all-done.tokens), channel_id=1, source_target_pairs={{0,1},{1,0},{2,3},{3,2},{4,5},{5,4},{6,7},{7,6},{8,9},{9,8},{10,11... | collective-permute-start | bytes 9437192 | tf_op jit(solution)/shard_map/ppermute | solution.py:44
  63.1 5.3 %collective-permute-start.2 = (f32[8,128]{1,0:T(8,128)S(1)}, f32[8,128]{1,0:T(8,128)S(1)}, u32[]{:S(2)}, u32[]{:S(2)}) collective-permute-start(f32[8,128]{1,0:T(8,128)S(1)} %get-tuple-element.36), channel_id=1, source_target_pairs={{0,2},{2,0},{1,3},{3,1},{4,6},{6,4},{5,7},{7,5},{8,10},{10,8},{9,1... | collective-permute-start | bytes 12296 | tf_op jit(solution)/shard_map/ppermute | solution.py:44
  66.2 29.7 %collective-permute-start.5 = (bf16[2,3,16,32,128]{4,3,2,1,0:T(8,128)(2,1)S(1)}, bf16[2,3,16,32,128]{4,3,2,1,0:T(8,128)(2,1)S(1)}, u32[]{:S(2)}, u32[]{:S(2)}) collective-permute-start(bf16[2,3,16,32,128]{4,3,2,1,0:T(8,128)(2,1)S(1)} %get-tuple-element.38.packed), channel_id=1, source_target_pairs={{0,2},{2,0},{1,3},{3,1},{4,6},{6,4},{5,7},{7,5},{8,10},{10,8},{9,1... | collective-permute-start | bytes 2359304 | tf_op jit(solution)/shard_map/ppermute | solution.py:44
  93.7 7.3 %collective-permute-start.3 = (bf16[32,8,128]{2,1,0:T(8,128)(2,1)S(1)}, bf16[32,8,128]{2,1,0:T(8,128)(2,1)S(1)}, u32[]{:S(2)}, u32[]{:S(2)}) collective-permute-start(bf16[32,8,128]{2,1,0:T(8,128)(2,1)S(1)} %all_to_all.20.own), channel_id=1, source_target_pairs={{0,2},{2,0},{1,3},{3,1},{4,6},{6,4},{5,7},{7,5},{8,10},{10,8},{9,1... | collective-permute-start | bytes 196616 | tf_op jit(solution)/shard_map/ppermute | solution.py:44
  102.6 17.2 %all-to-all-start.2 = ((f32[32,8,128]{2,1,0:T(8,128)}), f32[32,8,128]{2,1,0:T(8,128)S(1)}, u32[]{:S(2)}, u32[]{:S(2)}) async-start(f32[32,8,128]{2,1,0:T(8,128)} %bitcast.1), calls=%async_computation.2 | async-start | bytes 262144 | tf_op jit(solution)/shard_map/all_to_all | solution.py:365
  120.8 18.0 %all-to-all-start.3 = ((bf16[32,8,128]{2,1,0:T(8,128)(2,1)}), bf16[32,8,128]{2,1,0:T(8,128)(2,1)S(1)}, u32[]{:S(2)}, u32[]{:S(2)}) async-start(bf16[32,8,128]{2,1,0:T(8,128)(2,1)} %mixed.1), calls=%async_computation.3 | async-start | bytes 131072 | tf_op jit(solution)/shard_map/all_to_all | solution.py:375
  139.1 6.6 %collective-permute-start.6 = (bf16[768,128]{1,0:T(8,128)(2,1)S(1)}, bf16[768,128]{1,0:T(8,128)(2,1)S(1)}, u32[]{:S(2)}, u32[]{:S(2)}) collective-permute-start(bf16[768,128]{1,0:T(8,128)(2,1)S(1)} %get-tuple-element.52), channel_id=1, source_target_pairs={{0,1},{1,0},{2,3},{3,2},{4,5},{5,4},{6,7},{7,6},{8,9},{9,8},{10,11... | collective-permute-start | bytes 589832 | tf_op jit(solution)/shard_map/ppermute | solution.py:44

commit v11 on v10

--- a/solution.py
+++ b/solution.py
@@ -284,18 +284,7 @@
     )(column)
     core = shift(column, "c", 1)
     column, core = in_hbm(column, core)
-    core, later = lax.optimization_barrier((core, whole))
-    core_tokens = shift(later, "c", 1)
-    wide, packed = call(
-        prepare_kernel,
-        "prepare",
-        (shape((2, 16, 2, 32, 256), BF16), shape((2, 3, 16, 32, 128), BF16)),
-        [ANY, ANY],
-        1 << 10,
-        3 << 20,
-        [pltpu.SemaphoreType.DMA((4,))],
-    )(column, core)
-    landmark_pos, wide = lax.optimization_barrier((landmark_pos, wide))
+    landmark_pos, column = lax.optimization_barrier((landmark_pos, column))
     picked = call(
         pick_kernel,
         "pick",
@@ -309,7 +298,18 @@
             pltpu.SemaphoreType.DMA((8,)),
         ],
     )(landmark_pos, whole)
+    picked, column, whole = lax.optimization_barrier((picked, column, whole))
     other_picked = shift(picked, "xl", 1)
+    core_tokens = shift(whole, "c", 1)
+    wide, packed = call(
+        prepare_kernel,
+        "prepare",
+        (shape((2, 16, 2, 32, 256), BF16), shape((2, 3, 16, 32, 128), BF16)),
+        [ANY, ANY],
+        1 << 10,
+        3 << 20,
+        [pltpu.SemaphoreType.DMA((4,))],
+    )(column, core)
     keep, give = call(
         partial_kernel,
         "partial",

time: 147 us -> 147 us (level)
  waiting for transfers between devices: 24.2 us -> 22.4 us
    ppermute x7, waiting for transfers between devices: 2.82 us -> 0.8 us  [shift(): lax.ppermute(value, axis, [(i, (i + step) % size) for i in range(size)])]
  transfers between devices with their start and end apart: 10 -> 10, of which waited for: 4 -> 3; matrix products, arithmetic and copies ran while one was open for 0% -> 0% of each run, Pallas kernels for 7% -> 9%
where the time goes in v11:
time: 147 us; the launch traced here: 146 us
  blocking collectives  60 us (41%)
  starting transfers between devices  43.3 us (29%)
  waiting for transfers between devices  22.4 us (15%)
  Pallas kernels  17.1 us (12%)
  local copies, waits for them, and re-layouts  2.85 us (2%)
    all_gather x1, blocking collectives, shards(): lax.all_gather(weights, 'z', axis=1, tiled=True).reshape(3, 16, 32, 256)  34.6 us
    ppermute x7, starting transfers between devices, shift(): lax.ppermute(value, axis, [(i, (i + step) % size) for i in range(size)])  27.2 us
    all_to_all x1, blocking collectives, shards(): own_marks = lax.all_to_all(spread, CORES, 0, 0, tiled=True)  25.4 us
    all_to_all x1, waiting for transfers between devices, shards(): spread = lax.all_to_all(spread, CHIPS, 0, 0, tiled=True)  11.8 us
    all_to_all x1, waiting for transfers between devices, shards(): pieces = lax.all_to_all(chip.reshape(32, 8, 128), CHIPS, 0, 0, tiled=True)  9.84 us
    all_to_all x1, starting transfers between devices, shards(): lax.all_to_all(jnp.broadcast_to(tokens[None], (8,) + tokens.shape), HEAD,...  7.61 us
    pallas_call x1, Pallas kernels, shards(): call(project_kernel, 'project', (shape((1536, 128), BF16), shape((1536, 1...  5 us
    all_to_all x1, starting transfers between devices, shards(): spread = lax.all_to_all(spread, CHIPS, 0, 0, tiled=True)  4.61 us
  transfers between devices with their start and end apart: 10, of which 3 were waited for; matrix products, arithmetic and copies ran while one was open for 0% of the time, Pallas kernels for 9%

profile of v11, /device:TPU:1, one launch (start us, length us, event | category | flops | bytes accessed | tf_op | source)
XLA Modules:
  0.0 145.9 jit_solution(8443471334564365198)
XLA Ops:
  0.0 2.8 %broadcast_in_dim.2 = bf16[8,768,256]{2,1,0:T(8,128)(2,1)} broadcast(bf16[768,256]{1,0:T(8,128)(2,1)} %param.3), dimensions={1,2} | broadcast | bytes 3538944 | tf_op jit(solution)/shard_map/broadcast_in_dim | solution.py:272
  2.8 7.6 %all-to-all-start = ((bf16[8,768,256]{2,1,0:T(8,128)(2,1)}), bf16[8,768,256]{2,1,0:T(8,128)(2,1)S(1)}, u32[]{:S(2)}, u32[]{:S(2)}) async-start(bf16[8,768,256]{2,1,0:T(8,128)(2,1)} %broadcast_in_dim.2), calls=%async_computation | async-start | bytes 6291456 | tf_op jit(solution)/shard_map/all_to_all | solution.py:271
  10.5 34.6 %all_gather.3 = bf16[3,512,256]{2,1,0:T(8,128)(2,1)S(1)} all-gather(bf16[3,32,256]{2,1,0:T(8,128)(2,1)S(1)} %copy-done.1), channel_id=1, replica_groups=mesh['y'=4,'xh'=2,'z'=16,'xl'=2,'c'=2] {'z'}, dimensions={1}, use_global_device_ids=true | all-gather | bytes 835584 | tf_op jit(solution)/shard_map/all_gather | solution.py:274
  45.1 0.9 stage.1.column
  46.0 8.3 %collective-permute-start.1 = (bf16[3,16,32,256]{3,2,1,0:T(8,128)(2,1)}, bf16[3,16,32,256]{3,2,1,0:T(8,128)(2,1)}, u32[]{:S(2)}, u32[]{:S(2)}) collective-permute-start(bf16[3,16,32,256]{3,2,1,0:T(8,128)(2,1)} %stage.1.column), channel_id=1, source_target_pairs={{0,1},{1,0},{2,3},{3,2},{4,5},{5,4},{6,7},{7,6},{8,9},{9,8},{10,11... | collective-permute-start | bytes 2359304 | tf_op jit(solution)/shard_map/ppermute | solution.py:44
  54.3 0.0 all-to-all-done.tokens
  54.4 1.0 pick.1.own
  55.3 2.2 %collective-permute-start = (bf16[8,2048]{1,0:T(8,128)(2,1)S(1)}, bf16[8,2048]{1,0:T(8,128)(2,1)S(1)}, u32[]{:S(2)}, u32[]{:S(2)}) collective-permute-start(bf16[8,2048]{1,0:T(8,128)(2,1)S(1)} %pick.1.own), channel_id=1, source_target_pairs={{0,2},{2,0},{1,3},{3,1},{4,6},{6,4},{5,7},{7,5},{8,10},{10,8},{9,1... | collective-permute-start | bytes 98312 | tf_op jit(solution)/shard_map/ppermute | solution.py:44
  57.6 2.2 %collective-permute-start.4 = (bf16[8,768,256]{2,1,0:T(8,128)(2,1)S(1)}, bf16[8,768,256]{2,1,0:T(8,128)(2,1)S(1)}, u32[]{:S(2)}, u32[]{:S(2)}) collective-permute-start(bf16[8,768,256]{2,1,0:T(8,128)(2,1)S(1)} %all-to-all-done.tokens), channel_id=1, source_target_pairs={{0,1},{1,0},{2,3},{3,2},{4,5},{5,4},{6,7},{7,6},{8,9},{9,8},{10,11... | collective-permute-start | bytes 9437192 | tf_op jit(solution)/shard_map/ppermute | solution.py:44
  59.8 0.0 collective-permute-done.1.core
  59.8 1.5 %prepare.1 = (bf16[2,16,2,32,256]{4,3,2,1,0:T(8,128)(2,1)S(1)}, bf16[2,3,16,32,128]{4,3,2,1,0:T(8,128)(2,1)S(1)}) custom-call(bf16[3,16,32,256]{3,2,1,0:T(8,128)(2,1)} %stage.1.column, bf16[3,16,32,256]{3,2,1,0:T(8,128)(2,1)} %collective-permute-done.1.core), custom_call_target="tpu_custom_call" | custom-call | flops 1024 | bytes 3145728 | tf_op jit(solution)/shard_map/prepare/pallas_call | solution.py:304
  61.3 0.0 collective-permute-done.other
  61.3 0.3 partial.1
  61.5 3.1 %collective-permute-start.2 = (f32[8,128]{1,0:T(8,128)S(1)}, f32[8,128]{1,0:T(8,128)S(1)}, u32[]{:S(2)}, u32[]{:S(2)}) collective-permute-start(f32[8,128]{1,0:T(8,128)S(1)} %get-tuple-element.38), channel_id=1, source_target_pairs={{0,2},{2,0},{1,3},{3,1},{4,6},{6,4},{5,7},{7,5},{8,10},{10,8},{9,1... | collective-permute-start | bytes 12296 | tf_op jit(solution)/shard_map/ppermute | solution.py:44
  64.6 2.2 %collective-permute-start.5 = (bf16[2,3,16,32,128]{4,3,2,1,0:T(8,128)(2,1)S(1)}, bf16[2,3,16,32,128]{4,3,2,1,0:T(8,128)(2,1)S(1)}, u32[]{:S(2)}, u32[]{:S(2)}) collective-permute-start(bf16[2,3,16,32,128]{4,3,2,1,0:T(8,128)(2,1)S(1)} %get-tuple-element.40.packed), channel_id=1, source_target_pairs={{0,2},{2,0},{1,3},{3,1},{4,6},{6,4},{5,7},{7,5},{8,10},{10,8},{9,1... | collective-permute-start | bytes 2359304 | tf_op jit(solution)/shard_map/ppermute | solution.py:44
  66.9 0.0 collective-permute-done.2.received
  66.9 25.4 %all_to_all.20.own = bf16[32,8,128]{2,1,0:T(8,128)(2,1)S(1)} all-to-all(bf16[32,8,128]{2,1,0:T(8,128)(2,1)S(1)} %finish.1), channel_id=1, replica_groups=mesh['y'=4,'xh'=2,'z'=16,'xl'=2,'c'=2] {'z','c'}, dimensions={0} | all-to-all | bytes 131072 | tf_op jit(solution)/shard_map/all_to_all | solution.py:327
  92.3 3.0 %collective-permute-start.3 = (bf16[32,8,128]{2,1,0:T(8,128)(2,1)S(1)}, bf16[32,8,128]{2,1,0:T(8,128)(2,1)S(1)}, u32[]{:S(2)}, u32[]{:S(2)}) collective-permute-start(bf16[32,8,128]{2,1,0:T(8,128)(2,1)S(1)} %all_to_all.20.own), channel_id=1, source_target_pairs={{0,2},{2,0},{1,3},{3,1},{4,6},{6,4},{5,7},{7,5},{8,10},{10,8},{9,1... | collective-permute-start | bytes 196616 | tf_op jit(solution)/shard_map/ppermute | solution.py:44
  95.4 5.0 %project.1 = (bf16[1536,128]{1,0:T(8,128)(2,1)S(1)}, bf16[1536,128]{1,0:T(8,128)(2,1)S(1)}, bf16[1536,128]{1,0:T(8,128)(2,1)S(1)}, f32[1536,1]{1,0:T(8,128)S(1)}) custom-call(bf16[8,768,256]{2,1,0:T(8,128)(2,1)S(1)} %all-to-all-done.tokens, bf16[8,768,256]{2,1,0:T(8,128)(2,1)S(1)} %collective-permute-done.4.core_tokens, ...), custom_call_target="tpu_custom_call" | custom-call | flops 2415919104 | bytes 8388608 | tf_op jit(solution)/shard_map/project/pallas_call | solution.py:328
  100.4 1.7 %summary.1 = (bf16[256,128]{1,0:T(8,128)(2,1)S(1)}, f32[256,128]{1,0:T(8,128)}) custom-call(bf16[32,8,128]{2,1,0:T(8,128)(2,1)S(1)} %all_to_all.20.own, bf16[32,8,128]{2,1,0:T(8,128)(2,1)S(1)} %collective-permute-done.3.other, bf16[1536,128]{1,0:T(8,128)(2,1)S(1)} %get-tuple-element.41.keys, bf16[1536,128]{1,0:T(8,128)(2,1)S(1)} %get-tuple-element.42.values, ...), custom_call_target="tpu_custom_call" | custom-call | flops 201326592 | bytes 2097152 | tf_op jit(solution)/shard_map/summary/pallas_call | solution.py:344
  102.1 3.9 %all-to-all-start.2 = ((f32[32,8,128]{2,1,0:T(8,128)}), f32[32,8,128]{2,1,0:T(8,128)S(1)}, u32[]{:S(2)}, u32[]{:S(2)}) async-start(f32[32,8,128]{2,1,0:T(8,128)} %bitcast.1), calls=%async_computation.2 | async-start | bytes 262144 | tf_op jit(solution)/shard_map/all_to_all | solution.py:365
  105.9 3.6 %inverse.1 = f32[256,256]{1,0:T(8,128)S(1)} custom-call(bf16[256,128]{1,0:T(8,128)(2,1)S(1)} %get-tuple-element.50.marks_ref.marks), custom_call_target="tpu_custom_call" | custom-call | flops 2415919104 | bytes 524288 | tf_op jit(solution)/shard_map/inverse/pallas_call | solution.py:355
  109.6 9.8 %all-to-all-done.2.pieces = f32[32,8,128]{2,1,0:T(8,128)S(1)} async-done(((f32[32,8,128]{2,1,0:T(8,128)}), f32[32,8,128]{2,1,0:T(8,128)S(1)}, u32[]{:S(2)}, u32[]{:S(2)}) %all-to-all-start.2) | async-done | bytes 131104 | tf_op jit(solution)/shard_map/all_to_all | solution.py:365
  119.4 1.0 mixed.1
  120.4 4.6 %all-to-all-start.3 = ((bf16[32,8,128]{2,1,0:T(8,128)(2,1)}), bf16[32,8,128]{2,1,0:T(8,128)(2,1)S(1)}, u32[]{:S(2)}, u32[]{:S(2)}) async-start(bf16[32,8,128]{2,1,0:T(8,128)(2,1)} %mixed.1), calls=%async_computation.3 | async-start | bytes 131072 | tf_op jit(solution)/shard_map/all_to_all | solution.py:375
  125.0 0.8 query_weights.1.weights
  125.8 11.8 %all-to-all-done.3.spread = bf16[32,8,128]{2,1,0:T(8,128)(2,1)S(1)} async-done(((bf16[32,8,128]{2,1,0:T(8,128)(2,1)}), bf16[32,8,128]{2,1,0:T(8,128)(2,1)S(1)}, u32[]{:S(2)}, u32[]{:S(2)}) %all-to-all-start.3) | async-done | bytes 65568 | tf_op jit(solution)/shard_map/all_to_all | solution.py:375
  137.6 0.3 give.1
  137.9 6.1 %collective-permute-start.6 = (bf16[768,128]{1,0:T(8,128)(2,1)S(1)}, bf16[768,128]{1,0:T(8,128)(2,1)S(1)}, u32[]{:S(2)}, u32[]{:S(2)}) collective-permute-start(bf16[768,128]{1,0:T(8,128)(2,1)S(1)} %get-tuple-element.54), channel_id=1, source_target_pairs={{0,1},{1,0},{2,3},{3,2},{4,5},{5,4},{6,7},{7,6},{8,9},{9,8},{10,11... | collective-permute-start | bytes 589832 | tf_op jit(solution)/shard_map/ppermute | solution.py:44
  144.0 0.3 keep.1
  144.2 0.8 collective-permute-done.6.received
  145.0 0.9 join.1
  (8 shorter events, 0.0 us)
Async XLA Ops:
  2.8 7.6 %copy-start.1 = (bf16[3,32,256]{2,1,0:T(8,128)(2,1)S(1)}, bf16[3,32,256]{2,1,0:T(8,128)(2,1)}, u32[]{:S(2)}) copy-start(bf16[3,32,256]{2,1,0:T(8,128)(2,1)} %param.4) | copy-start | bytes 147460
  2.8 51.5 %copy-start = (s32[2,256]{1,0:T(2,128)S(1)}, s32[2,256]{1,0:T(2,128)}, u32[]{:S(2)}) copy-start(s32[2,256]{1,0:T(2,128)} %pos_ref) | copy-start | bytes 6148
  2.8 51.5 %all-to-all-start = ((bf16[8,768,256]{2,1,0:T(8,128)(2,1)}), bf16[8,768,256]{2,1,0:T(8,128)(2,1)S(1)}, u32[]{:S(2)}, u32[]{:S(2)}) async-start(bf16[8,768,256]{2,1,0:T(8,128)(2,1)} %broadcast_in_dim.2), calls=%async_computation | async-start | bytes 6291456 | tf_op jit(solution)/shard_map/all_to_all | solution.py:271
  46.0 13.8 %collective-permute-start.1 = (bf16[3,16,32,256]{3,2,1,0:T(8,128)(2,1)}, bf16[3,16,32,256]{3,2,1,0:T(8,128)(2,1)}, u32[]{:S(2)}, u32[]{:S(2)}) collective-permute-start(bf16[3,16,32,256]{3,2,1,0:T(8,128)(2,1)} %stage.1.column), channel_id=1, source_target_pairs={{0,1},{1,0},{2,3},{3,2},{4,5},{5,4},{6,7},{7,6},{8,9},{9,8},{10,11... | collective-permute-start | bytes 2359304 | tf_op jit(solution)/shard_map/ppermute | solution.py:44
  55.3 5.9 %collective-permute-start = (bf16[8,2048]{1,0:T(8,128)(2,1)S(1)}, bf16[8,2048]{1,0:T(8,128)(2,1)S(1)}, u32[]{:S(2)}, u32[]{:S(2)}) collective-permute-start(bf16[8,2048]{1,0:T(8,128)(2,1)S(1)} %pick.1.own), channel_id=1, source_target_pairs={{0,2},{2,0},{1,3},{3,1},{4,6},{6,4},{5,7},{7,5},{8,10},{10,8},{9,1... | collective-permute-start | bytes 98312 | tf_op jit(solution)/shard_map/ppermute | solution.py:44
  57.6 37.8 %collective-permute-start.4 = (bf16[8,768,256]{2,1,0:T(8,128)(2,1)S(1)}, bf16[8,768,256]{2,1,0:T(8,128)(2,1)S(1)}, u32[]{:S(2)}, u32[]{:S(2)}) collective-permute-start(bf16[8,768,256]{2,1,0:T(8,128)(2,1)S(1)} %all-to-all-done.tokens), channel_id=1, source_target_pairs={{0,1},{1,0},{2,3},{3,2},{4,5},{5,4},{6,7},{7,6},{8,9},{9,8},{10,11... | collective-permute-start | bytes 9437192 | tf_op jit(solution)/shard_map/ppermute | solution.py:44
  61.5 5.3 %collective-permute-start.2 = (f32[8,128]{1,0:T(8,128)S(1)}, f32[8,128]{1,0:T(8,128)S(1)}, u32[]{:S(2)}, u32[]{:S(2)}) collective-permute-start(f32[8,128]{1,0:T(8,128)S(1)} %get-tuple-element.38), channel_id=1, source_target_pairs={{0,2},{2,0},{1,3},{3,1},{4,6},{6,4},{5,7},{7,5},{8,10},{10,8},{9,1... | collective-permute-start | bytes 12296 | tf_op jit(solution)/shard_map/ppermute | solution.py:44
  64.6 30.8 %collective-permute-start.5 = (bf16[2,3,16,32,128]{4,3,2,1,0:T(8,128)(2,1)S(1)}, bf16[2,3,16,32,128]{4,3,2,1,0:T(8,128)(2,1)S(1)}, u32[]{:S(2)}, u32[]{:S(2)}) collective-permute-start(bf16[2,3,16,32,128]{4,3,2,1,0:T(8,128)(2,1)S(1)} %get-tuple-element.40.packed), channel_id=1, source_target_pairs={{0,2},{2,0},{1,3},{3,1},{4,6},{6,4},{5,7},{7,5},{8,10},{10,8},{9,1... | collective-permute-start | bytes 2359304 | tf_op jit(solution)/shard_map/ppermute | solution.py:44
  92.3 8.1 %collective-permute-start.3 = (bf16[32,8,128]{2,1,0:T(8,128)(2,1)S(1)}, bf16[32,8,128]{2,1,0:T(8,128)(2,1)S(1)}, u32[]{:S(2)}, u32[]{:S(2)}) collective-permute-start(bf16[32,8,128]{2,1,0:T(8,128)(2,1)S(1)} %all_to_all.20.own), channel_id=1, source_target_pairs={{0,2},{2,0},{1,3},{3,1},{4,6},{6,4},{5,7},{7,5},{8,10},{10,8},{9,1... | collective-permute-start | bytes 196616 | tf_op jit(solution)/shard_map/ppermute | solution.py:44
  102.1 17.3 %all-to-all-start.2 = ((f32[32,8,128]{2,1,0:T(8,128)}), f32[32,8,128]{2,1,0:T(8,128)S(1)}, u32[]{:S(2)}, u32[]{:S(2)}) async-start(f32[32,8,128]{2,1,0:T(8,128)} %bitcast.1), calls=%async_computation.2 | async-start | bytes 262144 | tf_op jit(solution)/shard_map/all_to_all | solution.py:365
  120.4 17.2 %all-to-all-start.3 = ((bf16[32,8,128]{2,1,0:T(8,128)(2,1)}), bf16[32,8,128]{2,1,0:T(8,128)(2,1)S(1)}, u32[]{:S(2)}, u32[]{:S(2)}) async-start(bf16[32,8,128]{2,1,0:T(8,128)(2,1)} %mixed.1), calls=%async_computation.3 | async-start | bytes 131072 | tf_op jit(solution)/shard_map/all_to_all | solution.py:375
  137.9 7.1 %collective-permute-start.6 = (bf16[768,128]{1,0:T(8,128)(2,1)S(1)}, bf16[768,128]{1,0:T(8,128)(2,1)S(1)}, u32[]{:S(2)}, u32[]{:S(2)}) collective-permute-start(bf16[768,128]{1,0:T(8,128)(2,1)S(1)} %get-tuple-element.54), channel_id=1, source_target_pairs={{0,1},{1,0},{2,3},{3,2},{4,5},{5,4},{6,7},{7,6},{8,9},{9,8},{10,11... | collective-permute-start | bytes 589832 | tf_op jit(solution)/shard_map/ppermute | solution.py:44

commit v12 on v11

--- a/solution.py
+++ b/solution.py
@@ -142,36 +142,57 @@
         spread[place] = chosen
 
 
-def project_kernel(tokens, core_tokens, packed, across, query, keys, values, norms, w, sems):
+def order_weights(first, packed, across, w, sems):
     xl = lax.axis_index("xl")
     copies = []
     for part in range(2):
         for source, row in ((packed, xl), (across, 1 - xl)):
             copies.append(
                 pltpu.make_async_copy(
-                    source.at[part], w.at[:, :, row, part], sems.at[len(copies)]
+                    source.at[part, pl.ds(first, w.shape[0])],
+                    w.at[:, :, row, part],
+                    sems.at[len(copies)],
                 )
             )
     run(copies)
+
+
+def side_by_side(source, start):
+    return jnp.concatenate(
+        [source[block, pl.ds(start, 256), :] for block in range(source.shape[0])], 1
+    )
+
+
+def key_value_kernel(tokens, core_tokens, packed, across, keys, values, norms, w, sems):
+    order_weights(1, packed, across, w, sems)
     blocks, rows, width = tokens.shape
-    weights = [w[kind].reshape(blocks * width, 128) for kind in range(3)]
-    pair = jnp.concatenate(weights[:2], 1)
+    pair = jnp.concatenate([w[kind].reshape(blocks * width, 128) for kind in range(2)], 1)
     for number, source in enumerate((tokens, core_tokens)):
 
         @pl.loop(0, 3)
         def _(step):
             start = pl.multiple_of(step * 256, 256)
             here = pl.ds(number * rows + start, 256)
-            left = jnp.concatenate(
-                [source[block, pl.ds(start, 256), :] for block in range(blocks)], 1
-            )
-            both = jnp.dot(left, pair, preferred_element_type=F32).astype(BF16)
-            query[here, :] = both[:, :128]
-            keys[here, :] = both[:, 128:]
-            values[here, :] = jnp.dot(
-                left, weights[2], preferred_element_type=F32
+            both = jnp.dot(
+                side_by_side(source, start), pair, preferred_element_type=F32
             ).astype(BF16)
-            norms[here, :] = down_norm(both[:, 128:])
+            keys[here, :] = both[:, :128]
+            values[here, :] = both[:, 128:]
+            norms[here, :] = down_norm(both[:, :128])
+
+
+def query_kernel(tokens, core_tokens, packed, across, query, w, sems):
+    order_weights(0, packed, across, w, sems)
+    blocks, rows, width = tokens.shape
+    matrix = w[0].reshape(blocks * width, 128)
+    for number, source in enumerate((tokens, core_tokens)):
+
+        @pl.loop(0, 3)
+        def _(step):
+            start = pl.multiple_of(step * 256, 256)
+            query[pl.ds(number * rows + start, 256), :] = jnp.dot(
+                side_by_side(source, start), matrix, preferred_element_type=F32
+            ).astype(BF16)
 
 
 def summary_kernel(own, other, keys, values, norms, marks, pieces, flat, part):
@@ -325,21 +346,15 @@
         finish_kernel, "finish", shape((32, 8, 128), BF16), [VMEM] * 2, 1 << 34, 1 << 16
     )(keep, received)
     own_marks = lax.all_to_all(spread, CORES, 0, 0, tiled=True)
-    query, keys, values, norms = call(
-        project_kernel,
-        "project",
-        (
-            shape((1536, 128), BF16),
-            shape((1536, 128), BF16),
-            shape((1536, 128), BF16),
-            shape((1536, 1), F32),
-        ),
+    keys, values, norms = call(
+        key_value_kernel,
+        "key_values",
+        (shape((1536, 128), BF16), shape((1536, 128), BF16), shape((1536, 1), F32)),
         [VMEM, VMEM, ANY, ANY],
-        2 * 1536 * 2048 * 384,
+        2 * 1536 * 2048 * 256,
         8 << 20,
-        [pltpu.VMEM((3, 16, 2, 2, 32, 128), BF16), pltpu.SemaphoreType.DMA((4,))],
+        [pltpu.VMEM((2, 16, 2, 2, 32, 128), BF16), pltpu.SemaphoreType.DMA((4,))],
     )(whole, core_tokens, packed, across)
-
     other_marks = shift(own_marks, "xl", 1)
     marks, chip = call(
         summary_kernel,
@@ -371,8 +386,17 @@
         2 * 6 * 16 * 256 * 128,
         1 << 19,
     )(pieces, inverse)
-    spread, marks = lax.optimization_barrier((spread, marks))
+    spread, marks, packed = lax.optimization_barrier((spread, marks, packed))
     spread = lax.all_to_all(spread, CHIPS, 0, 0, tiled=True)
+    query = call(
+        query_kernel,
+        "queries",
+        shape((1536, 128), BF16),
+        [VMEM, VMEM, ANY, ANY],
+        2 * 1536 * 2048 * 128,
+        7 << 20,
+        [pltpu.VMEM((1, 16, 2, 2, 32, 128), BF16), pltpu.SemaphoreType.DMA((4,))],
+    )(whole, core_tokens, packed, across)
     query_weights = call(
         query_weight_kernel,
         "query_weights",

time: 147 us -> 146 us (level)
  waiting for transfers between devices: 22.4 us -> 14.7 us
  local copies, waits for them, and re-layouts: 2.85 us -> 9.1 us
    all_to_all x1, waiting for transfers between devices: 11.8 us -> 4.91 us  [shards(): spread = lax.all_to_all(spread, CHIPS, 0, 0, tiled=True)]
    unnamed x4 -> x24, local copies, waits for them, and re-layouts: 0.01 us -> 6.27 us
    pallas_call x1 -> x2, Pallas kernels: 5 us -> 6 us  [the longest x1 3.28 us: shards(): call(key_value_kernel, 'key_values', (shape((1536, 128), BF16), shape((15...]
  transfers between devices with their start and end apart: 10 -> 10, of which waited for: 3 -> 3; matrix products, arithmetic and copies ran while one was open for 0% -> 0% of each run, Pallas kernels for 9% -> 10%
where the time goes in v12:
time: 146 us; the launch traced here: 145 us
  blocking collectives  60.1 us (41%)
  starting transfers between devices  43.3 us (30%)
  Pallas kernels  17.4 us (12%)
  waiting for transfers between devices  14.7 us (10%)
  local copies, waits for them, and re-layouts  9.1 us (6%)
    all_gather x1, blocking collectives, shards(): lax.all_gather(weights, 'z', axis=1, tiled=True).reshape(3, 16, 32, 256)  34.6 us
    ppermute x7, starting transfers between devices, shift(): lax.ppermute(value, axis, [(i, (i + step) % size) for i in range(size)])  27.2 us
    all_to_all x1, blocking collectives, shards(): own_marks = lax.all_to_all(spread, CORES, 0, 0, tiled=True)  25.5 us
    all_to_all x1, waiting for transfers between devices, shards(): pieces = lax.all_to_all(chip.reshape(32, 8, 128), CHIPS, 0, 0, tiled=True)  8.99 us
    all_to_all x1, starting transfers between devices, shards(): lax.all_to_all(jnp.broadcast_to(tokens[None], (8,) + tokens.shape), HEAD,...  7.61 us
    unnamed x24, local copies, waits for them, and re-layouts  6.27 us
    all_to_all x1, waiting for transfers between devices, shards(): spread = lax.all_to_all(spread, CHIPS, 0, 0, tiled=True)  4.91 us
    all_to_all x1, starting transfers between devices, shards(): spread = lax.all_to_all(spread, CHIPS, 0, 0, tiled=True)  4.62 us
  transfers between devices with their start and end apart: 10, of which 3 were waited for; matrix products, arithmetic and copies ran while one was open for 0% of the time, Pallas kernels for 10%

profile of v12, /device:TPU:1, one launch (start us, length us, event | category | flops | bytes accessed | tf_op | source)
XLA Modules:
  0.0 144.8 jit_solution(17985616243908853656)
XLA Ops:
  0.0 2.8 %broadcast_in_dim.2 = bf16[8,768,256]{2,1,0:T(8,128)(2,1)} broadcast(bf16[768,256]{1,0:T(8,128)(2,1)} %param.3), dimensions={1,2} | broadcast | bytes 3538944 | tf_op jit(solution)/shard_map/broadcast_in_dim | solution.py:293
  2.8 7.6 %all-to-all-start = ((bf16[8,768,256]{2,1,0:T(8,128)(2,1)}), bf16[8,768,256]{2,1,0:T(8,128)(2,1)S(1)}, u32[]{:S(2)}, u32[]{:S(2)}) async-start(bf16[8,768,256]{2,1,0:T(8,128)(2,1)} %broadcast_in_dim.2), calls=%async_computation | async-start | bytes 6291456 | tf_op jit(solution)/shard_map/all_to_all | solution.py:292
  10.5 34.6 %all_gather.3 = bf16[3,512,256]{2,1,0:T(8,128)(2,1)S(1)} all-gather(bf16[3,32,256]{2,1,0:T(8,128)(2,1)S(1)} %copy-done.11), channel_id=1, replica_groups=mesh['y'=4,'xh'=2,'z'=16,'xl'=2,'c'=2] {'z'}, dimensions={1}, use_global_device_ids=true | all-gather | bytes 835584 | tf_op jit(solution)/shard_map/all_gather | solution.py:295
  45.1 0.9 stage.1.column
  46.0 8.3 %collective-permute-start.1 = (bf16[3,16,32,256]{3,2,1,0:T(8,128)(2,1)}, bf16[3,16,32,256]{3,2,1,0:T(8,128)(2,1)}, u32[]{:S(2)}, u32[]{:S(2)}) collective-permute-start(bf16[3,16,32,256]{3,2,1,0:T(8,128)(2,1)} %stage.1.column), channel_id=1, source_target_pairs={{0,1},{1,0},{2,3},{3,2},{4,5},{5,4},{6,7},{7,6},{8,9},{9,8},{10,11... | collective-permute-start | bytes 2359304 | tf_op jit(solution)/shard_map/ppermute | solution.py:44
  54.3 1.0 pick.1.own
  55.3 2.2 %collective-permute-start = (bf16[8,2048]{1,0:T(8,128)(2,1)S(1)}, bf16[8,2048]{1,0:T(8,128)(2,1)S(1)}, u32[]{:S(2)}, u32[]{:S(2)}) collective-permute-start(bf16[8,2048]{1,0:T(8,128)(2,1)S(1)} %pick.1.own), channel_id=1, source_target_pairs={{0,2},{2,0},{1,3},{3,1},{4,6},{6,4},{5,7},{7,5},{8,10},{10,8},{9,1... | collective-permute-start | bytes 98312 | tf_op jit(solution)/shard_map/ppermute | solution.py:44
  57.5 2.2 %collective-permute-start.4 = (bf16[8,768,256]{2,1,0:T(8,128)(2,1)S(1)}, bf16[8,768,256]{2,1,0:T(8,128)(2,1)S(1)}, u32[]{:S(2)}, u32[]{:S(2)}) collective-permute-start(bf16[8,768,256]{2,1,0:T(8,128)(2,1)S(1)} %all-to-all-done.tokens), channel_id=1, source_target_pairs={{0,1},{1,0},{2,3},{3,2},{4,5},{5,4},{6,7},{7,6},{8,9},{9,8},{10,11... | collective-permute-start | bytes 9437192 | tf_op jit(solution)/shard_map/ppermute | solution.py:44
  59.7 1.5 %prepare.1 = (bf16[2,16,2,32,256]{4,3,2,1,0:T(8,128)(2,1)S(1)}, bf16[2,3,16,32,128]{4,3,2,1,0:T(8,128)(2,1)S(1)}) custom-call(bf16[3,16,32,256]{3,2,1,0:T(8,128)(2,1)} %stage.1.column, bf16[3,16,32,256]{3,2,1,0:T(8,128)(2,1)} %collective-permute-done.1.core), custom_call_target="tpu_custom_call" | custom-call | flops 1024 | bytes 3145728 | tf_op jit(solution)/shard_map/prepare/pallas_call | solution.py:325
  61.5 3.1 %collective-permute-start.2 = (f32[8,128]{1,0:T(8,128)S(1)}, f32[8,128]{1,0:T(8,128)S(1)}, u32[]{:S(2)}, u32[]{:S(2)}) collective-permute-start(f32[8,128]{1,0:T(8,128)S(1)} %get-tuple-element.38), channel_id=1, source_target_pairs={{0,2},{2,0},{1,3},{3,1},{4,6},{6,4},{5,7},{7,5},{8,10},{10,8},{9,1... | collective-permute-start | bytes 12296 | tf_op jit(solution)/shard_map/ppermute | solution.py:44
  64.6 2.2 %collective-permute-start.5 = (bf16[2,3,16,32,128]{4,3,2,1,0:T(8,128)(2,1)S(1)}, bf16[2,3,16,32,128]{4,3,2,1,0:T(8,128)(2,1)S(1)}, u32[]{:S(2)}, u32[]{:S(2)}) collective-permute-start(bf16[2,3,16,32,128]{4,3,2,1,0:T(8,128)(2,1)S(1)} %get-tuple-element.49.packed), channel_id=1, source_target_pairs={{0,2},{2,0},{1,3},{3,1},{4,6},{6,4},{5,7},{7,5},{8,10},{10,8},{9,1... | collective-permute-start | bytes 2359304 | tf_op jit(solution)/shard_map/ppermute | solution.py:44
  66.9 25.5 %all_to_all.20.own = bf16[32,8,128]{2,1,0:T(8,128)(2,1)S(1)} all-to-all(bf16[32,8,128]{2,1,0:T(8,128)(2,1)S(1)} %finish.1), channel_id=1, replica_groups=mesh['y'=4,'xh'=2,'z'=16,'xl'=2,'c'=2] {'z','c'}, dimensions={0} | all-to-all | bytes 131072 | tf_op jit(solution)/shard_map/all_to_all | solution.py:348
  92.3 3.0 %collective-permute-start.3 = (bf16[32,8,128]{2,1,0:T(8,128)(2,1)S(1)}, bf16[32,8,128]{2,1,0:T(8,128)(2,1)S(1)}, u32[]{:S(2)}, u32[]{:S(2)}) collective-permute-start(bf16[32,8,128]{2,1,0:T(8,128)(2,1)S(1)} %all_to_all.20.own), channel_id=1, source_target_pairs={{0,2},{2,0},{1,3},{3,1},{4,6},{6,4},{5,7},{7,5},{8,10},{10,8},{9,1... | collective-permute-start | bytes 196616 | tf_op jit(solution)/shard_map/ppermute | solution.py:44
  95.4 3.3 %key_values.1 = (bf16[1536,128]{1,0:T(8,128)(2,1)S(1)}, bf16[1536,128]{1,0:T(8,128)(2,1)S(1)}, f32[1536,1]{1,0:T(8,128)S(1)}) custom-call(bf16[8,768,256]{2,1,0:T(8,128)(2,1)S(1)} %all-to-all-done.tokens, bf16[8,768,256]{2,1,0:T(8,128)(2,1)S(1)} %collective-permute-done.4.core_tokens, bf16[2,3,16,32,128]{4,3,2,1,0:T(8,128)(2,1)S(1)} %get-tuple-element.49.packed, ...), custom_call_target="tpu_custom_call" | custom-call | flops 1610612736 | bytes 8388608 | tf_op jit(solution)/shard_map/key_values/pallas_call | solution.py:349
  98.8 1.7 %summary.1 = (bf16[256,128]{1,0:T(8,128)(2,1)S(1)}, f32[256,128]{1,0:T(8,128)}) custom-call(bf16[32,8,128]{2,1,0:T(8,128)(2,1)S(1)} %all_to_all.20.own, bf16[32,8,128]{2,1,0:T(8,128)(2,1)S(1)} %collective-permute-done.3.other, bf16[1536,128]{1,0:T(8,128)(2,1)S(1)} %get-tuple-element.41.keys, bf16[1536,128]{1,0:T(8,128)(2,1)S(1)} %get-tuple-element.42.values, ...), custom_call_target="tpu_custom_call" | custom-call | flops 201326592 | bytes 2097152 | tf_op jit(solution)/shard_map/summary/pallas_call | solution.py:359
  100.4 0.6 copy-done.7
  101.0 3.9 %all-to-all-start.2 = ((f32[32,8,128]{2,1,0:T(8,128)}), f32[32,8,128]{2,1,0:T(8,128)S(1)}, u32[]{:S(2)}, u32[]{:S(2)}) async-start(f32[32,8,128]{2,1,0:T(8,128)} %bitcast.1), calls=%async_computation.2 | async-start | bytes 262144 | tf_op jit(solution)/shard_map/all_to_all | solution.py:380
  104.9 0.8 copy-done.8
  105.7 3.6 %inverse.1 = f32[256,256]{1,0:T(8,128)S(1)} custom-call(bf16[256,128]{1,0:T(8,128)(2,1)S(1)} %copy-done.8), custom_call_target="tpu_custom_call" | custom-call | flops 2415919104 | bytes 524288 | tf_op jit(solution)/shard_map/inverse/pallas_call | solution.py:370
  109.4 9.0 %all-to-all-done.2.pieces = f32[32,8,128]{2,1,0:T(8,128)S(1)} async-done(((f32[32,8,128]{2,1,0:T(8,128)}), f32[32,8,128]{2,1,0:T(8,128)S(1)}, u32[]{:S(2)}, u32[]{:S(2)}) %all-to-all-start.2) | async-done | bytes 131104 | tf_op jit(solution)/shard_map/all_to_all | solution.py:380
  118.4 0.3 mixed.1
  118.7 0.6 copy-done.6
  119.3 4.6 %all-to-all-start.3 = ((bf16[32,8,128]{2,1,0:T(8,128)(2,1)}), bf16[32,8,128]{2,1,0:T(8,128)(2,1)S(1)}, u32[]{:S(2)}, u32[]{:S(2)}) async-start(bf16[32,8,128]{2,1,0:T(8,128)(2,1)} %copy-done.6), calls=%async_computation.3 | async-start | bytes 131072 | tf_op jit(solution)/shard_map/all_to_all | solution.py:390
  124.0 1.9 %copy-done.1 = bf16[8,768,256]{2,1,0:T(8,128)(2,1)S(1)} copy-done((bf16[8,768,256]{2,1,0:T(8,128)(2,1)S(1)}, bf16[8,768,256]{2,1,0:T(8,128)(2,1)}, u32[]{:S(2)}) %copy-start.1) | copy-done | bytes 3145752
  125.9 1.1 copy-done.3
  127.0 1.1 copy-done.5
  128.1 2.7 %queries.1.query = bf16[1536,128]{1,0:T(8,128)(2,1)S(1)} custom-call(bf16[8,768,256]{2,1,0:T(8,128)(2,1)S(1)} %all-to-all-done.tokens, bf16[8,768,256]{2,1,0:T(8,128)(2,1)S(1)} %copy-done.1, bf16[2,3,16,32,128]{4,3,2,1,0:T(8,128)(2,1)S(1)} %copy-done.3, bf16[2,3,16,32,128]{4,3,2,1,0:T(8,128)(2,1)S(1)} %copy-done.5), custom_call_target="tpu_custom_call" | custom-call | flops 805306368 | bytes 7340032 | tf_op jit(solution)/shard_map/queries/pallas_call | solution.py:391
  130.9 0.8 query_weights.1.weights
  131.6 4.9 %all-to-all-done.3.spread = bf16[32,8,128]{2,1,0:T(8,128)(2,1)S(1)} async-done(((bf16[32,8,128]{2,1,0:T(8,128)(2,1)}), bf16[32,8,128]{2,1,0:T(8,128)(2,1)S(1)}, u32[]{:S(2)}, u32[]{:S(2)}) %all-to-all-start.3) | async-done | bytes 65568 | tf_op jit(solution)/shard_map/all_to_all | solution.py:390
  136.8 6.1 %collective-permute-start.6 = (bf16[768,128]{1,0:T(8,128)(2,1)S(1)}, bf16[768,128]{1,0:T(8,128)(2,1)S(1)}, u32[]{:S(2)}, u32[]{:S(2)}) collective-permute-start(bf16[768,128]{1,0:T(8,128)(2,1)S(1)} %get-tuple-element.54), channel_id=1, source_target_pairs={{0,1},{1,0},{2,3},{3,2},{4,5},{5,4},{6,7},{7,6},{8,9},{9,8},{10,11... | collective-permute-start | bytes 589832 | tf_op jit(solution)/shard_map/ppermute | solution.py:44
  143.2 0.8 collective-permute-done.6.received
  144.0 0.9 join.1
  (29 shorter events, 0.9 us)
Async XLA Ops:
  2.8 7.6 %copy-start.11 = (bf16[3,32,256]{2,1,0:T(8,128)(2,1)S(1)}, bf16[3,32,256]{2,1,0:T(8,128)(2,1)}, u32[]{:S(2)}) copy-start(bf16[3,32,256]{2,1,0:T(8,128)(2,1)} %param.4) | copy-start | bytes 147460
  2.8 51.5 %copy-start.10 = (s32[2,256]{1,0:T(2,128)S(1)}, s32[2,256]{1,0:T(2,128)}, u32[]{:S(2)}) copy-start(s32[2,256]{1,0:T(2,128)} %pos_ref) | copy-start | bytes 6148
  2.8 51.5 %all-to-all-start = ((bf16[8,768,256]{2,1,0:T(8,128)(2,1)}), bf16[8,768,256]{2,1,0:T(8,128)(2,1)S(1)}, u32[]{:S(2)}, u32[]{:S(2)}) async-start(bf16[8,768,256]{2,1,0:T(8,128)(2,1)} %broadcast_in_dim.2), calls=%async_computation | async-start | bytes 6291456 | tf_op jit(solution)/shard_map/all_to_all | solution.py:292
  46.0 13.8 %collective-permute-start.1 = (bf16[3,16,32,256]{3,2,1,0:T(8,128)(2,1)}, bf16[3,16,32,256]{3,2,1,0:T(8,128)(2,1)}, u32[]{:S(2)}, u32[]{:S(2)}) collective-permute-start(bf16[3,16,32,256]{3,2,1,0:T(8,128)(2,1)} %stage.1.column), channel_id=1, source_target_pairs={{0,1},{1,0},{2,3},{3,2},{4,5},{5,4},{6,7},{7,6},{8,9},{9,8},{10,11... | collective-permute-start | bytes 2359304 | tf_op jit(solution)/shard_map/ppermute | solution.py:44
  55.3 5.9 %collective-permute-start = (bf16[8,2048]{1,0:T(8,128)(2,1)S(1)}, bf16[8,2048]{1,0:T(8,128)(2,1)S(1)}, u32[]{:S(2)}, u32[]{:S(2)}) collective-permute-start(bf16[8,2048]{1,0:T(8,128)(2,1)S(1)} %pick.1.own), channel_id=1, source_target_pairs={{0,2},{2,0},{1,3},{3,1},{4,6},{6,4},{5,7},{7,5},{8,10},{10,8},{9,1... | collective-permute-start | bytes 98312 | tf_op jit(solution)/shard_map/ppermute | solution.py:44
  57.5 37.9 %collective-permute-start.4 = (bf16[8,768,256]{2,1,0:T(8,128)(2,1)S(1)}, bf16[8,768,256]{2,1,0:T(8,128)(2,1)S(1)}, u32[]{:S(2)}, u32[]{:S(2)}) collective-permute-start(bf16[8,768,256]{2,1,0:T(8,128)(2,1)S(1)} %all-to-all-done.tokens), channel_id=1, source_target_pairs={{0,1},{1,0},{2,3},{3,2},{4,5},{5,4},{6,7},{7,6},{8,9},{9,8},{10,11... | collective-permute-start | bytes 9437192 | tf_op jit(solution)/shard_map/ppermute | solution.py:44
  61.2 34.2 %copy-start.2 = (bf16[2,3,16,32,128]{4,3,2,1,0:T(8,128)(2,1)}, bf16[2,3,16,32,128]{4,3,2,1,0:T(8,128)(2,1)S(1)}, u32[]{:S(2)}) copy-start(bf16[2,3,16,32,128]{4,3,2,1,0:T(8,128)(2,1)S(1)} %get-tuple-element.49.packed) | copy-start | bytes 2359300
  61.5 5.3 %collective-permute-start.2 = (f32[8,128]{1,0:T(8,128)S(1)}, f32[8,128]{1,0:T(8,128)S(1)}, u32[]{:S(2)}, u32[]{:S(2)}) collective-permute-start(f32[8,128]{1,0:T(8,128)S(1)} %get-tuple-element.38), channel_id=1, source_target_pairs={{0,2},{2,0},{1,3},{3,1},{4,6},{6,4},{5,7},{7,5},{8,10},{10,8},{9,1... | collective-permute-start | bytes 12296 | tf_op jit(solution)/shard_map/ppermute | solution.py:44
  64.6 30.8 %collective-permute-start.5 = (bf16[2,3,16,32,128]{4,3,2,1,0:T(8,128)(2,1)S(1)}, bf16[2,3,16,32,128]{4,3,2,1,0:T(8,128)(2,1)S(1)}, u32[]{:S(2)}, u32[]{:S(2)}) collective-permute-start(bf16[2,3,16,32,128]{4,3,2,1,0:T(8,128)(2,1)S(1)} %get-tuple-element.49.packed), channel_id=1, source_target_pairs={{0,2},{2,0},{1,3},{3,1},{4,6},{6,4},{5,7},{7,5},{8,10},{10,8},{9,1... | collective-permute-start | bytes 2359304 | tf_op jit(solution)/shard_map/ppermute | solution.py:44
  92.3 6.4 %collective-permute-start.3 = (bf16[32,8,128]{2,1,0:T(8,128)(2,1)S(1)}, bf16[32,8,128]{2,1,0:T(8,128)(2,1)S(1)}, u32[]{:S(2)}, u32[]{:S(2)}) collective-permute-start(bf16[32,8,128]{2,1,0:T(8,128)(2,1)S(1)} %all_to_all.20.own), channel_id=1, source_target_pairs={{0,2},{2,0},{1,3},{3,1},{4,6},{6,4},{5,7},{7,5},{8,10},{10,8},{9,1... | collective-permute-start | bytes 196616 | tf_op jit(solution)/shard_map/ppermute | solution.py:44
  95.4 3.3 %copy-start.4 = (bf16[2,3,16,32,128]{4,3,2,1,0:T(8,128)(2,1)}, bf16[2,3,16,32,128]{4,3,2,1,0:T(8,128)(2,1)S(1)}, u32[]{:S(2)}) copy-start(bf16[2,3,16,32,128]{4,3,2,1,0:T(8,128)(2,1)S(1)} %collective-permute-done.5.across) | copy-start | bytes 2359300
  95.4 3.3 %copy-start = (bf16[8,768,256]{2,1,0:T(8,128)(2,1)}, bf16[8,768,256]{2,1,0:T(8,128)(2,1)S(1)}, u32[]{:S(2)}) copy-start(bf16[8,768,256]{2,1,0:T(8,128)(2,1)S(1)} %collective-permute-done.4.core_tokens) | copy-start | bytes 9437188
  100.4 0.6 copy-start.7
  101.0 17.3 %all-to-all-start.2 = ((f32[32,8,128]{2,1,0:T(8,128)}), f32[32,8,128]{2,1,0:T(8,128)S(1)}, u32[]{:S(2)}, u32[]{:S(2)}) async-start(f32[32,8,128]{2,1,0:T(8,128)} %bitcast.1), calls=%async_computation.2 | async-start | bytes 262144 | tf_op jit(solution)/shard_map/all_to_all | solution.py:380
  104.9 0.8 copy-start.8
  118.7 0.7 copy-start.6
  119.3 17.2 %all-to-all-start.3 = ((bf16[32,8,128]{2,1,0:T(8,128)(2,1)}), bf16[32,8,128]{2,1,0:T(8,128)(2,1)S(1)}, u32[]{:S(2)}, u32[]{:S(2)}) async-start(bf16[32,8,128]{2,1,0:T(8,128)(2,1)} %copy-done.6), calls=%async_computation.3 | async-start | bytes 131072 | tf_op jit(solution)/shard_map/all_to_all | solution.py:390
  124.0 1.9 %copy-start.1 = (bf16[8,768,256]{2,1,0:T(8,128)(2,1)S(1)}, bf16[8,768,256]{2,1,0:T(8,128)(2,1)}, u32[]{:S(2)}) copy-start(bf16[8,768,256]{2,1,0:T(8,128)(2,1)} %copy-done) | copy-start | bytes 9437188
  125.9 1.1 copy-start.3
  127.0 1.1 copy-start.5
  128.1 2.7 %copy-start.9 = (bf16[256,128]{1,0:T(8,128)(2,1)S(1)}, bf16[256,128]{1,0:T(8,128)(2,1)}, u32[]{:S(2)}) copy-start(bf16[256,128]{1,0:T(8,128)(2,1)} %copy-done.7) | copy-start | bytes 196612
  136.8 7.1 %collective-permute-start.6 = (bf16[768,128]{1,0:T(8,128)(2,1)S(1)}, bf16[768,128]{1,0:T(8,128)(2,1)S(1)}, u32[]{:S(2)}, u32[]{:S(2)}) collective-permute-start(bf16[768,128]{1,0:T(8,128)(2,1)S(1)} %get-tuple-element.54), channel_id=1, source_target_pairs={{0,1},{1,0},{2,3},{3,2},{4,5},{5,4},{6,7},{7,6},{8,9},{9,8},{10,11... | collective-permute-start | bytes 589832 | tf_op jit(solution)/shard_map/ppermute | solution.py:44

commit v13 on v12

--- a/solution.py
+++ b/solution.py
@@ -268,16 +268,24 @@
     ).astype(BF16)
 
 
-def keep_kernel(mixed, weights, keep):
-    keep[...] = lax.dot_general(
+def keep_kernel(mixed, weights, out):
+    c = lax.axis_index("c")
+    out[:, pl.ds(pl.multiple_of(c * 128, 128), 128)] = lax.dot_general(
         weights[:768, :], mixed[...], ROWS, preferred_element_type=F32
     ).astype(BF16)
 
 
-def join_kernel(keep, received, out):
+def join_kernel(begun, received, out, sems):
     c = lax.axis_index("c")
-    out[:, pl.ds(pl.multiple_of(c * 128, 128), 128)] = keep[...]
-    out[:, pl.ds(pl.multiple_of((1 - c) * 128, 128), 128)] = received[...]
+    cols = pl.ds(pl.multiple_of((1 - c) * 128, 128), 128)
+    run(
+        [
+            pltpu.make_async_copy(
+                received.at[pl.ds(i * 192, 192)], out.at[pl.ds(i * 192, 192), cols], sems.at[i]
+            )
+            for i in range(4)
+        ]
+    )
 
 
 def shape(dims, dtype):
@@ -421,13 +429,20 @@
     keep = call(
         keep_kernel,
         "keep",
-        shape((768, 128), BF16),
+        shape((768, 256), BF16),
         [VMEM] * 2,
         2 * 768 * 256 * 128,
         1 << 19,
     )(mixed, query_weights)
-    return call(
-        join_kernel, "join", shape((768, 256), BF16), [VMEM] * 2, 1 << 10, 1 << 19
+    return pl.pallas_call(
+        join_kernel,
+        out_shape=shape((768, 256), BF16),
+        in_specs=[ANY, VMEM],
+        out_specs=ANY,
+        scratch_shapes=[pltpu.SemaphoreType.DMA((4,))],
+        input_output_aliases={0: 0},
+        cost_estimate=pl.CostEstimate(flops=1 << 10, bytes_accessed=1 << 19, transcendentals=0),
+        name="join",
     )(keep, received)
 
 

time: 146 us -> 147 us (level)
  Pallas kernels: 17.4 us -> 18.9 us
    pallas_call x2, Pallas kernels: 1.1 us -> 2.64 us  [the longest x1 1.63 us: shards(): pl.pallas_call(join_kernel, out_shape=shape((768, 256), BF16), in_specs=[...]
    unnamed x24 -> x26, local copies, waits for them, and re-layouts: 6.27 us -> 6.96 us
  transfers between devices with their start and end apart: 10 -> 10, of which waited for: 3 -> 2; matrix products, arithmetic and copies ran while one was open for 0% -> 0% of each run, Pallas kernels for 10% -> 10%
where the time goes in v13:
time: 147 us; the launch traced here: 146 us
  blocking collectives  60.1 us (41%)
  starting transfers between devices  43.3 us (29%)
  Pallas kernels  18.9 us (13%)
  waiting for transfers between devices  14 us (10%)
  local copies, waits for them, and re-layouts  9.78 us (7%)
    all_gather x1, blocking collectives, shards(): lax.all_gather(weights, 'z', axis=1, tiled=True).reshape(3, 16, 32, 256)  34.6 us
    ppermute x7, starting transfers between devices, shift(): lax.ppermute(value, axis, [(i, (i + step) % size) for i in range(size)])  27.2 us
    all_to_all x1, blocking collectives, shards(): own_marks = lax.all_to_all(spread, CORES, 0, 0, tiled=True)  25.5 us
    all_to_all x1, waiting for transfers between devices, shards(): pieces = lax.all_to_all(chip.reshape(32, 8, 128), CHIPS, 0, 0, tiled=True)  8.99 us
    all_to_all x1, starting transfers between devices, shards(): lax.all_to_all(jnp.broadcast_to(tokens[None], (8,) + tokens.shape), HEAD,...  7.61 us
    unnamed x26, local copies, waits for them, and re-layouts  6.96 us
    all_to_all x1, waiting for transfers between devices, shards(): spread = lax.all_to_all(spread, CHIPS, 0, 0, tiled=True)  4.9 us
    all_to_all x1, starting transfers between devices, shards(): spread = lax.all_to_all(spread, CHIPS, 0, 0, tiled=True)  4.61 us
  transfers between devices with their start and end apart: 10, of which 2 were waited for; matrix products, arithmetic and copies ran while one was open for 0% of the time, Pallas kernels for 10%

profile of v13, /device:TPU:1, one launch (start us, length us, event | category | flops | bytes accessed | tf_op | source)
XLA Modules:
  0.0 146.3 jit_solution(5013115079253212562)
XLA Ops:
  0.0 2.8 %broadcast_in_dim.2 = bf16[8,768,256]{2,1,0:T(8,128)(2,1)} broadcast(bf16[768,256]{1,0:T(8,128)(2,1)} %param.3), dimensions={1,2} | broadcast | bytes 3538944 | tf_op jit(solution)/shard_map/broadcast_in_dim | solution.py:301
  2.8 7.6 %all-to-all-start = ((bf16[8,768,256]{2,1,0:T(8,128)(2,1)}), bf16[8,768,256]{2,1,0:T(8,128)(2,1)S(1)}, u32[]{:S(2)}, u32[]{:S(2)}) async-start(bf16[8,768,256]{2,1,0:T(8,128)(2,1)} %broadcast_in_dim.2), calls=%async_computation | async-start | bytes 6291456 | tf_op jit(solution)/shard_map/all_to_all | solution.py:300
  10.4 34.6 %all_gather.3 = bf16[3,512,256]{2,1,0:T(8,128)(2,1)S(1)} all-gather(bf16[3,32,256]{2,1,0:T(8,128)(2,1)S(1)} %copy-done.12), channel_id=1, replica_groups=mesh['y'=4,'xh'=2,'z'=16,'xl'=2,'c'=2] {'z'}, dimensions={1}, use_global_device_ids=true | all-gather | bytes 835584 | tf_op jit(solution)/shard_map/all_gather | solution.py:303
  45.1 0.9 stage.1.column
  46.0 8.3 %collective-permute-start.1 = (bf16[3,16,32,256]{3,2,1,0:T(8,128)(2,1)}, bf16[3,16,32,256]{3,2,1,0:T(8,128)(2,1)}, u32[]{:S(2)}, u32[]{:S(2)}) collective-permute-start(bf16[3,16,32,256]{3,2,1,0:T(8,128)(2,1)} %stage.1.column), channel_id=1, source_target_pairs={{0,1},{1,0},{2,3},{3,2},{4,5},{5,4},{6,7},{7,6},{8,9},{9,8},{10,11... | collective-permute-start | bytes 2359304 | tf_op jit(solution)/shard_map/ppermute | solution.py:44
  54.3 1.0 pick.1.own
  55.3 2.2 %collective-permute-start = (bf16[8,2048]{1,0:T(8,128)(2,1)S(1)}, bf16[8,2048]{1,0:T(8,128)(2,1)S(1)}, u32[]{:S(2)}, u32[]{:S(2)}) collective-permute-start(bf16[8,2048]{1,0:T(8,128)(2,1)S(1)} %pick.1.own), channel_id=1, source_target_pairs={{0,2},{2,0},{1,3},{3,1},{4,6},{6,4},{5,7},{7,5},{8,10},{10,8},{9,1... | collective-permute-start | bytes 98312 | tf_op jit(solution)/shard_map/ppermute | solution.py:44
  57.5 2.2 %collective-permute-start.4 = (bf16[8,768,256]{2,1,0:T(8,128)(2,1)S(1)}, bf16[8,768,256]{2,1,0:T(8,128)(2,1)S(1)}, u32[]{:S(2)}, u32[]{:S(2)}) collective-permute-start(bf16[8,768,256]{2,1,0:T(8,128)(2,1)S(1)} %all-to-all-done.tokens), channel_id=1, source_target_pairs={{0,1},{1,0},{2,3},{3,2},{4,5},{5,4},{6,7},{7,6},{8,9},{9,8},{10,11... | collective-permute-start | bytes 9437192 | tf_op jit(solution)/shard_map/ppermute | solution.py:44
  59.7 1.5 %prepare.1 = (bf16[2,16,2,32,256]{4,3,2,1,0:T(8,128)(2,1)S(1)}, bf16[2,3,16,32,128]{4,3,2,1,0:T(8,128)(2,1)S(1)}) custom-call(bf16[3,16,32,256]{3,2,1,0:T(8,128)(2,1)} %stage.1.column, bf16[3,16,32,256]{3,2,1,0:T(8,128)(2,1)} %collective-permute-done.1.core), custom_call_target="tpu_custom_call" | custom-call | flops 1024 | bytes 3145728 | tf_op jit(solution)/shard_map/prepare/pallas_call | solution.py:333
  61.5 3.1 %collective-permute-start.2 = (f32[8,128]{1,0:T(8,128)S(1)}, f32[8,128]{1,0:T(8,128)S(1)}, u32[]{:S(2)}, u32[]{:S(2)}) collective-permute-start(f32[8,128]{1,0:T(8,128)S(1)} %get-tuple-element.38), channel_id=1, source_target_pairs={{0,2},{2,0},{1,3},{3,1},{4,6},{6,4},{5,7},{7,5},{8,10},{10,8},{9,1... | collective-permute-start | bytes 12296 | tf_op jit(solution)/shard_map/ppermute | solution.py:44
  64.6 2.2 %collective-permute-start.5 = (bf16[2,3,16,32,128]{4,3,2,1,0:T(8,128)(2,1)S(1)}, bf16[2,3,16,32,128]{4,3,2,1,0:T(8,128)(2,1)S(1)}, u32[]{:S(2)}, u32[]{:S(2)}) collective-permute-start(bf16[2,3,16,32,128]{4,3,2,1,0:T(8,128)(2,1)S(1)} %get-tuple-element.49.packed), channel_id=1, source_target_pairs={{0,2},{2,0},{1,3},{3,1},{4,6},{6,4},{5,7},{7,5},{8,10},{10,8},{9,1... | collective-permute-start | bytes 2359304 | tf_op jit(solution)/shard_map/ppermute | solution.py:44
  66.9 25.5 %all_to_all.20.own = bf16[32,8,128]{2,1,0:T(8,128)(2,1)S(1)} all-to-all(bf16[32,8,128]{2,1,0:T(8,128)(2,1)S(1)} %finish.1), channel_id=1, replica_groups=mesh['y'=4,'xh'=2,'z'=16,'xl'=2,'c'=2] {'z','c'}, dimensions={0} | all-to-all | bytes 131072 | tf_op jit(solution)/shard_map/all_to_all | solution.py:356
  92.3 3.0 %collective-permute-start.3 = (bf16[32,8,128]{2,1,0:T(8,128)(2,1)S(1)}, bf16[32,8,128]{2,1,0:T(8,128)(2,1)S(1)}, u32[]{:S(2)}, u32[]{:S(2)}) collective-permute-start(bf16[32,8,128]{2,1,0:T(8,128)(2,1)S(1)} %all_to_all.20.own), channel_id=1, source_target_pairs={{0,2},{2,0},{1,3},{3,1},{4,6},{6,4},{5,7},{7,5},{8,10},{10,8},{9,1... | collective-permute-start | bytes 196616 | tf_op jit(solution)/shard_map/ppermute | solution.py:44
  95.4 3.3 %key_values.1 = (bf16[1536,128]{1,0:T(8,128)(2,1)S(1)}, bf16[1536,128]{1,0:T(8,128)(2,1)S(1)}, f32[1536,1]{1,0:T(8,128)S(1)}) custom-call(bf16[8,768,256]{2,1,0:T(8,128)(2,1)S(1)} %all-to-all-done.tokens, bf16[8,768,256]{2,1,0:T(8,128)(2,1)S(1)} %collective-permute-done.4.core_tokens, bf16[2,3,16,32,128]{4,3,2,1,0:T(8,128)(2,1)S(1)} %get-tuple-element.49.packed, ...), custom_call_target="tpu_custom_call" | custom-call | flops 1610612736 | bytes 8388608 | tf_op jit(solution)/shard_map/key_values/pallas_call | solution.py:357
  98.7 1.7 %summary.1 = (bf16[256,128]{1,0:T(8,128)(2,1)S(1)}, f32[256,128]{1,0:T(8,128)}) custom-call(bf16[32,8,128]{2,1,0:T(8,128)(2,1)S(1)} %all_to_all.20.own, bf16[32,8,128]{2,1,0:T(8,128)(2,1)S(1)} %collective-permute-done.3.other, bf16[1536,128]{1,0:T(8,128)(2,1)S(1)} %get-tuple-element.41.keys, bf16[1536,128]{1,0:T(8,128)(2,1)S(1)} %get-tuple-element.42.values, ...), custom_call_target="tpu_custom_call" | custom-call | flops 201326592 | bytes 2097152 | tf_op jit(solution)/shard_map/summary/pallas_call | solution.py:367
  100.4 0.6 copy-done.7
  101.0 3.9 %all-to-all-start.2 = ((f32[32,8,128]{2,1,0:T(8,128)}), f32[32,8,128]{2,1,0:T(8,128)S(1)}, u32[]{:S(2)}, u32[]{:S(2)}) async-start(f32[32,8,128]{2,1,0:T(8,128)} %bitcast.1), calls=%async_computation.2 | async-start | bytes 262144 | tf_op jit(solution)/shard_map/all_to_all | solution.py:388
  104.9 0.8 copy-done.8
  105.7 3.6 %inverse.1 = f32[256,256]{1,0:T(8,128)S(1)} custom-call(bf16[256,128]{1,0:T(8,128)(2,1)S(1)} %copy-done.8), custom_call_target="tpu_custom_call" | custom-call | flops 2415919104 | bytes 524288 | tf_op jit(solution)/shard_map/inverse/pallas_call | solution.py:378
  109.4 9.0 %all-to-all-done.2.pieces = f32[32,8,128]{2,1,0:T(8,128)S(1)} async-done(((f32[32,8,128]{2,1,0:T(8,128)}), f32[32,8,128]{2,1,0:T(8,128)S(1)}, u32[]{:S(2)}, u32[]{:S(2)}) %all-to-all-start.2) | async-done | bytes 131104 | tf_op jit(solution)/shard_map/all_to_all | solution.py:388
  118.7 0.6 copy-done.6
  119.4 4.6 %all-to-all-start.3 = ((bf16[32,8,128]{2,1,0:T(8,128)(2,1)}), bf16[32,8,128]{2,1,0:T(8,128)(2,1)S(1)}, u32[]{:S(2)}, u32[]{:S(2)}) async-start(bf16[32,8,128]{2,1,0:T(8,128)(2,1)} %copy-done.6), calls=%async_computation.3 | async-start | bytes 131072 | tf_op jit(solution)/shard_map/all_to_all | solution.py:398
  124.0 1.9 %copy-done.1 = bf16[8,768,256]{2,1,0:T(8,128)(2,1)S(1)} copy-done((bf16[8,768,256]{2,1,0:T(8,128)(2,1)S(1)}, bf16[8,768,256]{2,1,0:T(8,128)(2,1)}, u32[]{:S(2)}) %copy-start.1) | copy-done | bytes 3145752
  125.9 1.1 copy-done.3
  127.0 1.1 copy-done.5
  128.1 2.7 %queries.1.query = bf16[1536,128]{1,0:T(8,128)(2,1)S(1)} custom-call(bf16[8,768,256]{2,1,0:T(8,128)(2,1)S(1)} %all-to-all-done.tokens, bf16[8,768,256]{2,1,0:T(8,128)(2,1)S(1)} %copy-done.1, bf16[2,3,16,32,128]{4,3,2,1,0:T(8,128)(2,1)S(1)} %copy-done.3, bf16[2,3,16,32,128]{4,3,2,1,0:T(8,128)(2,1)S(1)} %copy-done.5), custom_call_target="tpu_custom_call" | custom-call | flops 805306368 | bytes 7340032 | tf_op jit(solution)/shard_map/queries/pallas_call | solution.py:399
  130.9 0.8 query_weights.1.weights
  131.6 4.9 %all-to-all-done.3.spread = bf16[32,8,128]{2,1,0:T(8,128)(2,1)S(1)} async-done(((bf16[32,8,128]{2,1,0:T(8,128)(2,1)}), bf16[32,8,128]{2,1,0:T(8,128)(2,1)S(1)}, u32[]{:S(2)}, u32[]{:S(2)}) %all-to-all-start.3) | async-done | bytes 65568 | tf_op jit(solution)/shard_map/all_to_all | solution.py:398
  136.8 6.1 %collective-permute-start.6 = (bf16[768,128]{1,0:T(8,128)(2,1)S(1)}, bf16[768,128]{1,0:T(8,128)(2,1)S(1)}, u32[]{:S(2)}, u32[]{:S(2)}) collective-permute-start(bf16[768,128]{1,0:T(8,128)(2,1)S(1)} %get-tuple-element.54), channel_id=1, source_target_pairs={{0,1},{1,0},{2,3},{3,2},{4,5},{5,4},{6,7},{7,6},{8,9},{9,8},{10,11... | collective-permute-start | bytes 589832 | tf_op jit(solution)/shard_map/ppermute | solution.py:44
  142.9 1.0 keep.1.begun
  144.0 0.7 copy-done.11
  144.6 1.6 %join.1 = bf16[768,256]{1,0:T(8,128)(2,1)} custom-call(bf16[768,256]{1,0:T(8,128)(2,1)} %keep.1.begun, bf16[768,128]{1,0:T(8,128)(2,1)} %copy-done.11), custom_call_target="tpu_custom_call", output_to_operand_aliasing={{}: (0, {})} | custom-call | flops 1024 | bytes 524288 | tf_op jit(solution)/shard_map/join/pallas_call | solution.py:437
  (31 shorter events, 1.0 us)
Async XLA Ops:
  2.8 7.6 %copy-start.12 = (bf16[3,32,256]{2,1,0:T(8,128)(2,1)S(1)}, bf16[3,32,256]{2,1,0:T(8,128)(2,1)}, u32[]{:S(2)}) copy-start(bf16[3,32,256]{2,1,0:T(8,128)(2,1)} %param.4) | copy-start | bytes 147460
  2.8 51.5 %copy-start.10 = (s32[2,256]{1,0:T(2,128)S(1)}, s32[2,256]{1,0:T(2,128)}, u32[]{:S(2)}) copy-start(s32[2,256]{1,0:T(2,128)} %pos_ref) | copy-start | bytes 6148
  2.8 51.5 %all-to-all-start = ((bf16[8,768,256]{2,1,0:T(8,128)(2,1)}), bf16[8,768,256]{2,1,0:T(8,128)(2,1)S(1)}, u32[]{:S(2)}, u32[]{:S(2)}) async-start(bf16[8,768,256]{2,1,0:T(8,128)(2,1)} %broadcast_in_dim.2), calls=%async_computation | async-start | bytes 6291456 | tf_op jit(solution)/shard_map/all_to_all | solution.py:300
  46.0 13.8 %collective-permute-start.1 = (bf16[3,16,32,256]{3,2,1,0:T(8,128)(2,1)}, bf16[3,16,32,256]{3,2,1,0:T(8,128)(2,1)}, u32[]{:S(2)}, u32[]{:S(2)}) collective-permute-start(bf16[3,16,32,256]{3,2,1,0:T(8,128)(2,1)} %stage.1.column), channel_id=1, source_target_pairs={{0,1},{1,0},{2,3},{3,2},{4,5},{5,4},{6,7},{7,6},{8,9},{9,8},{10,11... | collective-permute-start | bytes 2359304 | tf_op jit(solution)/shard_map/ppermute | solution.py:44
  55.3 5.9 %collective-permute-start = (bf16[8,2048]{1,0:T(8,128)(2,1)S(1)}, bf16[8,2048]{1,0:T(8,128)(2,1)S(1)}, u32[]{:S(2)}, u32[]{:S(2)}) collective-permute-start(bf16[8,2048]{1,0:T(8,128)(2,1)S(1)} %pick.1.own), channel_id=1, source_target_pairs={{0,2},{2,0},{1,3},{3,1},{4,6},{6,4},{5,7},{7,5},{8,10},{10,8},{9,1... | collective-permute-start | bytes 98312 | tf_op jit(solution)/shard_map/ppermute | solution.py:44
  57.5 37.9 %collective-permute-start.4 = (bf16[8,768,256]{2,1,0:T(8,128)(2,1)S(1)}, bf16[8,768,256]{2,1,0:T(8,128)(2,1)S(1)}, u32[]{:S(2)}, u32[]{:S(2)}) collective-permute-start(bf16[8,768,256]{2,1,0:T(8,128)(2,1)S(1)} %all-to-all-done.tokens), channel_id=1, source_target_pairs={{0,1},{1,0},{2,3},{3,2},{4,5},{5,4},{6,7},{7,6},{8,9},{9,8},{10,11... | collective-permute-start | bytes 9437192 | tf_op jit(solution)/shard_map/ppermute | solution.py:44
  61.2 34.2 %copy-start.2 = (bf16[2,3,16,32,128]{4,3,2,1,0:T(8,128)(2,1)}, bf16[2,3,16,32,128]{4,3,2,1,0:T(8,128)(2,1)S(1)}, u32[]{:S(2)}) copy-start(bf16[2,3,16,32,128]{4,3,2,1,0:T(8,128)(2,1)S(1)} %get-tuple-element.49.packed) | copy-start | bytes 2359300
  61.5 5.3 %collective-permute-start.2 = (f32[8,128]{1,0:T(8,128)S(1)}, f32[8,128]{1,0:T(8,128)S(1)}, u32[]{:S(2)}, u32[]{:S(2)}) collective-permute-start(f32[8,128]{1,0:T(8,128)S(1)} %get-tuple-element.38), channel_id=1, source_target_pairs={{0,2},{2,0},{1,3},{3,1},{4,6},{6,4},{5,7},{7,5},{8,10},{10,8},{9,1... | collective-permute-start | bytes 12296 | tf_op jit(solution)/shard_map/ppermute | solution.py:44
  64.6 30.8 %collective-permute-start.5 = (bf16[2,3,16,32,128]{4,3,2,1,0:T(8,128)(2,1)S(1)}, bf16[2,3,16,32,128]{4,3,2,1,0:T(8,128)(2,1)S(1)}, u32[]{:S(2)}, u32[]{:S(2)}) collective-permute-start(bf16[2,3,16,32,128]{4,3,2,1,0:T(8,128)(2,1)S(1)} %get-tuple-element.49.packed), channel_id=1, source_target_pairs={{0,2},{2,0},{1,3},{3,1},{4,6},{6,4},{5,7},{7,5},{8,10},{10,8},{9,1... | collective-permute-start | bytes 2359304 | tf_op jit(solution)/shard_map/ppermute | solution.py:44
  92.3 6.4 %collective-permute-start.3 = (bf16[32,8,128]{2,1,0:T(8,128)(2,1)S(1)}, bf16[32,8,128]{2,1,0:T(8,128)(2,1)S(1)}, u32[]{:S(2)}, u32[]{:S(2)}) collective-permute-start(bf16[32,8,128]{2,1,0:T(8,128)(2,1)S(1)} %all_to_all.20.own), channel_id=1, source_target_pairs={{0,2},{2,0},{1,3},{3,1},{4,6},{6,4},{5,7},{7,5},{8,10},{10,8},{9,1... | collective-permute-start | bytes 196616 | tf_op jit(solution)/shard_map/ppermute | solution.py:44
  95.4 3.3 %copy-start.4 = (bf16[2,3,16,32,128]{4,3,2,1,0:T(8,128)(2,1)}, bf16[2,3,16,32,128]{4,3,2,1,0:T(8,128)(2,1)S(1)}, u32[]{:S(2)}) copy-start(bf16[2,3,16,32,128]{4,3,2,1,0:T(8,128)(2,1)S(1)} %collective-permute-done.5.across) | copy-start | bytes 2359300
  95.4 3.3 %copy-start = (bf16[8,768,256]{2,1,0:T(8,128)(2,1)}, bf16[8,768,256]{2,1,0:T(8,128)(2,1)S(1)}, u32[]{:S(2)}) copy-start(bf16[8,768,256]{2,1,0:T(8,128)(2,1)S(1)} %collective-permute-done.4.core_tokens) | copy-start | bytes 9437188
  100.4 0.6 copy-start.7
  101.0 17.3 %all-to-all-start.2 = ((f32[32,8,128]{2,1,0:T(8,128)}), f32[32,8,128]{2,1,0:T(8,128)S(1)}, u32[]{:S(2)}, u32[]{:S(2)}) async-start(f32[32,8,128]{2,1,0:T(8,128)} %bitcast.1), calls=%async_computation.2 | async-start | bytes 262144 | tf_op jit(solution)/shard_map/all_to_all | solution.py:388
  104.9 0.8 copy-start.8
  118.7 0.7 copy-start.6
  119.4 17.2 %all-to-all-start.3 = ((bf16[32,8,128]{2,1,0:T(8,128)(2,1)}), bf16[32,8,128]{2,1,0:T(8,128)(2,1)S(1)}, u32[]{:S(2)}, u32[]{:S(2)}) async-start(bf16[32,8,128]{2,1,0:T(8,128)(2,1)} %copy-done.6), calls=%async_computation.3 | async-start | bytes 131072 | tf_op jit(solution)/shard_map/all_to_all | solution.py:398
  124.0 1.9 %copy-start.1 = (bf16[8,768,256]{2,1,0:T(8,128)(2,1)S(1)}, bf16[8,768,256]{2,1,0:T(8,128)(2,1)}, u32[]{:S(2)}) copy-start(bf16[8,768,256]{2,1,0:T(8,128)(2,1)} %copy-done) | copy-start | bytes 9437188
  125.9 1.1 copy-start.3
  127.0 1.1 copy-start.5
  128.1 2.7 %copy-start.9 = (bf16[256,128]{1,0:T(8,128)(2,1)S(1)}, bf16[256,128]{1,0:T(8,128)(2,1)}, u32[]{:S(2)}) copy-start(bf16[256,128]{1,0:T(8,128)(2,1)} %copy-done.7) | copy-start | bytes 196612
  136.8 7.1 %collective-permute-start.6 = (bf16[768,128]{1,0:T(8,128)(2,1)S(1)}, bf16[768,128]{1,0:T(8,128)(2,1)S(1)}, u32[]{:S(2)}, u32[]{:S(2)}) collective-permute-start(bf16[768,128]{1,0:T(8,128)(2,1)S(1)} %get-tuple-element.54), channel_id=1, source_target_pairs={{0,1},{1,0},{2,3},{3,2},{4,5},{5,4},{6,7},{7,6},{8,9},{9,8},{10,11... | collective-permute-start | bytes 589832 | tf_op jit(solution)/shard_map/ppermute | solution.py:44
  144.0 0.7 copy-start.11
